TPU v7x, 32 devices: a whole 2x2x4 slice. The times are simulated.
32 devices in a mesh: dp: 8 (over z, x), ctx: 4 (over y, core).
Axes of the slice: x: 2, y: 2, z: 4, core: 2. Of those that a mesh axis runs over, the one named last changes fastest.
Arguments:
- hidden_in: bfloat16 [32, 1024, 960], P('dp', 'ctx'), may hold values from -41 to 41
- norm_gains: bfloat16 [1920], P(('dp', 'ctx')), may hold values from 0.099609375 to 1.8984375
- w_query: bfloat16 [960, 960], P('ctx', 'dp'), may hold values from -0.1875 to 0.1875
- w_key: bfloat16 [960, 320], P('ctx', 'dp'), may hold values from -0.1875 to 0.1875
- w_value: bfloat16 [960, 320], P('ctx', 'dp'), may hold values from -0.1875 to 0.1875
- w_out: bfloat16 [960, 960], P('ctx', 'dp'), may hold values from -1.5 to 1.5
- w_gate: bfloat16 [960, 2560], P('ctx', 'dp'), may hold values from -0.1875 to 0.1875
- w_up: bfloat16 [960, 2560], P('ctx', 'dp'), may hold values from -0.1875 to 0.1875
- w_down: bfloat16 [2560, 960], P('ctx', 'dp'), may hold values from -0.125 to 0.125
- cotangent: bfloat16 [32, 1024, 960], P('dp', 'ctx'), may hold values from -6 to 6
Outputs:
- hidden_out: bfloat16 [32, 1024, 960], P('dp', 'ctx')
- hidden_grad: bfloat16 [32, 1024, 960], P('dp', 'ctx')
- gains_grad: float32 [1920], P(('dp', 'ctx'))
- query_grad: float32 [960, 960], P('ctx', 'dp')
- key_grad: float32 [960, 320], P('ctx', 'dp')
- value_grad: float32 [960, 320], P('ctx', 'dp')
- out_grad: float32 [960, 960], P('ctx', 'dp')
- gate_grad: float32 [960, 2560], P('ctx', 'dp')
- up_grad: float32 [960, 2560], P('ctx', 'dp')
- down_grad: float32 [2560, 960], P('ctx', 'dp')
All inputs are finite; a program needn't handle non-finite values.
Results may differ from a plain program's by a relative error of at most 0.014.
Values may be sent and summed in bfloat16 or wider, within the bound.
No kernel may reach another device: no remote copies, remote signals or barrier semaphores. Data moves between devices by JAX's collectives and lax.ppermute only.
A program may use at most 640 MiB of HBM per device.

v0:
```python
import math

import jax
import jax.numpy as jnp
from jax import lax
from jax.sharding import PartitionSpec as P

QH = 15
KVH = 5
HD = 64


epsilon = 1e-05
rope_base = 100000.0
masked_score = -1e30
contract_last = (((1,), (1,)), ((), ()))
contract_first = (((0,), (0,)), ((), ()))


def rope_tables(positions, head_size):
    half_size = head_size // 2
    frequencies = jnp.exp(
        -(jnp.arange(half_size).astype(jnp.float32) * (2.0 / head_size)) * math.log(rope_base)
    )
    angles = positions[:, None] * frequencies[None, :]
    angles = jnp.concatenate([angles, angles], axis=-1)
    return (jnp.cos(angles), jnp.sin(angles))


def rotate(values, cos_table, sin_table):
    half_size = values.shape[-1] // 2
    turned = jnp.concatenate([-values[..., half_size:], values[..., :half_size]], axis=-1)
    return values * cos_table[:, None, :] + turned * sin_table[:, None, :]


def unrotate(grad_turned, cos_table, sin_table):
    primal_out, pullback = jax.vjp(lambda values: rotate(values, cos_table, sin_table), grad_turned)
    return pullback(grad_turned)[0]


def rms_scale(values, gain_row):
    return (
        values * lax.rsqrt(jnp.mean(values * values, axis=-1, keepdims=True) + epsilon) * gain_row
    )


def local(hidden_in, norm_gains, w_query, w_key, w_value, w_out, w_gate, w_up, w_down, cotangent):
    seqs_here, seg_len, model_width = hidden_in.shape
    ctx_size = lax.axis_size("ctx")
    dp_size = lax.axis_size("dp")
    full_len = seg_len * ctx_size
    rows_here = seqs_here * seg_len
    per_group = QH // KVH
    score_scale = HD ** (-0.5)
    row_parts = (
        lax.all_gather(w_query, "ctx", axis=0, tiled=True),
        lax.all_gather(w_key, "ctx", axis=0, tiled=True),
        lax.all_gather(w_value, "ctx", axis=0, tiled=True),
        lax.all_gather(w_out, "ctx", axis=0, tiled=True),
        lax.all_gather(w_gate, "ctx", axis=0, tiled=True),
        lax.all_gather(w_up, "ctx", axis=0, tiled=True),
        lax.all_gather(w_down, "ctx", axis=0, tiled=True),
        lax.all_gather(norm_gains.reshape(-1, 1), "ctx", axis=0, tiled=True),
    )
    gathered = (
        lax.all_gather(row_parts[0], "dp", axis=1, tiled=True),
        lax.all_gather(row_parts[1], "dp", axis=1, tiled=True),
        lax.all_gather(row_parts[2], "dp", axis=1, tiled=True),
        lax.all_gather(row_parts[3], "dp", axis=1, tiled=True),
        lax.all_gather(row_parts[4], "dp", axis=1, tiled=True),
        lax.all_gather(row_parts[5], "dp", axis=1, tiled=True),
        lax.all_gather(row_parts[6], "dp", axis=1, tiled=True),
        lax.all_gather(row_parts[7].reshape(1, -1), "dp", axis=1, tiled=True),
    )
    first_pos = lax.axis_index("ctx") * seg_len + jnp.arange(seg_len)
    cos_table, sin_table = rope_tables(first_pos.astype(jnp.float32), HD)
    row_pos = jnp.tile(first_pos, per_group)
    causal_mask = jnp.arange(full_len)[None, :] <= row_pos[:, None]

    def group_queries(tensor):
        return (
            tensor.reshape(seqs_here, seg_len, KVH, per_group, HD)
            .transpose(0, 2, 3, 1, 4)
            .reshape(seqs_here * KVH, per_group * seg_len, HD)
        )

    def ungroup_queries(tensor):
        return (
            tensor.reshape(seqs_here, KVH, per_group, seg_len, HD)
            .transpose(0, 3, 1, 2, 4)
            .reshape(rows_here, QH * HD)
        )

    def group_keys(tensor):
        return (
            tensor.reshape(seqs_here, full_len, KVH, HD)
            .transpose(0, 2, 1, 3)
            .reshape(seqs_here * KVH, full_len, HD)
        )

    def ungroup_keys(tensor):
        return (
            tensor.reshape(seqs_here, KVH, full_len, HD)
            .transpose(0, 2, 1, 3)
            .reshape(seqs_here, full_len, KVH * HD)
        )

    def block_scores(query_block, key_block):
        raw_scores = (
            lax.dot_general(
                query_block, key_block, contract_last, preferred_element_type=jnp.float32
            )
            * score_scale
        )
        return jnp.where(causal_mask, raw_scores, masked_score)

    def attend_forward(triple):
        query_block, key_block, value_block = triple
        scores = block_scores(query_block, key_block)
        row_top = jnp.max(scores, axis=-1, keepdims=True)
        exponents = jnp.exp(scores - row_top)
        totals = jnp.sum(exponents, axis=-1, keepdims=True)
        attn_weights = exponents / totals
        attended = jnp.dot(
            attn_weights.astype(jnp.bfloat16), value_block, preferred_element_type=jnp.float32
        )
        return (attended, (row_top + jnp.log(totals))[:, 0])

    gains_full = gathered[7].reshape(-1).astype(jnp.float32)
    inputs_f32 = hidden_in.reshape(rows_here, model_width).astype(jnp.float32)
    normed = rms_scale(inputs_f32, gains_full[:model_width]).astype(jnp.bfloat16)
    queries = jnp.dot(normed, gathered[0], preferred_element_type=jnp.float32).reshape(
        seqs_here, seg_len, QH, HD
    )
    key_proj = jnp.dot(normed, gathered[1], preferred_element_type=jnp.float32).reshape(
        seqs_here, seg_len, KVH, HD
    )
    value_proj = (
        jnp.dot(normed, gathered[2], preferred_element_type=jnp.float32)
        .astype(jnp.bfloat16)
        .reshape(seqs_here, seg_len, KVH * HD)
    )
    turned_query = rotate(queries, cos_table, sin_table).astype(jnp.bfloat16)
    turned_key = (
        rotate(key_proj, cos_table, sin_table)
        .astype(jnp.bfloat16)
        .reshape(seqs_here, seg_len, KVH * HD)
    )
    key_sets = (
        lax.all_gather(turned_key, "ctx", axis=1, tiled=True),
        lax.all_gather(value_proj, "ctx", axis=1, tiled=True),
    )
    grouped_query = group_queries(turned_query)
    attended, log_totals = lax.map(
        attend_forward, (grouped_query, group_keys(key_sets[0]), group_keys(key_sets[1]))
    )
    mixed_heads = ungroup_queries(attended).astype(jnp.bfloat16)
    middle = inputs_f32 + jnp.dot(mixed_heads, gathered[3], preferred_element_type=jnp.float32)
    normed_two = rms_scale(middle, gains_full[model_width:]).astype(jnp.bfloat16)
    gate_pre = jnp.dot(normed_two, gathered[4], preferred_element_type=jnp.float32)
    up_pre = jnp.dot(normed_two, gathered[5], preferred_element_type=jnp.float32)
    product = (jax.nn.silu(gate_pre) * up_pre).astype(jnp.bfloat16)
    result = middle + jnp.dot(product, gathered[6], preferred_element_type=jnp.float32)
    hidden_out = result.astype(jnp.bfloat16).reshape(seqs_here, seg_len, model_width)
    rows_again = (
        lax.all_gather(w_query, "ctx", axis=0, tiled=True),
        lax.all_gather(w_key, "ctx", axis=0, tiled=True),
        lax.all_gather(w_value, "ctx", axis=0, tiled=True),
        lax.all_gather(w_out, "ctx", axis=0, tiled=True),
        lax.all_gather(w_gate, "ctx", axis=0, tiled=True),
        lax.all_gather(w_up, "ctx", axis=0, tiled=True),
        lax.all_gather(w_down, "ctx", axis=0, tiled=True),
        lax.all_gather(norm_gains.reshape(-1, 1), "ctx", axis=0, tiled=True),
    )
    refetched = (
        lax.all_gather(rows_again[0], "dp", axis=1, tiled=True),
        lax.all_gather(rows_again[1], "dp", axis=1, tiled=True),
        lax.all_gather(rows_again[2], "dp", axis=1, tiled=True),
        lax.all_gather(rows_again[3], "dp", axis=1, tiled=True),
        lax.all_gather(rows_again[4], "dp", axis=1, tiled=True),
        lax.all_gather(rows_again[5], "dp", axis=1, tiled=True),
        lax.all_gather(rows_again[6], "dp", axis=1, tiled=True),
        lax.all_gather(rows_again[7].reshape(1, -1), "dp", axis=1, tiled=True),
    )
    keys_again = (
        lax.all_gather(turned_key, "ctx", axis=1, tiled=True),
        lax.all_gather(value_proj, "ctx", axis=1, tiled=True),
    )
    gains_back = refetched[7].reshape(-1).astype(jnp.float32)
    seed_low = cotangent.reshape(rows_here, model_width)
    seed_high = seed_low.astype(jnp.float32)
    down_part = lax.dot_general(
        product, seed_low, contract_first, preferred_element_type=jnp.float32
    )
    grad_product = lax.dot_general(
        seed_low, refetched[6], contract_last, preferred_element_type=jnp.float32
    )
    primal_gate, gate_pull = jax.vjp(
        lambda gate_in, up_in: jax.nn.silu(gate_in) * up_in, gate_pre, up_pre
    )
    grad_gate, grad_up = gate_pull(grad_product)
    grad_gate = grad_gate.astype(jnp.bfloat16)
    grad_up = grad_up.astype(jnp.bfloat16)
    gate_part = lax.dot_general(
        normed_two, grad_gate, contract_first, preferred_element_type=jnp.float32
    )
    up_part = lax.dot_general(
        normed_two, grad_up, contract_first, preferred_element_type=jnp.float32
    )
    grad_normed_two = lax.dot_general(
        grad_gate, refetched[4], contract_last, preferred_element_type=jnp.float32
    ) + lax.dot_general(grad_up, refetched[5], contract_last, preferred_element_type=jnp.float32)
    primal_two, second_pull = jax.vjp(rms_scale, middle, gains_back[model_width:])
    grad_middle_norm, gain_two_part = second_pull(grad_normed_two)
    grad_middle = seed_high + grad_middle_norm
    grad_branch = grad_middle.astype(jnp.bfloat16)
    out_part = lax.dot_general(
        mixed_heads, grad_branch, contract_first, preferred_element_type=jnp.float32
    )
    grad_mixed = lax.dot_general(
        grad_branch, refetched[3], contract_last, preferred_element_type=jnp.float32
    ).astype(jnp.bfloat16)

    def attend_backward(bundle):
        query_block, key_block, value_block, log_total, grad_block = bundle
        scores = block_scores(query_block, key_block)
        attn_weights = jnp.exp(scores - log_total[:, None])
        grad_weights = lax.dot_general(
            grad_block, value_block, contract_last, preferred_element_type=jnp.float32
        )
        grad_values = lax.dot_general(
            attn_weights.astype(jnp.bfloat16),
            grad_block,
            contract_first,
            preferred_element_type=jnp.float32,
        )
        grad_scores = (
            attn_weights
            * (grad_weights - jnp.sum(attn_weights * grad_weights, axis=-1, keepdims=True))
        ).astype(jnp.bfloat16)
        grad_queries = (
            jnp.dot(grad_scores, key_block, preferred_element_type=jnp.float32) * score_scale
        )
        grad_keys = (
            lax.dot_general(
                grad_scores, query_block, contract_first, preferred_element_type=jnp.float32
            )
            * score_scale
        )
        return (grad_queries, grad_keys, grad_values)

    grad_grouped = group_queries(grad_mixed.reshape(seqs_here, seg_len, QH, HD))
    query_blocks, key_blocks, value_blocks = lax.map(
        attend_backward,
        (
            grouped_query,
            group_keys(keys_again[0]),
            group_keys(keys_again[1]),
            log_totals,
            grad_grouped,
        ),
    )
    key_sums = (
        lax.psum_scatter(ungroup_keys(key_blocks), "ctx", scatter_dimension=1, tiled=True),
        lax.psum_scatter(ungroup_keys(value_blocks), "ctx", scatter_dimension=1, tiled=True),
    )
    grad_query = (
        unrotate(
            ungroup_queries(query_blocks).reshape(seqs_here, seg_len, QH, HD), cos_table, sin_table
        )
        .astype(jnp.bfloat16)
        .reshape(rows_here, QH * HD)
    )
    grad_key = (
        unrotate(key_sums[0].reshape(seqs_here, seg_len, KVH, HD), cos_table, sin_table)
        .astype(jnp.bfloat16)
        .reshape(rows_here, KVH * HD)
    )
    grad_value = key_sums[1].astype(jnp.bfloat16).reshape(rows_here, KVH * HD)
    query_part = lax.dot_general(
        normed, grad_query, contract_first, preferred_element_type=jnp.float32
    )
    key_part = lax.dot_general(normed, grad_key, contract_first, preferred_element_type=jnp.float32)
    value_part = lax.dot_general(
        normed, grad_value, contract_first, preferred_element_type=jnp.float32
    )
    grad_normed = (
        lax.dot_general(grad_query, refetched[0], contract_last, preferred_element_type=jnp.float32)
        + lax.dot_general(grad_key, refetched[1], contract_last, preferred_element_type=jnp.float32)
        + lax.dot_general(
            grad_value, refetched[2], contract_last, preferred_element_type=jnp.float32
        )
    )
    primal_one, first_pull = jax.vjp(rms_scale, inputs_f32, gains_back[:model_width])
    grad_inputs_norm, gain_one_part = first_pull(grad_normed)
    hidden_grad = (
        (grad_middle + grad_inputs_norm)
        .astype(jnp.bfloat16)
        .reshape(seqs_here, seg_len, model_width)
    )
    gain_part = jnp.concatenate([gain_one_part, gain_two_part])
    col_sums = (
        lax.psum_scatter(query_part, "dp", scatter_dimension=1, tiled=True),
        lax.psum_scatter(key_part, "dp", scatter_dimension=1, tiled=True),
        lax.psum_scatter(value_part, "dp", scatter_dimension=1, tiled=True),
        lax.psum_scatter(out_part, "dp", scatter_dimension=1, tiled=True),
        lax.psum_scatter(gate_part, "dp", scatter_dimension=1, tiled=True),
        lax.psum_scatter(up_part, "dp", scatter_dimension=1, tiled=True),
        lax.psum_scatter(down_part, "dp", scatter_dimension=1, tiled=True),
        lax.psum_scatter(gain_part.reshape(1, -1), "dp", scatter_dimension=1, tiled=True),
    )
    owned = (
        lax.psum_scatter(col_sums[0], "ctx", scatter_dimension=0, tiled=True),
        lax.psum_scatter(col_sums[1], "ctx", scatter_dimension=0, tiled=True),
        lax.psum_scatter(col_sums[2], "ctx", scatter_dimension=0, tiled=True),
        lax.psum_scatter(col_sums[3], "ctx", scatter_dimension=0, tiled=True),
        lax.psum_scatter(col_sums[4], "ctx", scatter_dimension=0, tiled=True),
        lax.psum_scatter(col_sums[5], "ctx", scatter_dimension=0, tiled=True),
        lax.psum_scatter(col_sums[6], "ctx", scatter_dimension=0, tiled=True),
        lax.psum_scatter(col_sums[7].reshape(-1, 1), "ctx", scatter_dimension=0, tiled=True),
    )
    factor = 1.0 / math.sqrt(dp_size * seqs_here * full_len)
    return (
        hidden_out,
        hidden_grad,
        owned[7].reshape(-1) * factor,
        owned[0] * factor,
        owned[1] * factor,
        owned[2] * factor,
        owned[3] * factor,
        owned[4] * factor,
        owned[5] * factor,
        owned[6] * factor,
    )


def solution(mesh):
    in_specs = (
        P("dp", "ctx", None),
        P(("dp", "ctx")),
        P("ctx", "dp"),
        P("ctx", "dp"),
        P("ctx", "dp"),
        P("ctx", "dp"),
        P("ctx", "dp"),
        P("ctx", "dp"),
        P("ctx", "dp"),
        P("dp", "ctx", None),
    )
    out_specs = (
        P("dp", "ctx", None),
        P("dp", "ctx", None),
        P(("dp", "ctx")),
        P("ctx", "dp"),
        P("ctx", "dp"),
        P("ctx", "dp"),
        P("ctx", "dp"),
        P("ctx", "dp"),
        P("ctx", "dp"),
        P("ctx", "dp"),
    )
    return jax.shard_map(local, mesh=mesh, in_specs=in_specs, out_specs=out_specs, check_vma=False)
```

profile of v0, /device:TPU:0, one launch (start us, length us, event | category | flops | bytes accessed | tf_op | source)
XLA Modules:
  0.0 2128.3 jit_solution(17298331334786552677)
XLA Ops:
  27.9 21.9 %all-reduce.5 = bf16[1920]{0:T(1024)(128)(2,1)S(1)} all-reduce(bf16[1920]{0:T(1024)(128)(2,1)S(1)} %dynamic-update-slice.1), channel_id=3, replica_groups=mesh['dp'=8,'ctx'=4] {'dp'}, use_global_device_ids=true, to_apply=%add.5 | all-reduce | flops 1920 | bytes 7680
  57.8 32.5 %all_gather.77 = bf16[960,320]{0,1:T(8,128)(2,1)S(1)} all-gather(bf16[960,40]{0,1:T(8,128)(2,1)S(1)} %reshape.345), channel_id=1, replica_groups=mesh['dp'=8,'ctx'=4] {'dp'}, dimensions={1}, use_global_device_ids=true | all-gather | bytes 691200 | tf_op jit(solution)/shard_map/all_gather | solution.py:67
  99.0 31.6 %all_gather.80 = bf16[960,320]{0,1:T(8,128)(2,1)S(1)} all-gather(bf16[960,40]{0,1:T(8,128)(2,1)S(1)} %reshape.347), channel_id=1, replica_groups=mesh['dp'=8,'ctx'=4] {'dp'}, dimensions={1}, use_global_device_ids=true | all-gather | bytes 691200 | tf_op jit(solution)/shard_map/all_gather | solution.py:68
  213.9 112.1 %while.30 = (s32[]{:T(128)}, bf16[20,768,64]{1,2,0:T(8,128)(2,1)S(1)}, f32[20,768]{1,0:T(8,128)S(1)}, bf16[20,768,64]{2,1,0:T(8,128)(2,1)}, bf16[20,1024,64]{2,1...) while((s32[]{:T(128)}, bf16[20,768,64]{1,2,0:T(8,128)(2,1)S(1)}, ...), condition=%wide.region_4.5_spmd.clone.clone, body=%wide.region_1.4_spmd.clone.sunk.clone | while | flops 213122304 | bytes 10405977 | solution.py:154
  355.2 31.3 %all-gather.22.cloned.1.call-done = bf16[960,2560]{0,1:T(8,128)(2,1)} async-done(((bf16[960,320]{0,1:T(8,128)(2,1)}), bf16[960,2560]{0,1:T(8,128)(2,1)}) %all-gather.22.cloned.1.call-update) | async-done | bytes 4915216 | tf_op jit(solution)/shard_map/all_gather | solution.py:70
  397.4 71.2 %all-gather.26.cloned.1.call-done = bf16[2560,960]{0,1:T(8,128)(2,1)} async-done(((bf16[2560,120]{0,1:T(8,128)(2,1)}), bf16[2560,960]{0,1:T(8,128)(2,1)}) %all-gather.26.cloned.1.call-update) | async-done | bytes 4915216 | tf_op jit(solution)/shard_map/all_gather | solution.py:72
  468.6 19.1 multiply_convert_fusion.1
  523.6 220.2 %while.31 = (s32[]{:T(128)}, f32[20,768,64]{1,2,0:T(8,128)}, f32[20,1024,64]{1,2,0:T(8,128)}, f32[20,1024,64]{1,2,0:T(8,128)}, bf16[20,768,64]{2,1,0:T(8,128)(2,...) while((s32[]{:T(128)}, f32[20,768,64]{1,2,0:T(8,128)}, ...), condition=%wide.region_9.10_spmd.clone.clone, body=%wide.region_7.9_spmd.clone.sunk.clone | while | flops 511294720 | bytes 25910384 | solution.py:253
  752.7 77.3 %copy.93 = f32[4,1024,320]{0,2,1:T(8,128)} copy(f32[4,1024,320]{1,0,2:T(4,128)} %bitcast.269) | data formatting | bytes 10485760
  830.0 144.6 %reshape.360 = f32[1024,1280]{1,0:T(8,128)} reshape(f32[1024,320,4]{2,1,0:T(8,128)} %bitcast.50) | data formatting | bytes 10485760
  1024.2 47.0 %reshape.361 = bf16[256,320,4]{2,1,0:T(8,128)(2,1)} reshape(f32[256,1280]{1,0:T(8,128)} %reduce-scatter.53.cloned.1.call-done) | data formatting | bytes 1966080
  1071.2 18.7 copy.94
  1135.9 64.5 %reduce-scatter.57.cloned.1.call-done = f32[120,960]{1,0:T(8,128)} async-done(((f32[960,960]{1,0:T(8,128)}), f32[120,960]{1,0:T(8,128)}) %reduce-scatter.57.cloned.1.call-update) | async-done | bytes 460816
  1211.5 56.9 %reduce-scatter.39.cloned.1.call-done = f32[960,40]{0,1:T(8,128)} async-done(((f32[960,320]{0,1:T(8,128)}), f32[960,40]{0,1:T(8,128)}) %reduce-scatter.39.cloned.1.call-update) | async-done | bytes 153616 | tf_op jit(solution)/shard_map/reduce_scatter | solution.py:304
  1270.3 65.4 %reduce-scatter.41.cloned.1.call-done = f32[960,40]{0,1:T(8,128)} async-done(((f32[960,320]{0,1:T(8,128)}), f32[960,40]{0,1:T(8,128)}) %reduce-scatter.41.cloned.1.call-update) | async-done | bytes 153616 | tf_op jit(solution)/shard_map/reduce_scatter | solution.py:305
  1337.7 178.6 %reduce-scatter.47.cloned.1.call-done = f32[960,320]{0,1:T(8,128)} async-done(((f32[960,2560]{0,1:T(8,128)}), f32[960,320]{0,1:T(8,128)}) %reduce-scatter.47.cloned.1.call-update) | async-done | bytes 1228816 | tf_op jit(solution)/shard_map/reduce_scatter | solution.py:308
  1519.3 177.8 %reduce-scatter.45.cloned.1.call-done = f32[960,320]{0,1:T(8,128)} async-done(((f32[960,2560]{0,1:T(8,128)}), f32[960,320]{0,1:T(8,128)}) %reduce-scatter.45.cloned.1.call-update) | async-done | bytes 1228816 | tf_op jit(solution)/shard_map/reduce_scatter | solution.py:307
  1700.8 168.7 %reduce-scatter.49.cloned.1.call-done = f32[2560,120]{0,1:T(8,128)} async-done(((f32[2560,960]{0,1:T(8,128)}), f32[2560,120]{0,1:T(8,128)}) %reduce-scatter.49.cloned.1.call-update) | async-done | bytes 1228816 | tf_op jit(solution)/shard_map/reduce_scatter | solution.py:309
  1893.8 22.8 %reduce-scatter.37.cloned.1.call-done = f32[240,120]{1,0:T(8,128)} async-done(((f32[960,120]{1,0:T(8,128)}), f32[240,120]{1,0:T(8,128)}) %reduce-scatter.37.cloned.1.call-update) | async-done | bytes 115216 | tf_op jit(solution)/shard_map/reduce_scatter | solution.py:313
  1925.0 59.1 %reduce-scatter.55.cloned.1.call-done = f32[240,1]{1,0:T(8,128)} async-done(((f32[1920,1]{1,0:T(8,128)}), f32[240,1]{1,0:T(8,128)}) %reduce-scatter.55.cloned.1.call-update) | async-done | bytes 976
  2007.8 23.0 %reduce-scatter.61.cloned.1.call-done = f32[240,40]{1,0:T(8,128)} async-done(((f32[960,40]{1,0:T(8,128)}), f32[240,40]{1,0:T(8,128)}) %reduce-scatter.61.cloned.1.call-update) | async-done | bytes 38416
  2033.1 27.8 %reduce-scatter.67.cloned.1.call-done = f32[240,320]{1,0:T(8,128)} async-done(((f32[960,320]{1,0:T(8,128)}), f32[240,320]{1,0:T(8,128)}) %reduce-scatter.67.cloned.1.call-update) | async-done | bytes 307216
  2062.0 28.9 %reduce-scatter.65.cloned.1.call-done = f32[240,320]{1,0:T(8,128)} async-done(((f32[960,320]{1,0:T(8,128)}), f32[240,320]{1,0:T(8,128)}) %reduce-scatter.65.cloned.1.call-update) | async-done | bytes 307216
  2093.5 25.7 %reduce-scatter.51.cloned.1.call-done = f32[640,120]{0,1:T(8,128)} async-done(((f32[2560,120]{0,1:T(8,128)}), f32[640,120]{0,1:T(8,128)}) %reduce-scatter.51.cloned.1.call-update) | async-done | bytes 307216 | tf_op jit(solution)/shard_map/reduce_scatter | solution.py:319
  (539 shorter events, 714.9 us)
Async XLA Ops:
  7.2 170.7 %all-gather.14.cloned.1.call-start = ((), (), s32[]{:S(2)}) async-start(), calls=%async_computation.17 | async-start | bytes 2211840 | tf_op jit(solution)/shard_map/all_gather | solution.py:66
  15.6 171.2 %all-gather.16.cloned.1.call-start = ((), (), s32[]{:S(2)}) async-start(), calls=%async_computation.18 | async-start | bytes 3276800 | tf_op jit(solution)/shard_map/all_gather | solution.py:150
  92.5 103.9 %all-gather.18.cloned.1.call-start = ((), (), s32[]{:S(2)}) async-start(), calls=%async_computation.19 | async-start | bytes 3276800 | tf_op jit(solution)/shard_map/all_gather | solution.py:151
  133.9 201.1 %all-gather.20.cloned.1.call-start = ((), (), s32[]{:S(2)}) async-start(), calls=%async_computation.20 | async-start | bytes 2211840 | tf_op jit(solution)/shard_map/all_gather | solution.py:69
  140.5 202.4 %all-gather.24.cloned.1.call-start = ((), (), s32[]{:S(2)}) async-start(), calls=%async_computation.22 | async-start | bytes 5898240 | tf_op jit(solution)/shard_map/all_gather | solution.py:71
  154.5 231.9 %all-gather.22.cloned.1.call-start = ((), (), s32[]{:S(2)}) async-start(), calls=%async_computation.21 | async-start | bytes 5898240 | tf_op jit(solution)/shard_map/all_gather | solution.py:70
  164.5 304.1 %all-gather.26.cloned.1.call-start = ((), (), s32[]{:S(2)}) async-start(), calls=%async_computation.23 | async-start | bytes 5529600 | tf_op jit(solution)/shard_map/all_gather | solution.py:72
  172.8 834.4 %reduce-scatter.35.cloned.1.call-start = ((), (), s32[]{:S(2)}) async-start(), calls=%async_computation.24 | async-start | bytes 6553600 | tf_op jit(solution)/shard_map/reduce_scatter | solution.py:264
  743.8 280.4 %reduce-scatter.53.cloned.1.call-start = ((), (), s32[]{:S(2)}) async-start(), calls=%async_computation.33 | async-start | bytes 6553600
  974.6 152.6 %reduce-scatter.63.cloned.1.call-start = ((), (), s32[]{:S(2)}) async-start(), calls=%async_computation.38 | async-start | bytes 4423680
  983.1 217.3 %reduce-scatter.57.cloned.1.call-start = ((), (), s32[]{:S(2)}) async-start(), calls=%async_computation.35 | async-start | bytes 4423680
  1007.2 261.2 %reduce-scatter.39.cloned.1.call-start = ((), (), s32[]{:S(2)}) async-start(), calls=%async_computation.26 | async-start | bytes 1474560 | tf_op jit(solution)/shard_map/reduce_scatter | solution.py:304
  1012.5 323.2 %reduce-scatter.41.cloned.1.call-start = ((), (), s32[]{:S(2)}) async-start(), calls=%async_computation.27 | async-start | bytes 1474560 | tf_op jit(solution)/shard_map/reduce_scatter | solution.py:305
  1092.0 424.3 %reduce-scatter.47.cloned.1.call-start = ((), (), s32[]{:S(2)}) async-start(), calls=%async_computation.30 | async-start | bytes 11796480 | tf_op jit(solution)/shard_map/reduce_scatter | solution.py:308
  1103.0 594.1 %reduce-scatter.45.cloned.1.call-start = ((), (), s32[]{:S(2)}) async-start(), calls=%async_computation.29 | async-start | bytes 11796480 | tf_op jit(solution)/shard_map/reduce_scatter | solution.py:307
  1115.4 754.1 %reduce-scatter.49.cloned.1.call-start = ((), (), s32[]{:S(2)}) async-start(), calls=%async_computation.31 | async-start | bytes 11059200 | tf_op jit(solution)/shard_map/reduce_scatter | solution.py:309
  1127.2 765.1 %reduce-scatter.43.cloned.1.call-start = ((), (), s32[]{:S(2)}) async-start(), calls=%async_computation.28 | async-start | bytes 614400 | tf_op jit(solution)/shard_map/reduce_scatter | solution.py:316
  1129.3 787.3 %reduce-scatter.37.cloned.1.call-start = ((), (), s32[]{:S(2)}) async-start(), calls=%async_computation.25 | async-start | bytes 614400 | tf_op jit(solution)/shard_map/reduce_scatter | solution.py:313
  1202.4 781.6 %reduce-scatter.55.cloned.1.call-start = ((), (), s32[]{:S(2)}) async-start(), calls=%async_computation.34 | async-start | bytes 1105920
  1211.4 795.4 %reduce-scatter.59.cloned.1.call-start = ((), (), s32[]{:S(2)}) async-start(), calls=%async_computation.36 | async-start | bytes 614400
  1270.3 760.5 %reduce-scatter.61.cloned.1.call-start = ((), (), s32[]{:S(2)}) async-start(), calls=%async_computation.37 | async-start | bytes 614400
  1337.7 723.2 %reduce-scatter.67.cloned.1.call-start = ((), (), s32[]{:S(2)}) async-start(), calls=%async_computation.40 | async-start | bytes 1843200
  1519.3 571.6 %reduce-scatter.65.cloned.1.call-start = ((), (), s32[]{:S(2)}) async-start(), calls=%async_computation.39 | async-start | bytes 1843200
  1700.1 419.2 %reduce-scatter.51.cloned.1.call-start = ((), (), s32[]{:S(2)}) async-start(), calls=%async_computation.32 | async-start | bytes 1536000 | tf_op jit(solution)/shard_map/reduce_scatter | solution.py:319
  (44 other events, 1003.6 us)
Sparse Core Ops, SparseCore 0:
  15.7 49.7 all-gather.13
  92.6 22.4 all-gather.15
  134.0 25.9 all-gather.17
  162.6 51.0 all-gather.19
  215.7 84.4 all-gather.23
  302.3 84.0 all-gather.21
  388.6 79.9 all-gather.25
  743.9 49.4 reduce-scatter.34
  974.7 49.4 reduce-scatter.52
  1027.7 84.6 reduce-scatter.62
  1116.1 84.2 reduce-scatter.56
  1203.6 64.6 reduce-scatter.38
  1271.7 63.9 reduce-scatter.40
  1339.2 177.1 reduce-scatter.46
  1519.8 177.3 reduce-scatter.44
  1700.6 168.8 reduce-scatter.48
  1871.8 20.3 reduce-scatter.42
  1895.2 21.3 reduce-scatter.36
  1920.0 64.0 reduce-scatter.54
  1986.5 20.3 reduce-scatter.58
  2009.4 21.3 reduce-scatter.60
  2033.4 27.3 reduce-scatter.66
  2063.4 27.3 reduce-scatter.64
  2093.3 25.9 reduce-scatter.50
where the time goes:
time: 2140 us; the launch traced here: 2130 us
  waiting for transfers between devices  1040 us (49%)
  matrix products  447 us (21%)
  local copies, waits for them, and re-layouts  415 us (19%)
  blocking collectives  151 us (7%)
  other arithmetic  53.6 us (3%)
    unnamed x127, local copies, waits for them, and re-layouts  346 us
    unnamed x32, waiting for transfers between devices  231 us
    reduce_scatter x1, waiting for transfers between devices, local(): lax.psum_scatter(up_part, 'dp', scatter_dimension=1, tiled=True)  179 us
    reduce_scatter x1, waiting for transfers between devices, local(): lax.psum_scatter(gate_part, 'dp', scatter_dimension=1, tiled=True)  178 us
    reduce_scatter x1, waiting for transfers between devices, local(): lax.psum_scatter(down_part, 'dp', scatter_dimension=1, tiled=True)  169 us
    dot_general x40, matrix products, block_scores(): lax.dot_general(query_block, key_block, contract_last, preferred_element_...  88.5 us
    all_gather x1, waiting for transfers between devices, local(): lax.all_gather(row_parts[6], 'dp', axis=1, tiled=True)  71.2 us
    reduce_scatter x1, waiting for transfers between devices, local(): lax.psum_scatter(value_part, 'dp', scatter_dimension=1, tiled=True)  65.4 us
  transfers between devices with their start and end apart: 24, of which 17 were waited for; matrix products, arithmetic and copies ran while one was open for 29% of the time, Pallas kernels for 0%

commit v1 on v0

--- a/solution.py
+++ b/solution.py
@@ -1,9 +1,13 @@
+import functools
 import math
 
 import jax
 import jax.numpy as jnp
 from jax import lax
+from jax.experimental import pallas as pl
+from jax.experimental.pallas import tpu as pltpu
 from jax.sharding import PartitionSpec as P
+
 
 QH = 15
 KVH = 5
@@ -34,7 +38,7 @@
 
 
 def unrotate(grad_turned, cos_table, sin_table):
-    primal_out, pullback = jax.vjp(lambda values: rotate(values, cos_table, sin_table), grad_turned)
+    _, pullback = jax.vjp(lambda values: rotate(values, cos_table, sin_table), grad_turned)
     return pullback(grad_turned)[0]
 
 
@@ -195,7 +199,7 @@
     grad_product = lax.dot_general(
         seed_low, refetched[6], contract_last, preferred_element_type=jnp.float32
     )
-    primal_gate, gate_pull = jax.vjp(
+    _, gate_pull = jax.vjp(
         lambda gate_in, up_in: jax.nn.silu(gate_in) * up_in, gate_pre, up_pre
     )
     grad_gate, grad_up = gate_pull(grad_product)
@@ -210,7 +214,7 @@
     grad_normed_two = lax.dot_general(
         grad_gate, refetched[4], contract_last, preferred_element_type=jnp.float32
     ) + lax.dot_general(grad_up, refetched[5], contract_last, preferred_element_type=jnp.float32)
-    primal_two, second_pull = jax.vjp(rms_scale, middle, gains_back[model_width:])
+    _, second_pull = jax.vjp(rms_scale, middle, gains_back[model_width:])
     grad_middle_norm, gain_two_part = second_pull(grad_normed_two)
     grad_middle = seed_high + grad_middle_norm
     grad_branch = grad_middle.astype(jnp.bfloat16)
@@ -291,7 +295,7 @@
             grad_value, refetched[2], contract_last, preferred_element_type=jnp.float32
         )
     )
-    primal_one, first_pull = jax.vjp(rms_scale, inputs_f32, gains_back[:model_width])
+    _, first_pull = jax.vjp(rms_scale, inputs_f32, gains_back[:model_width])
     grad_inputs_norm, gain_one_part = first_pull(grad_normed)
     hidden_grad = (
         (grad_middle + grad_inputs_norm)
@@ -334,6 +338,532 @@
     )
 
 
+BF=jnp.bfloat16; F32=jnp.float32
+T=1024; D=960; DP=1024
+NT=(((1,),(1,)),((),())); NN=(((1,),(0,)),((),())); TN=(((0,),(0,)),((),()))
+def dot(a,b,dn=NN): return lax.dot_general(a,b,dn,preferred_element_type=F32)
+ANY=pl.BlockSpec(memory_space=pl.ANY)
+SMEM=pl.BlockSpec(memory_space=pltpu.SMEM)
+def flip(a,b): return lax.bitwise_xor(a,b)
+def const(shape): return pl.BlockSpec(shape,lambda *g:(0,)*len(shape))
+def params(): return pltpu.CompilerParams(vmem_limit_bytes=60<<20)
+def cost(us): return pl.CostEstimate(flops=int(us*9e8),bytes_accessed=int(us*2e6),transcendentals=0)
+def sds(shape,dt): return jax.ShapeDtypeStruct(shape,dt)
+
+def pieces_of(idx, order):
+    for p in range(4):
+        for f in range(2):
+            dx,dy=(p%2,f) if order=="yx" else (f,p%2)
+            x=flip(idx[1],dx); ctx=flip(idx[2],dy)*2+flip(idx[3],p//2)
+            yield p,f,x,ctx,flip(idx[2],dy)
+
+def load_rows(idx, pieces, dst, sem, groups):
+    for z in groups:
+        dz=lax.rem(z-idx[0]+4,4)
+        for p,f,x,ctx,_ in pieces_of(idx,"yx"):
+            pltpu.make_async_copy(pieces[p].at[f,dz], dst.at[2*z+x,pl.ds(pl.multiple_of(ctx*240,16),240)], sem.at[z//2]).start()
+
+def wait_rows(dst, sem, j):
+    half=dst.at[pl.ds(4*j,4),pl.ds(0,960)]
+    pltpu.make_async_copy(half,half,sem.at[j]).wait()
+
+def load_cols(idx, pieces, dst, sem):
+    for p,f,x,ctx,y in pieces_of(idx,"xy"):
+        for dz in range(4):
+            for t in range(dst.shape[2]//128):
+                pltpu.make_async_copy(pieces[p].at[f,dz,:,pl.ds(128*t,128)], dst.at[ctx,lax.rem(idx[0]+dz,4)*2+x,pl.ds(128*t,128)], sem.at[y]).start()
+
+def wait_cols(dst, sem, j):
+    half=dst.at[pl.ds(2*j,2)]
+    pltpu.make_async_copy(half,half,sem.at[j]).wait()
+
+def ffn_fwd_kernel(S, last, idx, n2, mid, *refs):
+    gp=refs[:4]; dp_=refs[4:8]
+    out, h_ref, wd_ref, gu_s, d_s, acc, sem = refs[8:]
+    j=pl.program_id(0); i=pl.program_id(1)
+    @pl.when((j==0)&(i==0))
+    def _():
+        load_rows(idx,gp,gu_s,sem.at[0],(0,1))
+        load_cols(idx,dp_,d_s,sem.at[1])
+        load_rows(idx,gp,gu_s,sem.at[0],(2,3))
+    @pl.when(i==0)
+    def _():
+        wait_rows(gu_s,sem.at[0],j); wait_cols(d_s,sem.at[1],j)
+        for k in range(4): gu_s[4*j+k,960:1024,:]=jnp.zeros((64,2*S),BF)
+        for b in range(2):
+            wd_ref[0,b*2*S:(b+1)*2*S,:]=jnp.concatenate([d_s[2*j+b,k][:,:120] for k in range(8)]+[jnp.zeros((2*S,64),BF)],axis=-1)
+    rows=pl.ds(pl.multiple_of(i*256,256),256)
+    xb=n2[rows,:]
+    acts=[]
+    for q in range(2):
+        w=jnp.concatenate([gu_s[4*j+2*q],gu_s[4*j+2*q+1]],axis=-1)
+        h=dot(xb,w)
+        h_ref[0,:,q*4*S:(q+1)*4*S]=h.astype(BF)
+        for b in range(2):
+            g=h[:,b*2*S:b*2*S+S]; u=h[:,b*2*S+S:b*2*S+2*S]
+            acts.append((g/(1+jnp.exp(-g))*u).astype(BF))
+    act=jnp.concatenate(acts,axis=-1)
+    o=dot(act,wd_ref[0])
+    @pl.when(j==0)
+    def _(): acc[rows,:]=o+mid[rows,:]
+    @pl.when(j==1)
+    def _():
+        r=acc[rows,:]+o
+        if last: out[0,0]=r.T[:D,:].astype(BF)
+        else: out[...]=r
+
+def ffn_fwd(idx, n2, mid, gp, dp_, last):
+    S=gp[0].shape[3]//2
+    full=pl.BlockSpec((T,DP),lambda j,i,idx:(0,0))
+    if last: ospec=pl.BlockSpec((1,1,D,256),lambda j,i,idx:(flip((i*j)%2,idx[3]),flip((i*j)//2,idx[2]),0,0))
+    else: ospec=pl.BlockSpec((256,DP),lambda j,i,idx:(i*j,0))
+    return pl.pallas_call(functools.partial(ffn_fwd_kernel,S,last), grid_spec=pltpu.PrefetchScalarGridSpec(num_scalar_prefetch=1,grid=(2,4),
+        in_specs=[full,full]+[ANY]*8,
+        out_specs=[ospec, pl.BlockSpec((1,256,8*S),lambda j,i,idx:(j,i,0)), pl.BlockSpec((1,4*S,DP),lambda j,i,idx:(j,0,0))],
+        scratch_shapes=[pltpu.VMEM((8,DP,2*S),BF),pltpu.VMEM((4,8,2*S,128),BF),pltpu.VMEM((T,DP),F32),pltpu.SemaphoreType.DMA((2,2))]),
+        out_shape=[sds((2,2,D,256),BF) if last else sds((T,DP),F32),sds((2,T,8*S),BF),sds((2,4*S,DP),BF)],
+        compiler_params=params(), cost_estimate=cost(20), name="ffn_fwd")(idx,n2,mid,*gp,*dp_)
+
+def slot_of(idx, dpi, ctx):
+    z=dpi//2; x=dpi%2; y=ctx//2; c=ctx%2
+    return flip(c,idx[3]), flip(x,idx[1]), flip(y,idx[2]), lax.rem(z-idx[0]+4,4)
+
+def put(idx, src, keep, send, sem, yx, dpi, ctx, *at):
+    c,x,y,z=slot_of(idx,dpi,ctx)
+    if yx: x,y=y,x
+    @pl.when(c==0)
+    def _(): pltpu.make_async_copy(src,keep.at[(x,y,z)+at],sem).start()
+    @pl.when(c==1)
+    def _(): pltpu.make_async_copy(src,send.at[(x,y,z)+at],sem).start()
+
+def ffn_bwd_kernel(S, idx, cb, n2, h, wd, dn2in, *refs):
+    gp=refs[:4]
+    dn2, gk, gs, gu_s, dh_s, act_s, dw_s, dd_s, sem, osem = refs[4:]
+    q=pl.program_id(0)
+    nq=4*S
+    @pl.when(q==0)
+    def _(): load_rows(idx,gp,gu_s,sem,(0,1,2,3))
+    wait_rows(gu_s,sem,q)
+    for k in range(4): gu_s[4*q+k,960:1024,:]=jnp.zeros((64,2*S),BF)
+    w=jnp.concatenate([gu_s[4*q+k] for k in range(4)],axis=-1)
+    wdq=wd[0]
+    def rows_step(i,_):
+        rows=pl.ds(pl.multiple_of(i*256,256),256)
+        dact=dot(cb[rows,:],wdq,NT)
+        parts=[];acts=[]
+        for b in range(4):
+            g=h[0,rows,b*2*S:b*2*S+S].astype(F32); u=h[0,rows,b*2*S+S:b*2*S+2*S].astype(F32)
+            da=dact[:,b*S:(b+1)*S]
+            sg=1/(1+jnp.exp(-g)); sl=g*sg
+            acts.append((sl*u).astype(BF))
+            parts.append((da*u*(sg+sl*(1-sg))).astype(BF)); parts.append((da*sl).astype(BF))
+        dh=jnp.concatenate(parts,axis=-1)
+        dh_s[rows,:]=dh; act_s[rows,:]=jnp.concatenate(acts,axis=-1)
+        t=dot(dh,w,NT)
+        dn2[rows,:]=jnp.where(q==0,dn2in[rows,:],dn2[rows,:])+t
+        return 0
+    lax.fori_loop(0,4,rows_step,0)
+    @pl.when(q==1)
+    def _():
+        pltpu.make_async_copy(dw_s.at[pl.ds(0,960)],dw_s.at[pl.ds(0,960)],osem.at[0]).wait()
+        pltpu.make_async_copy(dd_s,dd_s,osem.at[1]).wait()
+    def dw_step(m,_):
+        cols=pl.ds(pl.multiple_of(m*256,256),256)
+        dw_s[cols,:]=dot(n2[:,cols],dh_s[...],TN).astype(BF)
+        return 0
+    lax.fori_loop(0,4,dw_step,0)
+    for b in range(4):
+        for ctx in range(4):
+            put(idx,dw_s.at[pl.ds(ctx*240,240),pl.ds(b*2*S,2*S)],gk,gs,osem.at[0],False,4*q+b,ctx,pl.ds(0,240))
+    for m in range(nq//256):
+        r=dot(act_s[:,m*256:(m+1)*256],cb[...],TN)
+        for k in range(8):
+            dd_s[k,m*256:(m+1)*256,:]=jnp.concatenate([r[:,k*120:(k+1)*120],jnp.zeros((256,8),F32)],axis=-1).astype(BF)
+    for k in range(8):
+        for cc in range(2):
+            for t in range(2*S//128):
+                put(idx,dd_s.at[k,pl.ds(cc*2*S+128*t,128)],gk,gs,osem.at[1],True,k,2*q+cc,pl.ds(240,128),pl.ds(128*t,128))
+    @pl.when(q==1)
+    def _():
+        pltpu.make_async_copy(dw_s.at[pl.ds(0,960)],dw_s.at[pl.ds(0,960)],osem.at[0]).wait()
+        pltpu.make_async_copy(dd_s,dd_s,osem.at[1]).wait()
+
+def ffn_bwd(idx, cb, n2, h, wd, dn2in, gp):
+    S=gp[0].shape[3]//2
+    full=const((T,DP))
+    return pl.pallas_call(functools.partial(ffn_bwd_kernel,S), grid=(2,),
+        in_specs=[SMEM,full,full,pl.BlockSpec((1,T,8*S),lambda q:(q,0,0)),pl.BlockSpec((1,4*S,DP),lambda q:(q,0,0)),full]+[ANY]*4,
+        out_specs=[full,ANY,ANY],
+        out_shape=[sds((T,DP),F32)]+[sds((2,2,4,368,2*S),BF)]*2,
+        scratch_shapes=[pltpu.VMEM((8,DP,2*S),BF),pltpu.VMEM((T,8*S),BF),pltpu.VMEM((T,4*S),BF),pltpu.VMEM((DP,8*S),BF),pltpu.VMEM((8,4*S,128),BF),pltpu.SemaphoreType.DMA((2,)),pltpu.SemaphoreType.DMA((2,))],
+        compiler_params=params(), cost_estimate=cost(33), name="ffn_bwd")(idx,cb,n2,h,wd,dn2in,*gp)
+
+NEG=-1e30
+QB=256
+def attn_fwd_kernel(q, k, v, o, lse):
+    ri=lax.broadcasted_iota(jnp.int32,(QB,QB),0); ci=lax.broadcasted_iota(jnp.int32,(QB,QB),1)
+    for qi in range(T//QB):
+        rows=slice(qi*QB,(qi+1)*QB); kn=(qi+1)*QB
+        qb=q[0,rows,:]
+        s=dot(qb,k[0,0:kn,:],NT)
+        sd=jnp.where(ci<=ri,s[:,kn-QB:],NEG)
+        s=sd if qi==0 else jnp.concatenate([s[:,:kn-QB],sd],axis=-1)
+        m=jnp.max(s,axis=-1,keepdims=True)
+        p=jnp.exp(s-m)
+        r=dot(p.astype(BF),v[0,0:kn,:])
+        l=r[:,64:65]
+        o[0,rows,:]=(r/l).astype(BF)
+        e=jnp.broadcast_to(m+jnp.log(l),(QB,128))
+        lse[0,:,rows]=e.T[0:1,:]
+
+def attn_fwd(q,k,v,g0,ng):
+    qs=pl.BlockSpec((1,T,128),lambda g,r:(3*(g+g0)+r,0,0)); ks=pl.BlockSpec((1,T,128),lambda g,r:(g+g0,0,0)); os_=pl.BlockSpec((1,T,128),lambda g,r:(3*g+r,0,0))
+    return pl.pallas_call(attn_fwd_kernel,grid=(ng,3),in_specs=[qs,ks,ks],
+        out_specs=[os_,pl.BlockSpec((1,1,T),lambda g,r:(3*g+r,0,0))],
+        out_shape=[sds((3*ng,T,128),BF),sds((3*ng,1,T),F32)],compiler_params=params(),cost_estimate=cost(6*ng), name="attn_fwd")(q,k,v)
+
+def unrot(g,c,s,low):
+    t=jnp.where(low,pltpu.roll(g,96,1),-pltpu.roll(g,32,1))
+    return g*c+t*s
+
+def attn_bwd_kernel(q,k,v,do,lse,c,s,dq,dk,dv,dka,dva,dqa):
+    r_=pl.program_id(1)
+    @pl.when(r_==0)
+    def _():
+        dka[...]=jnp.zeros_like(dka); dva[...]=jnp.zeros_like(dva)
+    ki=lax.broadcasted_iota(jnp.int32,(QB,QB),0); qi_=lax.broadcasted_iota(jnp.int32,(QB,QB),1)
+    low=lax.broadcasted_iota(jnp.int32,(QB,128),1)%64<32
+    for qi in range(T//QB):
+        rows=slice(qi*QB,(qi+1)*QB); kn=(qi+1)*QB
+        qb=q[0,rows,:]; dob=do[0,rows,:]; kb=k[0,0:kn,:]
+        st=dot(kb,qb,NT)
+        pt=jnp.exp(st-lse[0,:,rows])
+        pd=jnp.where(ki<=qi_,pt[kn-QB:],0.0)
+        pt=pd if qi==0 else jnp.concatenate([pt[:kn-QB],pd],axis=0)
+        dpt=dot(v[0,0:kn,:],dob,NT)
+        dva[0:kn,:]+=dot(pt.astype(BF),dob)
+        t=pt*dpt
+        delta=jnp.sum(t,axis=0,keepdims=True)
+        dst=(t-pt*delta).astype(BF)
+        dka[0:kn,:]+=dot(dst,qb)
+        dqr=dot(dst,kb,TN)*0.125
+        dq[0,rows,:]=unrot(dqr,c[rows,:],s[rows,:],low).astype(BF)
+    @pl.when(r_==2)
+    def _():
+        for qi in range(T//QB):
+            rows=slice(qi*QB,(qi+1)*QB)
+            dk[0,rows,:]=unrot(dka[rows,:],c[rows,:],s[rows,:],low).astype(BF)
+            dv[0,rows,:]=dva[rows,:].astype(BF)
+
+def attn_bwd(q,k,v,do,lse,c,s,g0,ng):
+    qs=pl.BlockSpec((1,T,128),lambda g,r:(3*(g+g0)+r,0,0)); ks=pl.BlockSpec((1,T,128),lambda g,r:(g+g0,0,0))
+    qo=pl.BlockSpec((1,T,128),lambda g,r:(3*g+r,0,0)); ko=pl.BlockSpec((1,T,128),lambda g,r:(g,0,0))
+    return pl.pallas_call(attn_bwd_kernel,grid=(ng,3),in_specs=[qs,ks,ks,qs,pl.BlockSpec((1,1,T),lambda g,r:(3*g+r,0,0)),const((T,128)),const((T,128))],
+        out_specs=[qo,ko,ko],
+        out_shape=[sds((3*ng,T,128),BF),sds((ng,T,128),BF),sds((ng,T,128),BF)],
+        scratch_shapes=[pltpu.VMEM((T,128),F32),pltpu.VMEM((T,128),F32),pltpu.VMEM((8,128),F32)],
+        compiler_params=params(),cost_estimate=cost(9*ng), name="attn_bwd")(q,k,v,do,lse,c,s)
+
+EPS=1e-5
+WN=1664
+CUT=160
+def prefetch(grid,in_specs,out_specs,scratch): return pltpu.PrefetchScalarGridSpec(num_scalar_prefetch=1,grid=grid,in_specs=in_specs,out_specs=out_specs,scratch_shapes=scratch)
+def tok(i,idx): return (flip(i%2,idx[3]),flip(i//2,idx[2]),0,0)
+tok_spec=lambda: pl.BlockSpec((1,1,D,256),tok)
+row_spec=lambda n: pl.BlockSpec((256,n),lambda i,idx:(i,0))
+head_spec=lambda h: pl.BlockSpec((h,256,128),lambda i,idx:(0,i,0))
+def cst(shape): return pl.BlockSpec(shape,lambda *g:(0,)*len(shape))
+def zeros(r,n,dt=F32): return jnp.zeros((r,n),dt)
+
+def qkv_kernel(idx, x, c, s, *refs):
+    pa=refs[:4]; pb=refs[4:8]
+    n1,q,k,v,w,wo,gains,s1,sem=refs[8:]
+    i=pl.program_id(0)
+    @pl.when(i==0)
+    def _():
+        for order,pc,lo,n in (("yx",pa,0,CUT),("xy",pb,CUT,256-CUT)):
+            for p,f,xx,ctx,_ in pieces_of(idx,order):
+                for dz in range(4):
+                    pltpu.make_async_copy(pc[p].at[f,dz], s1.at[lax.rem(idx[0]+dz,4)*2+xx,ctx,pl.ds(lo,n)], sem).start()
+        pltpu.make_async_copy(s1,s1,sem).wait()
+        for t in range(4):
+            rows=slice(240*t,240*t+240)
+            w[rows,:]=jnp.concatenate([s1[d,t,0:240,0:120] for d in range(8)]+[s1[d,t,0:240,128:168] for d in range(8)]+[s1[d,t,0:240,168:208] for d in range(8)]+[zeros(240,64,BF)],axis=-1)
+            wo[rows,:]=jnp.concatenate([s1[d,t,0:240,256:376] for d in range(8)]+[zeros(240,64,BF)],axis=-1)
+        w[960:1024,:]=zeros(64,WN,BF); wo[960:1024,:]=zeros(64,DP,BF)
+        gl=[s1[d,t,240:256,0:128].astype(F32)[0:1,0:60] for d in range(8) for t in range(4)]
+        gains[0:1,:]=jnp.concatenate(gl[:16]+[zeros(1,64)],axis=-1)
+        gains[1:2,:]=jnp.concatenate(gl[16:]+[zeros(1,64)],axis=-1)
+    xf=x[:,0:D].astype(F32)
+    r=lax.rsqrt(jnp.sum(xf*xf,axis=-1,keepdims=True)*(1.0/D)+EPS)
+    n=jnp.concatenate([(xf*r*gains[0:1,0:D]).astype(BF),zeros(256,64,BF)],axis=-1)
+    n1[...]=n
+    h=dot(n,w[...])
+    low=lax.broadcasted_iota(jnp.int32,(256,128),1)%64<32
+    z64=zeros(256,64,BF)
+    one=jnp.where(lax.broadcasted_iota(jnp.int32,(256,64),1)==0,1.0,0.0).astype(BF)
+    for t in range(10):
+        g=h[:,128*t:128*t+128]
+        u=jnp.where(low,-pltpu.roll(g,96,1),pltpu.roll(g,32,1))
+        o=g*c[...]+u*s[...]
+        for e in range(2):
+            hd=2*t+e
+            oh=o[:,64*e:64*e+64]
+            if hd<15: q[hd]=jnp.concatenate([(oh*0.125).astype(BF),z64],axis=-1)
+            else: k[hd-15]=jnp.concatenate([oh.astype(BF),z64],axis=-1)
+    for e in range(5):
+        v[e]=jnp.concatenate([h[:,1280+64*e:1344+64*e].astype(BF),one],axis=-1)
+
+def qkv_fwd(idx,x,c,s,pa,pb):
+    return pl.pallas_call(qkv_kernel,grid_spec=prefetch((4,),[row_spec(DP),row_spec(128),row_spec(128)]+[ANY]*8,
+        [row_spec(DP),head_spec(15),head_spec(5),head_spec(5),cst((DP,WN)),cst((DP,DP)),cst((2,DP))],
+        [pltpu.VMEM((8,4,256,384),BF),pltpu.SemaphoreType.DMA]),
+        out_shape=[sds((T,DP),BF),sds((15,T,128),BF),sds((5,T,128),BF),sds((5,T,128),BF),sds((DP,WN),BF),sds((DP,DP),BF),sds((2,DP),F32)],
+        compiler_params=params(),cost_estimate=cost(16), name="qkv_fwd")(idx,x,c,s,*pa,*pb)
+
+def out_kernel(idx,o1,o2,x,gains,wo,att,mid,n2):
+    a=jnp.concatenate([o[h][:,0:64] for o in (o1,o2) for h in range(o.shape[0])]+[zeros(256,64,BF)],axis=-1)
+    att[...]=a
+    m=dot(a,wo[...])+x[...].astype(F32)
+    mid[...]=m
+    r=lax.rsqrt(jnp.sum(m*m,axis=-1,keepdims=True)*(1.0/D)+EPS)
+    n2[...]=(m*r*gains[1:2,:]).astype(BF)
+
+def out_fwd(idx,o1,o2,x,gains,wo):
+    return pl.pallas_call(out_kernel,grid_spec=prefetch((4,),[head_spec(o1.shape[0]),head_spec(o2.shape[0]),row_spec(DP),cst((2,DP)),cst((DP,DP))],
+        [row_spec(DP)]*3,[]),out_shape=[sds((T,DP),BF),sds((T,DP),F32),sds((T,DP),BF)],compiler_params=params(),cost_estimate=cost(9), name="out_fwd")(idx,o1,o2,x,gains,wo)
+
+def tok_in_kernel(idx,h,r,g,o):
+    y=idx[2]; c=idx[3]
+    for ys,cs,v in ((0,0,h[2*y+c]),(1,0,r[c]),(0,1,g[0]),(1,1,g[1])):
+        b=2*flip(y,ys)+flip(c,cs)
+        o[pl.ds(pl.multiple_of(256*b,256),256),:]=jnp.concatenate([v,zeros(64,256,BF)],axis=0).T
+def tok_in(idx,h,r,g):
+    return pl.pallas_call(tok_in_kernel,in_specs=[SMEM]+[pl.BlockSpec(memory_space=pltpu.VMEM)]*3,out_specs=pl.BlockSpec(memory_space=pltpu.VMEM),out_shape=sds((T,DP),BF),compiler_params=params(),cost_estimate=cost(4),name="tok_in")(idx,h,r,g)
+
+def out_bwd_kernel(idx,dn2,cb,mid,gains,wo,att,dmid,do,dg,ok,os_,dbr_s,st,sem):
+    i=pl.program_id(0)
+    m=mid[...]; r=lax.rsqrt(jnp.sum(m*m,axis=-1,keepdims=True)*(1.0/D)+EPS)
+    d=dn2[...]; gd=gains[1:2,:]*d
+    dm=cb[...].astype(F32)+r*gd-m*(r*r*r)*(jnp.sum(gd*m,axis=-1,keepdims=True)*(1.0/D))
+    dmid[...]=dm
+    g=jnp.sum(d*m*r,axis=0,keepdims=True)
+    dg[...]=g+jnp.where(i==0,0.0,dg[...])
+    b=dm.astype(BF)
+    dbr_s[pl.ds(pl.multiple_of(i*256,256),256),:]=b
+    da=dot(b,wo[...],NT)
+    z64=zeros(256,64,BF)
+    for h in range(15): do[h]=jnp.concatenate([da[:,64*h:64*h+64].astype(BF),z64],axis=-1)
+    @pl.when(i==3)
+    def _():
+        for mm in range(4):
+            rr=dot(att[:,256*mm:256*mm+256],dbr_s[...],TN)
+            for k in range(8):
+                st[k,256*mm:256*mm+256,:]=jnp.concatenate([rr[:,120*k:120*k+120],zeros(256,8)],axis=-1).astype(BF)
+        for k in range(8):
+            for t in range(4):
+                put(idx,st.at[k,pl.ds(240*t,CUT)],ok,os_,sem,False,k,t,pl.ds(0,CUT)); put(idx,st.at[k,pl.ds(240*t+CUT,240-CUT)],ok,os_,sem,True,k,t,pl.ds(CUT,240-CUT))
+        pltpu.make_async_copy(st.at[:,pl.ds(0,960)],st.at[:,pl.ds(0,960)],sem).wait()
+
+def out_bwd(idx,dn2,cb,mid,gains,wo,att):
+    return pl.pallas_call(out_bwd_kernel,grid_spec=prefetch((4,),[row_spec(DP)]*3+[cst((2,DP)),cst((DP,DP)),cst((T,DP))],
+        [row_spec(DP),head_spec(15),cst((1,DP)),ANY,ANY],[pltpu.VMEM((T,DP),BF),pltpu.VMEM((8,DP,128),BF),pltpu.SemaphoreType.DMA]),
+        out_shape=[sds((T,DP),F32),sds((15,T,128),BF),sds((1,DP),F32)]+[sds((2,2,4,240,128),BF)]*2,
+        compiler_params=params(),cost_estimate=cost(16), name="out_bwd")(idx,dn2,cb,mid,gains,wo,att)
+
+def qkv_bwd_kernel(idx,dq1,dk1,dv1,dq2,dk2,dv2,x,gains,n1,dmid,w,dg2,hg,wk,ws,dh_s,st,sg,dg1,sem):
+    i=pl.program_id(0)
+    dh=jnp.concatenate([r[h][:,0:64] for r in (dq1,dq2,dk1,dk2,dv1,dv2) for h in range(r.shape[0])]+[zeros(256,64,BF)],axis=-1)
+    dh_s[pl.ds(pl.multiple_of(i*256,256),256),:]=dh
+    d=dot(dh,w[...],NT)[:,0:D]
+    xf=x[:,0:D].astype(F32)
+    r=lax.rsqrt(jnp.sum(xf*xf,axis=-1,keepdims=True)*(1.0/D)+EPS)
+    gd=gains[0:1,0:D]*d
+    hh=dmid[:,0:D]+r*gd-xf*(r*r*r)*(jnp.sum(gd*xf,axis=-1,keepdims=True)*(1.0/D))
+    hg[0,0]=jnp.concatenate([hh,zeros(256,64)],axis=-1).T[:D,:].astype(BF)
+    g=jnp.sum(d*xf*r,axis=0,keepdims=True)
+    dg1[...]=g+jnp.where(i==0,0.0,dg1[...])
+    @pl.when(i==3)
+    def _():
+        for m in range(4):
+            r_=dot(n1[:,256*m:256*m+256],dh_s[...],TN)
+            for k in range(8):
+                st[k,256*m:256*m+256,:]=jnp.concatenate([r_[:,120*k:120*k+120],zeros(256,8),r_[:,960+40*k:1000+40*k],r_[:,1280+40*k:1320+40*k],zeros(256,48)],axis=-1).astype(BF)
+        sg[...]=jnp.zeros_like(sg)
+        for k in range(8):
+            for t in range(4):
+                o=(4*k+t)*60
+                src=dg1[:,o:o+60] if k<4 else dg2[:,o-960:o-900]
+                sg[k,t,:,0:128]=jnp.broadcast_to(jnp.concatenate([src,zeros(1,68)],axis=-1),(16,128)).astype(BF)
+                c,xx,y,z=slot_of(idx,k,t)
+                def go(dst):
+                    pltpu.make_async_copy(st.at[k,pl.ds(240*t,CUT)],dst.at[xx,y,z,pl.ds(0,CUT)],sem).start()
+                    pltpu.make_async_copy(st.at[k,pl.ds(240*t+CUT,240-CUT)],dst.at[y,xx,z,pl.ds(CUT,240-CUT)],sem).start()
+                    pltpu.make_async_copy(sg.at[k,t],dst.at[y,xx,z,pl.ds(240,16)],sem).start()
+                @pl.when(c==0)
+                def _(): go(wk)
+                @pl.when(c==1)
+                def _(): go(ws)
+        pltpu.make_async_copy(st.at[:,pl.ds(0,960)],st.at[:,pl.ds(0,960)],sem).wait()
+        pltpu.make_async_copy(sg,sg,sem).wait()
+
+def qkv_bwd(idx,g1,g2,x,gains,n1,dmid,w,dg2):
+    return pl.pallas_call(qkv_bwd_kernel,grid_spec=prefetch((4,),[head_spec(a.shape[0]) for a in (*g1,*g2)]+[row_spec(DP),cst((2,DP)),cst((T,DP)),row_spec(DP),cst((DP,WN)),cst((1,DP))],
+        [tok_spec(),ANY,ANY],[pltpu.VMEM((T,WN),BF),pltpu.VMEM((8,DP,256),BF),pltpu.VMEM((8,4,16,256),BF),pltpu.VMEM((1,D),F32),pltpu.SemaphoreType.DMA]),
+        out_shape=[sds((2,2,D,256),BF)]+[sds((2,2,4,256,256),BF)]*2,
+        compiler_params=params(),cost_estimate=cost(18), name="qkv_bwd")(idx,*g1,*g2,x,gains,n1,dmid,w,dg2)
+
+def tok_out_kernel(idx,a,r,b,o):
+    y=idx[2]; c=idx[3]
+    o[2*y+c]=a[0,0]; o[2*y+1-c]=r[0]
+    o[2*(1-y)+c]=b[0]; o[2*(1-y)+1-c]=b[1]
+def tok_out(idx,a,r,b):
+    v=pl.BlockSpec(memory_space=pltpu.VMEM)
+    return pl.pallas_call(tok_out_kernel,grid=(1,),in_specs=[SMEM,pl.BlockSpec((1,1,D,256),lambda i:(0,0,0,0)),pl.BlockSpec((1,D,256),lambda i:(0,0,0)),v],out_specs=v,out_shape=sds((4,D,256),BF),compiler_params=params(),cost_estimate=cost(4),name="tok_out")(idx,a,r,b)
+
+
+def swap(a, axis, bit):
+    n = lax.axis_size(axis)
+    return lax.ppermute(a, axis, [(i, i ^ bit) for i in range(n)])
+
+def move(a, name):
+    if name == "x": return swap(a, "dp", 1)
+    if name == "y": return swap(a, "ctx", 2)
+    return swap(a, "ctx", 1)
+
+def from_z(a, k):
+    return lax.ppermute(a, "dp", [(((z + k) % 4) * 2 + x, z * 2 + x) for z in range(4) for x in range(2)])
+
+def after(a, *others):
+    return lax.optimization_barrier((a,) + others)[0]
+
+def gather_z(shard, cut):
+    ps = [shard] + [from_z(shard, k) for k in (1, 2, 3)]
+    return jnp.stack([p[:cut] for p in ps]), jnp.stack([p[cut:] for p in ps])
+
+def gather_first(g):
+    a, b = g
+    return jnp.stack([a, move(a, "y")]), jnp.stack([b, move(b, "x")])
+
+def gather_second(g):
+    a, b = g
+    return (a, move(a, "x")), (b, move(b, "y"))
+
+def gather_core(g):
+    return [list(h) + [move(p, "c") for p in h] for h in g]
+
+def add(*terms):
+    total = terms[0].astype(F32)
+    for t in terms[1:]: total = total + t.astype(F32)
+    return total
+
+def reduce_core(send):
+    return move(send, "c")
+
+def reduce_first(keep, rc, cut):
+    low = add(keep[1], rc[1]).astype(BF)
+    return move(low[:, :, :cut], "x"), move(low[:, :, cut:], "y")
+
+def reduce_second(keep, rc, r1, cut):
+    a, b = r1
+    low = add(keep[0, 1], rc[0, 1])
+    return (move((low[:, :cut] + a[1].astype(F32)).astype(BF), "y"),
+            move((low[:, cut:] + b[1].astype(F32)).astype(BF), "x"))
+
+def reduce_z(keep, rc, r1, r2):
+    own = add(keep[0, 0], rc[0, 0], jnp.concatenate([r1[0][0], r1[1][0]], axis=1), jnp.concatenate(r2, axis=1))
+    low = own.astype(BF)
+    return own[0], [from_z(low[k], 4 - k) for k in (1, 2, 3)]
+
+def exchange_in_y(idx, a):
+    return move(lax.dynamic_slice_in_dim(a, 2 * (1 - idx[2]), 2, 0), "y")
+
+def exchange_in_c(idx, a, r):
+    y, c = idx[2], idx[3]
+    give = jnp.concatenate([lax.dynamic_slice_in_dim(a, 2 * y + 1 - c, 1, 0), lax.dynamic_slice_in_dim(r, 1 - c, 1, 0)])
+    return move(give, "c")
+
+SPLIT = ((0, 192), (192, 320))
+
+def fast(hidden_in, norm_gains, w_query, w_key, w_value, w_out, w_gate, w_up, w_down, cotangent):
+    di, ci = lax.axis_index("dp"), lax.axis_index("ctx")
+    idx = jnp.stack([di // 2, di % 2, ci // 2, ci % 2]).astype(jnp.int32)
+    pz = lambda r, n: jnp.zeros((r, n), BF)
+    c1 = jnp.concatenate([w_query, pz(240, 8), w_key, w_value, pz(240, 48), w_out, pz(240, 8)], axis=1)
+    gain_row = jnp.pad(norm_gains.reshape(1, 60), ((0, 15), (0, 324)))
+    c1 = jnp.concatenate([c1, gain_row], axis=0)
+    def pack(lo, hi):
+        s = hi - lo
+        gu = jnp.concatenate([w_gate[:, lo:hi], w_up[:, lo:hi]], axis=1)
+        d = jnp.concatenate([w_down[lo:hi], w_down[320 + lo:320 + hi]], axis=0)
+        d = jnp.pad(d, ((0, 0), (0, 8)))
+        d = jnp.concatenate([d[128 * t:128 * t + 128] for t in range(2 * s // 128)], axis=1)
+        return jnp.concatenate([gu, d], axis=0)
+    ht, ct = jnp.swapaxes(hidden_in, 1, 2), jnp.swapaxes(cotangent, 1, 2)
+    xr = exchange_in_y(idx, ht)
+    g1 = gather_z(c1, CUT)
+    ga = gather_z(after(pack(*SPLIT[0]), g1[0]), 240)
+    gb = gather_z(after(pack(*SPLIT[1]), ga[0]), 240)
+    xg = exchange_in_c(idx, ht, xr)
+    x = tok_in(idx, ht, xr, xg)
+    p1 = gather_core(gather_second(gather_first(g1)))
+    pa = gather_core(gather_second(gather_first(ga)))
+    pb = gather_core(gather_second(gather_first(gb)))
+    cr = exchange_in_y(idx, ct)
+    cg = exchange_in_c(idx, ct, cr)
+    cos, sin = rope_tables(jnp.arange(T).astype(F32), HD)
+    cos, sin = jnp.tile(cos, (1, 2)), jnp.tile(sin, (1, 2))
+    n1, q, k, v, w, wo, gains = qkv_fwd(idx, x, cos, sin, *p1)
+    o1, lse1 = attn_fwd(q, k, v, 0, 3)
+    o2, lse2 = attn_fwd(q, k, v, 3, 2)
+    att, mid, n2 = out_fwd(idx, o1, o2, x, gains, wo)
+    acc, ha, wda = ffn_fwd(idx, n2, mid, *pa, False)
+    out, hb, wdb = ffn_fwd(idx, n2, acc, *pb, True)
+    cb = tok_in(idx, ct, cr, cg)
+    hr = move(out[1], "c")
+    hb_ = move(jnp.stack([out[0, 1], hr[1]]), "y")
+    hidden_out = tok_out(idx, out, hr, hb_)
+    dn2, ka, sa = ffn_bwd(idx, cb, n2, ha, wda, jnp.zeros((T, DP), F32), pa[0])
+    ra_c = reduce_core(sa)
+    dn2, kb, sb = ffn_bwd(idx, cb, n2, hb, wdb, dn2, pb[0])
+    rb_c = reduce_core(sb)
+    dmid, do, dg2, ko, so = out_bwd(idx, dn2, cb, mid, gains, wo, att)
+    ro_c = reduce_core(so)
+    b1 = attn_bwd(q, k, v, do, lse1, cos, sin, 0, 3)
+    b2 = attn_bwd(q, k, v, do, lse2, cos, sin, 3, 2)
+    hg, kq, sq = qkv_bwd(idx, b1, b2, x, gains, n1, dmid, w, dg2)
+    rq_c = reduce_core(sq)
+    gr = move(hg[1], "c")
+    gb_ = move(jnp.stack([hg[0, 1], gr[1]]), "y")
+    hidden_grad = tok_out(idx, hg, gr, gb_)
+    factor = 1.0 / math.sqrt(lax.axis_size("dp") * hidden_in.shape[0] * T)
+    def finish(keep, rc, cut):
+        r1 = reduce_first(keep, rc, cut)
+        r2 = reduce_second(keep, rc, r1, cut)
+        own, others = reduce_z(keep, rc, r1, r2)
+        return add(own, *others) * factor
+    ra = finish(ka, ra_c, 240)
+    rb = finish(kb, rb_c, 240)
+    ro = finish(ko, ro_c, CUT)
+    rq = finish(kq, rq_c, CUT)
+    gate, up, down = [], [], []
+    for (lo, hi), r in zip(SPLIT, (ra, rb)):
+        s = hi - lo
+        gate.append(r[:240, :s]); up.append(r[:240, s:])
+        d = jnp.concatenate([r[240:, 128 * t:128 * t + 128] for t in range(2 * s // 128)], axis=0)[:, :120]
+        down.append((d[:s], d[s:]))
+    return (jnp.swapaxes(hidden_out, 1, 2), jnp.swapaxes(hidden_grad, 1, 2), rq[240, :60], rq[:240, :120], rq[:240, 128:168],
+            rq[:240, 168:208], ro[:, :120], jnp.concatenate(gate, axis=1), jnp.concatenate(up, axis=1),
+            jnp.concatenate([down[0][0], down[1][0], down[0][1], down[1][1]], axis=0))
+
+
+def body(hidden_in, *rest):
+    seqs_here, seg_len, _ = hidden_in.shape
+    if (lax.axis_size("dp"), lax.axis_size("ctx"), seqs_here, seg_len) == (8, 4, 4, 256):
+        return fast(hidden_in, *rest)
+    return local(hidden_in, *rest)
+
+
 def solution(mesh):
     in_specs = (
         P("dp", "ctx", None),
@@ -359,4 +889,4 @@
         P("ctx", "dp"),
         P("ctx", "dp"),
     )
-    return jax.shard_map(local, mesh=mesh, in_specs=in_specs, out_specs=out_specs, check_vma=False)
+    return jax.shard_map(body, mesh=mesh, in_specs=in_specs, out_specs=out_specs, check_vma=False)

time: 2140 us -> 598 us (0.28)
  waiting for transfers between devices: 1040 us -> 184 us
  matrix products: 447 us -> 0 us
  local copies, waits for them, and re-layouts: 415 us -> 37 us
  Pallas kernels: 0 us -> 259 us
  blocking collectives: 151 us -> 0 us
  starting transfers between devices: 2.1 us -> 74.1 us
    reduce_scatter x9 -> x0, waiting for transfers between devices: 708 us -> none  [the longest x1 179 us: local(): lax.psum_scatter(up_part, 'dp', scatter_dimension=1, tiled=True)]
    dot_general x159 -> x0, matrix products: 436 us -> none  [the longest x40 88.5 us: block_scores(): lax.dot_general(query_block, key_block, contract_last, preferred_element_...]
    unnamed x127 -> x57, local copies, waits for them, and re-layouts: 346 us -> 9.41 us
    pallas_call x0 -> x16, Pallas kernels: none -> 259 us  [the longest x2 67.9 us: ffn_bwd(): pl.pallas_call(functools.partial(ffn_bwd_kernel, S), grid=(2,), in_specs=...]
    unnamed x32 -> x0, waiting for transfers between devices: 231 us -> none
    ppermute x0 -> x73, waiting for transfers between devices: none -> 184 us  [the longest x52 124 us: swap(): return lax.ppermute(a, axis, [(i, i ^ bit) for i in range(n)])]
    all_gather x9 -> x0, blocking collectives: 116 us -> none  [the longest x1 32.5 us: local(): lax.all_gather(row_parts[1], 'dp', axis=1, tiled=True)]
    all_gather x7 -> x0, waiting for transfers between devices: 102 us -> none  [the longest x1 71.2 us: local(): lax.all_gather(row_parts[6], 'dp', axis=1, tiled=True)]
  transfers between devices with their start and end apart: 24 -> 73, of which waited for: 17 -> 33; matrix products, arithmetic and copies ran while one was open for 29% -> 10% of each run, Pallas kernels for 0% -> 33%
where the time goes in v1:
time: 598 us; the launch traced here: 591 us
  Pallas kernels  259 us (43%)
  waiting for transfers between devices  184 us (31%)
  starting transfers between devices  74.1 us (12%)
  local copies, waits for them, and re-layouts  37 us (6%)
  other arithmetic  34.4 us (6%)
    ppermute x52, waiting for transfers between devices, swap(): return lax.ppermute(a, axis, [(i, i ^ bit) for i in range(n)])  124 us
    pallas_call x2, Pallas kernels, ffn_bwd(): pl.pallas_call(functools.partial(ffn_bwd_kernel, S), grid=(2,), in_specs=...  67.9 us
    ppermute x21, waiting for transfers between devices, from_z(): lax.ppermute(a, 'dp', [((z + k) % 4 * 2 + x, z * 2 + x) for z in range(4)...  59.9 us
    pallas_call x2, Pallas kernels, attn_bwd(): pl.pallas_call(attn_bwd_kernel, grid=(ng, 3), in_specs=[qs, ks, ks, qs, p...  46.1 us
    pallas_call x2, Pallas kernels, ffn_fwd(): pl.pallas_call(functools.partial(ffn_fwd_kernel, S, last), grid_spec=pltp...  39.7 us
    ppermute x21, starting transfers between devices, from_z(): lax.ppermute(a, 'dp', [((z + k) % 4 * 2 + x, z * 2 + x) for z in range(4)...  37.9 us
    ppermute x52, starting transfers between devices, swap(): return lax.ppermute(a, axis, [(i, i ^ bit) for i in range(n)])  36.2 us
    pallas_call x2, Pallas kernels, attn_fwd(): pl.pallas_call(attn_fwd_kernel, grid=(ng, 3), in_specs=[qs, ks, ks], out_...  31.4 us
  transfers between devices with their start and end apart: 73, of which 33 were waited for; matrix products, arithmetic and copies ran while one was open for 10% of the time, Pallas kernels for 33%

profile of v1, /device:TPU:0, one launch (start us, length us, event | category | flops | bytes accessed | tf_op | source)
XLA Modules:
  0.0 590.7 jit_solution(14317348803335778947)
XLA Ops:
  41.1 9.8 %collective-permute-done.14 = bf16[368,384]{1,0:T(8,128)(2,1)S(1)} collective-permute-done((bf16[368,384]{1,0:T(8,128)(2,1)S(1)}, bf16[368,384]{1,0:T(8,128)(2,1)S(1)}, u32[]{:S(2)}, u32[]{:S(2)}) %collective-permute-start.14) | collective-permute-done | bytes 282656 | tf_op jit(solution)/shard_map/ppermute | solution.py:735
  58.6 5.9 %collective-permute-done.26 = bf16[368,256]{1,0:T(8,128)(2,1)S(1)} collective-permute-done((bf16[368,256]{1,0:T(8,128)(2,1)S(1)}, bf16[368,256]{1,0:T(8,128)(2,1)S(1)}, u32[]{:S(2)}, u32[]{:S(2)}) %collective-permute-start.26) | collective-permute-done | bytes 188448 | tf_op jit(solution)/shard_map/ppermute | solution.py:735
  64.9 9.7 %collective-permute-done.25 = bf16[368,256]{1,0:T(8,128)(2,1)S(1)} collective-permute-done((bf16[368,256]{1,0:T(8,128)(2,1)S(1)}, bf16[368,256]{1,0:T(8,128)(2,1)S(1)}, u32[]{:S(2)}, u32[]{:S(2)}) %collective-permute-start.25) | collective-permute-done | bytes 188448 | tf_op jit(solution)/shard_map/ppermute | solution.py:735
  95.7 19.8 %collective-permute-done.31 = bf16[4,128,256]{2,1,0:T(8,128)(2,1)S(1)} collective-permute-done((bf16[4,128,256]{2,1,0:T(8,128)(2,1)S(1)}, bf16[4,128,256]{2,1,0:T(8,128)(2,1)S(1)}, u32[]{:S(2)}, u32[]{:S(2)}) %collective-permute-start.31) | collective-permute-done | bytes 262176 | tf_op jit(solution)/shard_map/ppermute | solution.py:727
  141.0 16.2 %qkv_fwd.1 = (bf16[1024,1024]{1,0:T(8,128)(2,1)}, bf16[15,1024,128]{2,1,0:T(8,128)(2,1)}, bf16[5,1024,128]{2,1,0:T(8,128)(2,1)}, bf16[5,1024,128]{2,1,0:T(8,128)...) custom-call(s32[4]{0:T(128)} %pad_add_fusion.idx, bf16[1024,1024]{1,0:T(8,128)(2,1)} %tok_in.2.x, ...), custom_call_target="tpu_custom_call" | custom-call | flops 14400000000 | bytes 32000000 | tf_op jit(solution)/shard_map/qkv_fwd/pallas_call | solution.py:618
  157.1 18.5 %attn_fwd.2 = (bf16[9,1024,128]{2,1,0:T(8,128)(2,1)}, f32[9,1,1024]{2,1,0:T(1,128)}) custom-call(bf16[15,1024,128]{2,1,0:T(8,128)(2,1)} %get-tuple-element.52.q, bf16[5,1024,128]{2,1,0:T(8,128)(2,1)} %get-tuple-element.53.k, bf16[5,1024,128]{2,1,0:T(8,128)(2,1)} %get-tuple-element.54.v), custom_call_target="tpu_custom_call" | custom-call | flops 16199999488 | bytes 36000000 | tf_op jit(solution)/shard_map/attn_fwd/pallas_call | solution.py:521
  176.2 18.3 %collective-permute-done.17.refs_1_ = bf16[2,4,240,384]{3,2,1,0:T(8,128)(2,1)} collective-permute-done((bf16[2,4,240,384]{3,2,1,0:T(8,128)(2,1)S(1)}, bf16[2,4,240,384]{3,2,1,0:T(8,128)(2,1)}, u32[]{:S(2)}, u32[]{:S(2)}) %collective-permute-start.17) | collective-permute-done | bytes 1474592 | tf_op jit(solution)/shard_map/ppermute | solution.py:727
  194.5 12.9 %attn_fwd.3 = (bf16[6,1024,128]{2,1,0:T(8,128)(2,1)}, f32[6,1,1024]{2,1,0:T(1,128)}) custom-call(bf16[15,1024,128]{2,1,0:T(8,128)(2,1)} %get-tuple-element.52.q, bf16[5,1024,128]{2,1,0:T(8,128)(2,1)} %get-tuple-element.53.k, bf16[5,1024,128]{2,1,0:T(8,128)(2,1)} %get-tuple-element.54.v), custom_call_target="tpu_custom_call" | custom-call | flops 10800000000 | bytes 24000000 | tf_op jit(solution)/shard_map/attn_fwd/pallas_call | solution.py:521
  207.4 9.2 %out_fwd.1 = (bf16[1024,1024]{1,0:T(8,128)(2,1)}, f32[1024,1024]{1,0:T(8,128)}, bf16[1024,1024]{1,0:T(8,128)(2,1)}) custom-call(s32[4]{0:T(128)} %pad_add_fusion.idx, bf16[9,1024,128]{2,1,0:T(8,128)(2,1)} %get-tuple-element.55.o1, bf16[6,1024,128]{2,1,0:T(8,128)(2,1)} %get-tuple-element.56.o2, bf16[1024,1024]{1,0:T(8,128)(2,1)} %tok_in.2.x, ...), custom_call_target="tpu_custom_call" | custom-call | flops 8099999744 | bytes 18000000 | tf_op jit(solution)/shard_map/out_fwd/pallas_call | solution.py:633
  217.7 22.4 %ffn_fwd.2 = (f32[1024,1024]{1,0:T(8,128)}, bf16[2,1024,1536]{2,1,0:T(8,128)(2,1)}, bf16[2,768,1024]{2,1,0:T(8,128)(2,1)}) custom-call(s32[4]{0:T(128)} %pad_add_fusion.idx, bf16[1024,1024]{1,0:T(8,128)(2,1)} %get-tuple-element.59.n2, f32[1024,1024]{1,0:T(8,128)} %get-tuple-element.60.mid, bf16[2,4,240,384]{3,2,1,0:T(8,128)(2,1)} %copy-done.2, ...), custom_call_target="tpu_custom_call" | custom-call | flops 17999998976 | bytes 40000000 | tf_op jit(solution)/shard_map/ffn_fwd/pallas_call | solution.py:420
  242.6 38.4 %ffn_bwd.2 = (f32[1024,1024]{1,0:T(8,128)}, bf16[2,2,4,368,384]{4,3,2,1,0:T(8,128)(2,1)}, bf16[2,2,4,368,384]{4,3,2,1,0:T(8,128)(2,1)}) custom-call(s32[4]{0:T(128)} %pad_add_fusion.idx, bf16[1024,1024]{1,0:T(8,128)(2,1)} %tok_in.3.cb, bf16[1024,1024]{1,0:T(8,128)(2,1)} %get-tuple-element.59.n2, bf16[2,1024,1536]{2,1,0:T(8,128)(2,1)} %get-tuple-element.67.h, ...), custom_call_target="tpu_custom_call" | custom-call | flops 29699999744 | bytes 66000000 | tf_op jit(solution)/shard_map/ffn_bwd/pallas_call | solution.py:494
  282.2 17.3 %ffn_fwd.3 = (bf16[2,2,960,256]{3,2,1,0:T(8,128)(2,1)}, bf16[2,1024,1024]{2,1,0:T(8,128)(2,1)}, bf16[2,512,1024]{2,1,0:T(8,128)(2,1)}) custom-call(s32[4]{0:T(128)} %pad_add_fusion.idx, bf16[1024,1024]{1,0:T(8,128)(2,1)} %get-tuple-element.59.n2, f32[1024,1024]{1,0:T(8,128)} %get-tuple-element.62.mid, bf16[2,4,240,256]{3,2,1,0:T(8,128)(2,1)} %pad_maximum_fusion.3.refs_0_, ...), custom_call_target="tpu_custom_call" | custom-call | flops 17999998976 | bytes 40000000 | tf_op jit(solution)/shard_map/ffn_fwd/pallas_call | solution.py:420
  299.5 29.4 %ffn_bwd.3 = (f32[1024,1024]{1,0:T(8,128)}, bf16[2,2,4,368,256]{4,3,2,1,0:T(8,128)(2,1)}, bf16[2,2,4,368,256]{4,3,2,1,0:T(8,128)(2,1)}) custom-call(s32[4]{0:T(128)} %pad_add_fusion.idx, bf16[1024,1024]{1,0:T(8,128)(2,1)} %tok_in.3.cb, bf16[1024,1024]{1,0:T(8,128)(2,1)} %get-tuple-element.59.n2, bf16[2,1024,1024]{2,1,0:T(8,128)(2,1)} %get-tuple-element.65.h, ...), custom_call_target="tpu_custom_call" | custom-call | flops 29699999744 | bytes 66000000 | tf_op jit(solution)/shard_map/ffn_bwd/pallas_call | solution.py:494
  329.0 16.2 %out_bwd.1 = (f32[1024,1024]{1,0:T(8,128)}, bf16[15,1024,128]{2,1,0:T(8,128)(2,1)}, f32[1,1024]{1,0:T(1,128)}, bf16[2,2,4,240,128]{4,3,2,1,0:T(8,128)(2,1)}, bf16[2,2,4,240,128]{4,3,2,1,0:T(8,128)(2,1)}) custom-call(s32[4]{0:T(128)} %pad_add_fusion.idx, f32[1024,1024]{1,0:T(8,128)} %get-tuple-element.70.dn2, bf16[1024,1024]{1,0:T(8,128)(2,1)} %tok_in.3.cb, ...), custom_call_target="tpu_custom_call" | custom-call | flops 14400000000 | bytes 32000000 | tf_op jit(solution)/shard_map/out_bwd/pallas_call | solution.py:669
  345.7 18.9 %attn_bwd.3 = (bf16[6,1024,128]{2,1,0:T(8,128)(2,1)}, bf16[2,1024,128]{2,1,0:T(8,128)(2,1)}, bf16[2,1024,128]{2,1,0:T(8,128)(2,1)}) custom-call(bf16[15,1024,128]{2,1,0:T(8,128)(2,1)} %get-tuple-element.52.q, bf16[5,1024,128]{2,1,0:T(8,128)(2,1)} %get-tuple-element.53.k, bf16[5,1024,128]{2,1,0:T(8,128)(2,1)} %get-tuple-element.54.v, ...), custom_call_target="tpu_custom_call" | custom-call | flops 16199999488 | bytes 36000000 | tf_op jit(solution)/shard_map/attn_bwd/pallas_call | solution.py:561
  364.6 27.2 %attn_bwd.2 = (bf16[9,1024,128]{2,1,0:T(8,128)(2,1)}, bf16[3,1024,128]{2,1,0:T(8,128)(2,1)}, bf16[3,1024,128]{2,1,0:T(8,128)(2,1)}) custom-call(bf16[15,1024,128]{2,1,0:T(8,128)(2,1)} %get-tuple-element.52.q, bf16[5,1024,128]{2,1,0:T(8,128)(2,1)} %get-tuple-element.53.k, bf16[5,1024,128]{2,1,0:T(8,128)(2,1)} %get-tuple-element.54.v, ...), custom_call_target="tpu_custom_call" | custom-call | flops 24299999232 | bytes 54000000 | tf_op jit(solution)/shard_map/attn_bwd/pallas_call | solution.py:561
  391.8 18.4 %qkv_bwd.1 = (bf16[2,2,960,256]{3,2,1,0:T(8,128)(2,1)}, bf16[2,2,4,256,256]{4,3,2,1,0:T(8,128)(2,1)}, bf16[2,2,4,256,256]{4,3,2,1,0:T(8,128)(2,1)}) custom-call(s32[4]{0:T(128)} %pad_add_fusion.idx, bf16[9,1024,128]{2,1,0:T(8,128)(2,1)} %get-tuple-element.74.dq1, bf16[3,1024,128]{2,1,0:T(8,128)(2,1)} %get-tuple-element.75.dk1, ...), custom_call_target="tpu_custom_call" | custom-call | flops 16199999488 | bytes 36000000 | tf_op jit(solution)/shard_map/qkv_bwd/pallas_call | solution.py:711
  426.4 19.1 %collective-permute-done.52 = bf16[4,160,128]{2,1,0:T(8,128)(2,1)S(1)} collective-permute-done((bf16[4,160,128]{2,1,0:T(8,128)(2,1)S(1)}, bf16[4,160,128]{2,1,0:T(8,128)(2,1)S(1)}, u32[]{:S(2)}, u32[]{:S(2)}) %collective-permute-start.52) | collective-permute-done | bytes 163872 | tf_op jit(solution)/shard_map/ppermute | solution.py:727
  465.2 11.7 %collective-permute-done.36.b = bf16[2,960,256]{2,1,0:T(8,128)(2,1)} collective-permute-done((bf16[2,960,256]{2,1,0:T(8,128)(2,1)}, bf16[2,960,256]{2,1,0:T(8,128)(2,1)}, u32[]{:S(2)}, u32[]{:S(2)}) %collective-permute-start.36) | collective-permute-done | bytes 983072 | tf_op jit(solution)/shard_map/ppermute | solution.py:727
  486.4 10.1 %collective-permute-done.42 = bf16[2,4,160,256]{3,2,1,0:T(8,128)(2,1)S(1)} collective-permute-done((bf16[2,4,160,256]{3,2,1,0:T(8,128)(2,1)S(1)}, bf16[2,4,160,256]{3,2,1,0:T(8,128)(2,1)S(1)}, u32[]{:S(2)}, u32[]{:S(2)}) %collective-permute-start.42) | collective-permute-done | bytes 655392 | tf_op jit(solution)/shard_map/ppermute | solution.py:727
  519.6 7.2 %collective-permute-done.67 = bf16[2,4,128,256]{3,2,1,0:T(8,128)(2,1)} collective-permute-done((bf16[2,4,128,256]{3,2,1,0:T(8,128)(2,1)S(1)}, bf16[2,4,128,256]{3,2,1,0:T(8,128)(2,1)}, u32[]{:S(2)}, u32[]{:S(2)}) %collective-permute-start.67) | collective-permute-done | bytes 524320 | tf_op jit(solution)/shard_map/ppermute | solution.py:727
  537.2 6.4 %collective-permute-done.68 = bf16[4,240,256]{2,1,0:T(8,128)(2,1)S(1)} collective-permute-done((bf16[4,240,256]{2,1,0:T(8,128)(2,1)S(1)}, bf16[4,240,256]{2,1,0:T(8,128)(2,1)S(1)}, u32[]{:S(2)}, u32[]{:S(2)}) %collective-permute-start.68) | collective-permute-done | bytes 491552 | tf_op jit(solution)/shard_map/ppermute | solution.py:727
  563.3 7.5 %collective-permute-done.61 = bf16[4,128,384]{2,1,0:T(8,128)(2,1)S(1)} collective-permute-done((bf16[4,128,384]{2,1,0:T(8,128)(2,1)S(1)}, bf16[4,128,384]{2,1,0:T(8,128)(2,1)S(1)}, u32[]{:S(2)}, u32[]{:S(2)}) %collective-permute-start.61) | collective-permute-done | bytes 393248 | tf_op jit(solution)/shard_map/ppermute | solution.py:727
  581.4 5.9 collective-permute-done.63
  (332 shorter events, 212.2 us)
Async XLA Ops:
  14.1 69.4 %collective-permute-start = (bf16[2,960,256]{2,1,0:T(8,128)(2,1)}, bf16[2,960,256]{2,1,0:T(8,128)(2,1)}, u32[]{:S(2)}, u32[]{:S(2)}) collective-permute-start(bf16[2,960,256]{2,1,0:T(8,128)(2,1)} %dynamic-slice_bitcast_fusion.1), channel_id=1, source_target_pairs={{0,2},{1,3},{2,0},{3,1},{4,6},{5,7},{6,4},{7,5},{8,10},{9,11},{10,... | collective-permute-start | bytes 2949128 | tf_op jit(solution)/shard_map/ppermute | solution.py:727
  16.6 76.1 %collective-permute-start.37 = (bf16[2,960,256]{2,1,0:T(8,128)(2,1)}, bf16[2,960,256]{2,1,0:T(8,128)(2,1)}, u32[]{:S(2)}, u32[]{:S(2)}) collective-permute-start(bf16[2,960,256]{2,1,0:T(8,128)(2,1)} %dynamic-slice_bitcast_fusion), channel_id=1, source_target_pairs={{0,2},{1,3},{2,0},{3,1},{4,6},{5,7},{6,4},{7,5},{8,10},{9,11},{10,... | collective-permute-start | bytes 2949128 | tf_op jit(solution)/shard_map/ppermute | solution.py:727
  25.7 55.2 %collective-permute-start.5 = (bf16[4,160,384]{2,1,0:T(8,128)(2,1)S(1)}, bf16[4,160,384]{2,1,0:T(8,128)(2,1)S(1)}, u32[]{:S(2)}, u32[]{:S(2)}) collective-permute-start(bf16[4,160,384]{2,1,0:T(8,128)(2,1)S(1)} %get-tuple-element.141), channel_id=1, source_target_pairs={{0,2},{1,3},{2,0},{3,1},{4,6},{5,7},{6,4},{7,5},{8,10},{9,11},{10,... | collective-permute-start | bytes 1474568 | tf_op jit(solution)/shard_map/ppermute | solution.py:727
  50.9 34.3 %collective-permute-start.9 = (bf16[4,96,384]{2,1,0:T(8,128)(2,1)S(1)}, bf16[4,96,384]{2,1,0:T(8,128)(2,1)S(1)}, u32[]{:S(2)}, u32[]{:S(2)}) collective-permute-start(bf16[4,96,384]{2,1,0:T(8,128)(2,1)S(1)} %get-tuple-element.149), channel_id=1, source_target_pairs={{0,4},{4,0},{8,12},{12,8},{16,20},{20,16},{24,28},{28,24},{1,5},{5... | collective-permute-start | bytes 884744 | tf_op jit(solution)/shard_map/ppermute | solution.py:727
  82.0 38.3 %collective-permute-start.6 = (bf16[2,4,160,384]{3,2,1,0:T(8,128)(2,1)}, bf16[2,4,160,384]{3,2,1,0:T(8,128)(2,1)}, u32[]{:S(2)}, u32[]{:S(2)}) collective-permute-start(bf16[2,4,160,384]{3,2,1,0:T(8,128)(2,1)} %pad_maximum_fusion.2.refs_0_), channel_id=1, source_target_pairs={{0,4},{4,0},{8,12},{12,8},{16,20},{20,16},{24,28},{28,24},{1,5},{5... | collective-permute-start | bytes 2949128 | tf_op jit(solution)/shard_map/ppermute | solution.py:727
  83.5 36.3 %collective-permute-start.16 = (bf16[4,240,384]{2,1,0:T(8,128)(2,1)}, bf16[4,240,384]{2,1,0:T(8,128)(2,1)}, u32[]{:S(2)}, u32[]{:S(2)}) collective-permute-start(bf16[4,240,384]{2,1,0:T(8,128)(2,1)} %get-tuple-element.129), channel_id=1, source_target_pairs={{0,2},{1,3},{2,0},{3,1},{4,6},{5,7},{6,4},{7,5},{8,10},{9,11},{10,... | collective-permute-start | bytes 2211848 | tf_op jit(solution)/shard_map/ppermute | solution.py:727
  85.2 30.8 %collective-permute-start.27 = (bf16[4,240,256]{2,1,0:T(8,128)(2,1)S(1)}, bf16[4,240,256]{2,1,0:T(8,128)(2,1)S(1)}, u32[]{:S(2)}, u32[]{:S(2)}) collective-permute-start(bf16[4,240,256]{2,1,0:T(8,128)(2,1)S(1)} %get-tuple-element.139), channel_id=1, source_target_pairs={{0,2},{1,3},{2,0},{3,1},{4,6},{5,7},{6,4},{7,5},{8,10},{9,11},{10,... | collective-permute-start | bytes 1474568 | tf_op jit(solution)/shard_map/ppermute | solution.py:727
  92.7 35.2 %collective-permute-start.1 = (bf16[2,960,256]{2,1,0:T(8,128)(2,1)}, bf16[2,960,256]{2,1,0:T(8,128)(2,1)}, u32[]{:S(2)}, u32[]{:S(2)}) collective-permute-start(bf16[2,960,256]{2,1,0:T(8,128)(2,1)} %pad_maximum_fusion.1), channel_id=1, source_target_pairs={{0,1},{1,0},{2,3},{3,2},{4,5},{5,4},{6,7},{7,6},{8,9},{9,8},{10,11... | collective-permute-start | bytes 2949128 | tf_op jit(solution)/shard_map/ppermute | solution.py:727
  132.6 43.1 %collective-permute-start.21 = (bf16[2,4,128,384]{3,2,1,0:T(8,128)(2,1)S(1)}, bf16[2,4,128,384]{3,2,1,0:T(8,128)(2,1)}, u32[]{:S(2)}, u32[]{:S(2)}) collective-permute-start(bf16[2,4,128,384]{3,2,1,0:T(8,128)(2,1)S(1)} %copy-done.7), channel_id=1, source_target_pairs={{0,2},{1,3},{2,0},{3,1},{4,6},{5,7},{6,4},{7,5},{8,10},{9,11},{10,... | collective-permute-start | bytes 2359304 | tf_op jit(solution)/shard_map/ppermute | solution.py:727
  137.3 79.2 %collective-permute-start.22 = (bf16[2,4,128,384]{3,2,1,0:T(8,128)(2,1)S(1)}, bf16[2,4,128,384]{3,2,1,0:T(8,128)(2,1)}, u32[]{:S(2)}, u32[]{:S(2)}) collective-permute-start(bf16[2,4,128,384]{3,2,1,0:T(8,128)(2,1)S(1)} %copy-done.7), channel_id=1, source_target_pairs={{0,1},{1,0},{2,3},{3,2},{4,5},{5,4},{6,7},{7,6},{8,9},{9,8},{10,11... | collective-permute-start | bytes 2359304 | tf_op jit(solution)/shard_map/ppermute | solution.py:727
  137.3 38.2 %collective-permute-start.32 = (bf16[2,4,128,256]{3,2,1,0:T(8,128)(2,1)S(1)}, bf16[2,4,128,256]{3,2,1,0:T(8,128)(2,1)}, u32[]{:S(2)}, u32[]{:S(2)}) collective-permute-start(bf16[2,4,128,256]{3,2,1,0:T(8,128)(2,1)S(1)} %copy-done.8), channel_id=1, source_target_pairs={{0,2},{1,3},{2,0},{3,1},{4,6},{5,7},{6,4},{7,5},{8,10},{9,11},{10,... | collective-permute-start | bytes 1572872 | tf_op jit(solution)/shard_map/ppermute | solution.py:727
  138.9 78.1 %collective-permute-start.28 = (bf16[2,4,240,256]{3,2,1,0:T(8,128)(2,1)S(1)}, bf16[2,4,240,256]{3,2,1,0:T(8,128)(2,1)}, u32[]{:S(2)}, u32[]{:S(2)}) collective-permute-start(bf16[2,4,240,256]{3,2,1,0:T(8,128)(2,1)S(1)} %copy-done.5), channel_id=1, source_target_pairs={{0,4},{4,0},{8,12},{12,8},{16,20},{20,16},{24,28},{28,24},{1,5},{5... | collective-permute-start | bytes 2949128 | tf_op jit(solution)/shard_map/ppermute | solution.py:727
  139.5 55.0 %collective-permute-start.17 = (bf16[2,4,240,384]{3,2,1,0:T(8,128)(2,1)S(1)}, bf16[2,4,240,384]{3,2,1,0:T(8,128)(2,1)}, u32[]{:S(2)}, u32[]{:S(2)}) collective-permute-start(bf16[2,4,240,384]{3,2,1,0:T(8,128)(2,1)S(1)} %pad_maximum_fusion.refs_0_), channel_id=1, source_target_pairs={{0,4},{4,0},{8,12},{12,8},{16,20},{20,16},{24,28},{28,24},{1,5},{5... | collective-permute-start | bytes 4423688 | tf_op jit(solution)/shard_map/ppermute | solution.py:727
  175.6 42.0 %collective-permute-start.18 = (bf16[2,4,240,384]{3,2,1,0:T(8,128)(2,1)S(1)}, bf16[2,4,240,384]{3,2,1,0:T(8,128)(2,1)}, u32[]{:S(2)}, u32[]{:S(2)}) collective-permute-start(bf16[2,4,240,384]{3,2,1,0:T(8,128)(2,1)S(1)} %pad_maximum_fusion.refs_0_), channel_id=1, source_target_pairs={{0,1},{1,0},{2,3},{3,2},{4,5},{5,4},{6,7},{7,6},{8,9},{9,8},{10,11... | collective-permute-start | bytes 4423688 | tf_op jit(solution)/shard_map/ppermute | solution.py:727
  175.7 41.5 %collective-permute-start.23 = (bf16[2,4,128,384]{3,2,1,0:T(8,128)(2,1)}, bf16[2,4,128,384]{3,2,1,0:T(8,128)(2,1)}, u32[]{:S(2)}, u32[]{:S(2)}) collective-permute-start(bf16[2,4,128,384]{3,2,1,0:T(8,128)(2,1)} %collective-permute-done.21.refs_5_), channel_id=1, source_target_pairs={{0,1},{1,0},{2,3},{3,2},{4,5},{5,4},{6,7},{7,6},{8,9},{9,8},{10,11... | collective-permute-start | bytes 2359304 | tf_op jit(solution)/shard_map/ppermute | solution.py:727
  216.5 64.5 %collective-permute-start.33 = (bf16[2,4,128,256]{3,2,1,0:T(8,128)(2,1)S(1)}, bf16[2,4,128,256]{3,2,1,0:T(8,128)(2,1)S(1)}, u32[]{:S(2)}, u32[]{:S(2)}) collective-permute-start(bf16[2,4,128,256]{3,2,1,0:T(8,128)(2,1)S(1)} %copy-done.8), channel_id=1, source_target_pairs={{0,1},{1,0},{2,3},{3,2},{4,5},{5,4},{6,7},{7,6},{8,9},{9,8},{10,11... | collective-permute-start | bytes 1572872 | tf_op jit(solution)/shard_map/ppermute | solution.py:727
  217.1 64.0 %collective-permute-start.29 = (bf16[2,4,240,256]{3,2,1,0:T(8,128)(2,1)S(1)}, bf16[2,4,240,256]{3,2,1,0:T(8,128)(2,1)}, u32[]{:S(2)}, u32[]{:S(2)}) collective-permute-start(bf16[2,4,240,256]{3,2,1,0:T(8,128)(2,1)S(1)} %copy-done.5), channel_id=1, source_target_pairs={{0,1},{1,0},{2,3},{3,2},{4,5},{5,4},{6,7},{7,6},{8,9},{9,8},{10,11... | collective-permute-start | bytes 2949128 | tf_op jit(solution)/shard_map/ppermute | solution.py:727
  217.2 63.9 %collective-permute-start.34 = (bf16[2,4,128,256]{3,2,1,0:T(8,128)(2,1)}, bf16[2,4,128,256]{3,2,1,0:T(8,128)(2,1)}, u32[]{:S(2)}, u32[]{:S(2)}) collective-permute-start(bf16[2,4,128,256]{3,2,1,0:T(8,128)(2,1)} %collective-permute-done.32.refs_5_), channel_id=1, source_target_pairs={{0,1},{1,0},{2,3},{3,2},{4,5},{5,4},{6,7},{7,6},{8,9},{9,8},{10,11... | collective-permute-start | bytes 1572872 | tf_op jit(solution)/shard_map/ppermute | solution.py:727
  217.6 63.5 %collective-permute-start.30 = (bf16[2,4,240,256]{3,2,1,0:T(8,128)(2,1)}, bf16[2,4,240,256]{3,2,1,0:T(8,128)(2,1)S(1)}, u32[]{:S(2)}, u32[]{:S(2)}) collective-permute-start(bf16[2,4,240,256]{3,2,1,0:T(8,128)(2,1)} %collective-permute-done.28.refs_1_), channel_id=1, source_target_pairs={{0,1},{1,0},{2,3},{3,2},{4,5},{5,4},{6,7},{7,6},{8,9},{9,8},{10,11... | collective-permute-start | bytes 2949128 | tf_op jit(solution)/shard_map/ppermute | solution.py:727
  345.2 68.8 %collective-permute-start.49 = (bf16[2,2,4,240,128]{4,3,2,1,0:T(8,128)(2,1)}, bf16[2,2,4,240,128]{4,3,2,1,0:T(8,128)(2,1)S(1)}, u32[]{:S(2)}, u32[]{:S(2)}) collective-permute-start(bf16[2,2,4,240,128]{4,3,2,1,0:T(8,128)(2,1)} %get-tuple-element.89), channel_id=1, source_target_pairs={{0,1},{1,0},{2,3},{3,2},{4,5},{5,4},{6,7},{7,6},{8,9},{9,8},{10,11... | collective-permute-start | bytes 2949128 | tf_op jit(solution)/shard_map/ppermute | solution.py:727
  412.4 85.0 %collective-permute-start.65 = (bf16[2,2,4,368,256]{4,3,2,1,0:T(8,128)(2,1)}, bf16[2,2,4,368,256]{4,3,2,1,0:T(8,128)(2,1)S(1)}, u32[]{:S(2)}, u32[]{:S(2)}) collective-permute-start(bf16[2,2,4,368,256]{4,3,2,1,0:T(8,128)(2,1)} %get-tuple-element.93), channel_id=1, source_target_pairs={{0,1},{1,0},{2,3},{3,2},{4,5},{5,4},{6,7},{7,6},{8,9},{9,8},{10,11... | collective-permute-start | bytes 9043976 | tf_op jit(solution)/shard_map/ppermute | solution.py:727
  412.7 49.0 %collective-permute-start.41 = (bf16[2,2,4,256,256]{4,3,2,1,0:T(8,128)(2,1)}, bf16[2,2,4,256,256]{4,3,2,1,0:T(8,128)(2,1)}, u32[]{:S(2)}, u32[]{:S(2)}) collective-permute-start(bf16[2,2,4,256,256]{4,3,2,1,0:T(8,128)(2,1)} %get-tuple-element.87), channel_id=1, source_target_pairs={{0,1},{1,0},{2,3},{3,2},{4,5},{5,4},{6,7},{7,6},{8,9},{9,8},{10,11... | collective-permute-start | bytes 6291464 | tf_op jit(solution)/shard_map/ppermute | solution.py:727
  415.8 43.0 %collective-permute-start.40 = (bf16[2,960,256]{2,1,0:T(8,128)(2,1)S(1)}, bf16[2,960,256]{2,1,0:T(8,128)(2,1)}, u32[]{:S(2)}, u32[]{:S(2)}) collective-permute-start(bf16[2,960,256]{2,1,0:T(8,128)(2,1)S(1)} %pad_maximum_fusion.6), channel_id=1, source_target_pairs={{0,2},{1,3},{2,0},{3,1},{4,6},{5,7},{6,4},{7,5},{8,10},{9,11},{10,... | collective-permute-start | bytes 2949128 | tf_op jit(solution)/shard_map/ppermute | solution.py:727
  458.1 72.1 %collective-permute-start.57 = (bf16[2,2,4,368,384]{4,3,2,1,0:T(8,128)(2,1)}, bf16[2,2,4,368,384]{4,3,2,1,0:T(8,128)(2,1)}, u32[]{:S(2)}, u32[]{:S(2)}) collective-permute-start(bf16[2,2,4,368,384]{4,3,2,1,0:T(8,128)(2,1)} %get-tuple-element.91), channel_id=1, source_target_pairs={{0,1},{1,0},{2,3},{3,2},{4,5},{5,4},{6,7},{7,6},{8,9},{9,8},{10,11... | collective-permute-start | bytes 13565960 | tf_op jit(solution)/shard_map/ppermute | solution.py:727
  (74 other events, 834.3 us)

commit v2 on v1

--- a/solution.py
+++ b/solution.py
@@ -350,42 +350,40 @@
 def cost(us): return pl.CostEstimate(flops=int(us*9e8),bytes_accessed=int(us*2e6),transcendentals=0)
 def sds(shape,dt): return jax.ShapeDtypeStruct(shape,dt)
 
-def pieces_of(idx, order):
-    for p in range(4):
-        for f in range(2):
-            dx,dy=(p%2,f) if order=="yx" else (f,p%2)
-            x=flip(idx[1],dx); ctx=flip(idx[2],dy)*2+flip(idx[3],p//2)
-            yield p,f,x,ctx,flip(idx[2],dy)
-
-def load_rows(idx, pieces, dst, sem, groups):
-    for z in groups:
-        dz=lax.rem(z-idx[0]+4,4)
-        for p,f,x,ctx,_ in pieces_of(idx,"yx"):
-            pltpu.make_async_copy(pieces[p].at[f,dz], dst.at[2*z+x,pl.ds(pl.multiple_of(ctx*240,16),240)], sem.at[z//2]).start()
+def places(idx, kind, pieces):
+    for dc in range(2):
+        for dx in range(2):
+            for dy in range(2):
+                for dz in range(4):
+                    src=pieces[4*dc+2*dx+dy].at[dz] if kind=="z" else pieces[4*dc+dz].at[2*dx+dy]
+                    z=lax.rem(idx[0]+dz,4); y=flip(idx[2],dy)
+                    yield src, 2*z+flip(idx[1],dx), 2*y+flip(idx[3],dc), z, y
+
+def load_rows(idx, kind, pieces, dst, sem):
+    for src,dpi,ctx,z,_ in places(idx,kind,pieces):
+        pltpu.make_async_copy(src.at[pl.ds(0,240)], dst.at[dpi,pl.ds(pl.multiple_of(ctx*240,16),240)], sem.at[z//2]).start()
 
 def wait_rows(dst, sem, j):
     half=dst.at[pl.ds(4*j,4),pl.ds(0,960)]
     pltpu.make_async_copy(half,half,sem.at[j]).wait()
 
-def load_cols(idx, pieces, dst, sem):
-    for p,f,x,ctx,y in pieces_of(idx,"xy"):
-        for dz in range(4):
-            for t in range(dst.shape[2]//128):
-                pltpu.make_async_copy(pieces[p].at[f,dz,:,pl.ds(128*t,128)], dst.at[ctx,lax.rem(idx[0]+dz,4)*2+x,pl.ds(128*t,128)], sem.at[y]).start()
+def load_cols(idx, kind, pieces, dst, sem):
+    for src,dpi,ctx,_,y in places(idx,kind,pieces):
+        for t in range(dst.shape[2]//128):
+            pltpu.make_async_copy(src.at[pl.ds(240,128),pl.ds(128*t,128)], dst.at[ctx,dpi,pl.ds(128*t,128)], sem.at[y]).start()
 
 def wait_cols(dst, sem, j):
     half=dst.at[pl.ds(2*j,2)]
     pltpu.make_async_copy(half,half,sem.at[j]).wait()
 
-def ffn_fwd_kernel(S, last, idx, n2, mid, *refs):
-    gp=refs[:4]; dp_=refs[4:8]
+def ffn_fwd_kernel(S, kind, last, idx, n2, mid, *refs):
+    gp=refs[:8]
     out, h_ref, wd_ref, gu_s, d_s, acc, sem = refs[8:]
     j=pl.program_id(0); i=pl.program_id(1)
     @pl.when((j==0)&(i==0))
     def _():
-        load_rows(idx,gp,gu_s,sem.at[0],(0,1))
-        load_cols(idx,dp_,d_s,sem.at[1])
-        load_rows(idx,gp,gu_s,sem.at[0],(2,3))
+        load_rows(idx,kind,gp,gu_s,sem.at[0])
+        load_cols(idx,kind,gp,d_s,sem.at[1])
     @pl.when(i==0)
     def _():
         wait_rows(gu_s,sem.at[0],j); wait_cols(d_s,sem.at[1],j)
@@ -412,43 +410,44 @@
         if last: out[0,0]=r.T[:D,:].astype(BF)
         else: out[...]=r
 
-def ffn_fwd(idx, n2, mid, gp, dp_, last):
-    S=gp[0].shape[3]//2
+def ffn_fwd(idx, n2, mid, gp, kind, last):
+    S=gp[0].shape[2]//2
     full=pl.BlockSpec((T,DP),lambda j,i,idx:(0,0))
     if last: ospec=pl.BlockSpec((1,1,D,256),lambda j,i,idx:(flip((i*j)%2,idx[3]),flip((i*j)//2,idx[2]),0,0))
     else: ospec=pl.BlockSpec((256,DP),lambda j,i,idx:(i*j,0))
-    return pl.pallas_call(functools.partial(ffn_fwd_kernel,S,last), grid_spec=pltpu.PrefetchScalarGridSpec(num_scalar_prefetch=1,grid=(2,4),
+    return pl.pallas_call(functools.partial(ffn_fwd_kernel,S,kind,last), grid_spec=pltpu.PrefetchScalarGridSpec(num_scalar_prefetch=1,grid=(2,4),
         in_specs=[full,full]+[ANY]*8,
         out_specs=[ospec, pl.BlockSpec((1,256,8*S),lambda j,i,idx:(j,i,0)), pl.BlockSpec((1,4*S,DP),lambda j,i,idx:(j,0,0))],
         scratch_shapes=[pltpu.VMEM((8,DP,2*S),BF),pltpu.VMEM((4,8,2*S,128),BF),pltpu.VMEM((T,DP),F32),pltpu.SemaphoreType.DMA((2,2))]),
         out_shape=[sds((2,2,D,256),BF) if last else sds((T,DP),F32),sds((2,T,8*S),BF),sds((2,4*S,DP),BF)],
-        compiler_params=params(), cost_estimate=cost(20), name="ffn_fwd")(idx,n2,mid,*gp,*dp_)
+        compiler_params=params(), cost_estimate=cost(20), name="ffn_fwd")(idx,n2,mid,*gp)
 
 def slot_of(idx, dpi, ctx):
     z=dpi//2; x=dpi%2; y=ctx//2; c=ctx%2
     return flip(c,idx[3]), flip(x,idx[1]), flip(y,idx[2]), lax.rem(z-idx[0]+4,4)
 
-def put(idx, src, keep, send, sem, yx, dpi, ctx, *at):
+def put(idx, src, keep, send, sem, dpi, ctx, *at):
     c,x,y,z=slot_of(idx,dpi,ctx)
-    if yx: x,y=y,x
     @pl.when(c==0)
     def _(): pltpu.make_async_copy(src,keep.at[(x,y,z)+at],sem).start()
     @pl.when(c==1)
     def _(): pltpu.make_async_copy(src,send.at[(x,y,z)+at],sem).start()
 
-def ffn_bwd_kernel(S, idx, cb, n2, h, wd, dn2in, *refs):
-    gp=refs[:4]
-    dn2, gk, gs, gu_s, dh_s, act_s, dw_s, dd_s, sem, osem = refs[4:]
+def ffn_bwd_kernel(S, kind, first, idx, cb, h, wd, n2h, *refs):
+    if not first:
+        dn2in,*refs=refs
+    gp=refs[:8]
+    dn2, gk, gs, n2, gu_s, dh_s, act_s, dw_s, dd_s, sem, osem, nsem = refs[8:]
     q=pl.program_id(0)
     nq=4*S
     @pl.when(q==0)
-    def _(): load_rows(idx,gp,gu_s,sem,(0,1,2,3))
-    wait_rows(gu_s,sem,q)
-    for k in range(4): gu_s[4*q+k,960:1024,:]=jnp.zeros((64,2*S),BF)
-    w=jnp.concatenate([gu_s[4*q+k] for k in range(4)],axis=-1)
+    def _():
+        load_rows(idx,kind,gp,gu_s,sem)
+        if not first: pltpu.make_async_copy(dn2in,dn2,nsem.at[1]).start()
+        pltpu.make_async_copy(n2h,n2,nsem.at[0]).start()
     wdq=wd[0]
-    def rows_step(i,_):
-        rows=pl.ds(pl.multiple_of(i*256,256),256)
+    def grads(i):
+        rows=slice(i*256,(i+1)*256)
         dact=dot(cb[rows,:],wdq,NT)
         parts=[];acts=[]
         for b in range(4):
@@ -457,24 +456,27 @@
             sg=1/(1+jnp.exp(-g)); sl=g*sg
             acts.append((sl*u).astype(BF))
             parts.append((da*u*(sg+sl*(1-sg))).astype(BF)); parts.append((da*sl).astype(BF))
-        dh=jnp.concatenate(parts,axis=-1)
-        dh_s[rows,:]=dh; act_s[rows,:]=jnp.concatenate(acts,axis=-1)
-        t=dot(dh,w,NT)
-        dn2[rows,:]=jnp.where(q==0,dn2in[rows,:],dn2[rows,:])+t
-        return 0
-    lax.fori_loop(0,4,rows_step,0)
+        dh_s[rows,:]=jnp.concatenate(parts,axis=-1); act_s[rows,:]=jnp.concatenate(acts,axis=-1)
+    def back(i):
+        rows=slice(i*256,(i+1)*256)
+        t=dot(dh_s[rows,:],w,NT)
+        dn2[rows,:]=(jnp.where(q==0,0.0,dn2[rows,:]) if first else dn2[rows,:])+t
+    grads(0)
+    wait_rows(gu_s,sem,q)
+    @pl.when(q==0)
+    def _():
+        if not first: pltpu.make_async_copy(dn2in,dn2,nsem.at[1]).wait()
+        pltpu.make_async_copy(n2h,n2,nsem.at[0]).wait()
     @pl.when(q==1)
     def _():
         pltpu.make_async_copy(dw_s.at[pl.ds(0,960)],dw_s.at[pl.ds(0,960)],osem.at[0]).wait()
         pltpu.make_async_copy(dd_s,dd_s,osem.at[1]).wait()
-    def dw_step(m,_):
-        cols=pl.ds(pl.multiple_of(m*256,256),256)
-        dw_s[cols,:]=dot(n2[:,cols],dh_s[...],TN).astype(BF)
-        return 0
-    lax.fori_loop(0,4,dw_step,0)
-    for b in range(4):
-        for ctx in range(4):
-            put(idx,dw_s.at[pl.ds(ctx*240,240),pl.ds(b*2*S,2*S)],gk,gs,osem.at[0],False,4*q+b,ctx,pl.ds(0,240))
+    for k in range(4): gu_s[4*q+k,960:1024,:]=jnp.zeros((64,2*S),BF)
+    w=jnp.concatenate([gu_s[4*q+k] for k in range(4)],axis=-1)
+    for i in range(1,4):
+        back(i-1)
+        grads(i)
+    back(3)
     for m in range(nq//256):
         r=dot(act_s[:,m*256:(m+1)*256],cb[...],TN)
         for k in range(8):
@@ -482,91 +484,115 @@
     for k in range(8):
         for cc in range(2):
             for t in range(2*S//128):
-                put(idx,dd_s.at[k,pl.ds(cc*2*S+128*t,128)],gk,gs,osem.at[1],True,k,2*q+cc,pl.ds(240,128),pl.ds(128*t,128))
+                put(idx,dd_s.at[k,pl.ds(cc*2*S+128*t,128)],gk,gs,osem.at[1],k,2*q+cc,pl.ds(240,128),pl.ds(128*t,128))
+    def dw_step(m):
+        cols=pl.ds(pl.multiple_of(m*256,256),256)
+        dw_s[cols,:]=dot(n2[:,cols],dh_s[...],TN).astype(BF)
+        return 0
+    for m in range(4): dw_step(m)
+    for b in range(4):
+        for ctx in range(4):
+            put(idx,dw_s.at[pl.ds(ctx*240,240),pl.ds(b*2*S,2*S)],gk,gs,osem.at[0],4*q+b,ctx,pl.ds(0,240))
     @pl.when(q==1)
     def _():
         pltpu.make_async_copy(dw_s.at[pl.ds(0,960)],dw_s.at[pl.ds(0,960)],osem.at[0]).wait()
         pltpu.make_async_copy(dd_s,dd_s,osem.at[1]).wait()
 
-def ffn_bwd(idx, cb, n2, h, wd, dn2in, gp):
-    S=gp[0].shape[3]//2
+def ffn_bwd(idx, cb, n2, h, wd, dn2in, gp, kind, rows):
+    S=gp[0].shape[2]//2
     full=const((T,DP))
-    return pl.pallas_call(functools.partial(ffn_bwd_kernel,S), grid=(2,),
-        in_specs=[SMEM,full,full,pl.BlockSpec((1,T,8*S),lambda q:(q,0,0)),pl.BlockSpec((1,4*S,DP),lambda q:(q,0,0)),full]+[ANY]*4,
+    return pl.pallas_call(functools.partial(ffn_bwd_kernel,S,kind,dn2in is None), grid=(2,),
+        in_specs=[SMEM,full,pl.BlockSpec((1,T,8*S),lambda q:(q,0,0)),pl.BlockSpec((1,4*S,DP),lambda q:(q,0,0))]+[ANY]*(9+(dn2in is not None)),
         out_specs=[full,ANY,ANY],
-        out_shape=[sds((T,DP),F32)]+[sds((2,2,4,368,2*S),BF)]*2,
-        scratch_shapes=[pltpu.VMEM((8,DP,2*S),BF),pltpu.VMEM((T,8*S),BF),pltpu.VMEM((T,4*S),BF),pltpu.VMEM((DP,8*S),BF),pltpu.VMEM((8,4*S,128),BF),pltpu.SemaphoreType.DMA((2,)),pltpu.SemaphoreType.DMA((2,))],
-        compiler_params=params(), cost_estimate=cost(33), name="ffn_bwd")(idx,cb,n2,h,wd,dn2in,*gp)
+        out_shape=[sds((T,DP),F32)]+[sds((2,2,4,rows,2*S),BF)]*2,
+        scratch_shapes=[pltpu.VMEM((T,DP),BF),pltpu.VMEM((8,DP,2*S),BF),pltpu.VMEM((T,8*S),BF),pltpu.VMEM((T,4*S),BF),pltpu.VMEM((DP,8*S),BF),pltpu.VMEM((8,4*S,128),BF)]+[pltpu.SemaphoreType.DMA((2,))]*3,
+        compiler_params=params(), cost_estimate=cost(33), name="ffn_bwd")(idx,cb,h,wd,n2,*([] if dn2in is None else [dn2in]),*gp)
+
+def block(f): return f.astype(F32)
+def reduce_one_kernel(keep, rc, sx, sy, sxy):
+    def s(x,y): return (block(keep[x,y,0])+block(rc[x,y,0])).astype(BF)
+    sx[0]=s(1,0); sy[0]=s(0,1); sxy[0]=s(1,1)
+def reduce_one(keep, rc):
+    _,_,_,r,n=keep.shape
+    b=pl.BlockSpec((2,2,1,r,n),lambda k:(0,0,k,0,0)); o=pl.BlockSpec((1,r,n),lambda k:(k,0,0))
+    return pl.pallas_call(reduce_one_kernel,grid=(4,),in_specs=[b,b],out_specs=[o]*3,out_shape=[sds((4,r,n),BF)]*3,compiler_params=params(),cost_estimate=cost(3),name="reduce_one")(keep,rc)
+def reduce_two_kernel(keep, rc, a, b, c, own, s1, s2, s3):
+    k=pl.program_id(0)
+    t=block(keep[0,0,0])+block(rc[0,0,0])+block(a[0])+block(b[0])+block(c[0])
+    @pl.when(k==0)
+    def _(): own[...]=t
+    for j,s in ((1,s1),(2,s2),(3,s3)):
+        @pl.when(k==j)
+        def _(s=s): s[...]=t.astype(BF)
+def reduce_two(keep, rc, a, b, c):
+    _,_,_,r,n=keep.shape
+    kb=pl.BlockSpec((1,1,1,r,n),lambda k:(0,0,k,0,0)); ib=pl.BlockSpec((1,r,n),lambda k:(k,0,0)); ob=pl.BlockSpec((r,n),lambda k:(0,0))
+    return pl.pallas_call(reduce_two_kernel,grid=(4,),in_specs=[kb,kb,ib,ib,ib],out_specs=[ob]*4,out_shape=[sds((r,n),F32)]+[sds((r,n),BF)]*3,compiler_params=params(),cost_estimate=cost(3),name="reduce_two")(keep,rc,a,b,c)
 
 NEG=-1e30
 QB=256
+def causal(keys, shape):
+    a=lax.broadcasted_iota(jnp.int32,shape,keys); b=lax.broadcasted_iota(jnp.int32,shape,1-keys)%QB
+    return a<=b
+
 def attn_fwd_kernel(q, k, v, o, lse):
-    ri=lax.broadcasted_iota(jnp.int32,(QB,QB),0); ci=lax.broadcasted_iota(jnp.int32,(QB,QB),1)
+    n=3*QB
     for qi in range(T//QB):
         rows=slice(qi*QB,(qi+1)*QB); kn=(qi+1)*QB
-        qb=q[0,rows,:]
-        s=dot(qb,k[0,0:kn,:],NT)
-        sd=jnp.where(ci<=ri,s[:,kn-QB:],NEG)
+        s=dot(q[:,rows,:].reshape(n,128),k[0,0:kn,:],NT)
+        sd=jnp.where(causal(1,(n,QB)),s[:,kn-QB:],NEG)
         s=sd if qi==0 else jnp.concatenate([s[:,:kn-QB],sd],axis=-1)
         m=jnp.max(s,axis=-1,keepdims=True)
-        p=jnp.exp(s-m)
-        r=dot(p.astype(BF),v[0,0:kn,:])
+        r=dot(jnp.exp(s-m).astype(BF),v[0,0:kn,:])
         l=r[:,64:65]
-        o[0,rows,:]=(r/l).astype(BF)
-        e=jnp.broadcast_to(m+jnp.log(l),(QB,128))
-        lse[0,:,rows]=e.T[0:1,:]
+        o[:,rows,:]=(r/l).astype(BF).reshape(3,QB,128)
+        e=jnp.broadcast_to(m+jnp.log(l),(n,128)).T[0:1,:]
+        for h in range(3): lse[h,:,rows]=e[:,h*QB:(h+1)*QB]
 
 def attn_fwd(q,k,v,g0,ng):
-    qs=pl.BlockSpec((1,T,128),lambda g,r:(3*(g+g0)+r,0,0)); ks=pl.BlockSpec((1,T,128),lambda g,r:(g+g0,0,0)); os_=pl.BlockSpec((1,T,128),lambda g,r:(3*g+r,0,0))
-    return pl.pallas_call(attn_fwd_kernel,grid=(ng,3),in_specs=[qs,ks,ks],
-        out_specs=[os_,pl.BlockSpec((1,1,T),lambda g,r:(3*g+r,0,0))],
-        out_shape=[sds((3*ng,T,128),BF),sds((3*ng,1,T),F32)],compiler_params=params(),cost_estimate=cost(6*ng), name="attn_fwd")(q,k,v)
+    qs=pl.BlockSpec((3,T,128),lambda g:(g+g0,0,0)); ks=pl.BlockSpec((1,T,128),lambda g:(g+g0,0,0))
+    return pl.pallas_call(attn_fwd_kernel,grid=(ng,),in_specs=[qs,ks,ks],
+        out_specs=[pl.BlockSpec((3,T,128),lambda g:(g,0,0)),pl.BlockSpec((3,1,T),lambda g:(g,0,0))],
+        out_shape=[sds((3*ng,T,128),BF),sds((3*ng,1,T),F32)],compiler_params=params(),cost_estimate=cost(6*ng),name="attn_fwd")(q,k,v)
 
 def unrot(g,c,s,low):
     t=jnp.where(low,pltpu.roll(g,96,1),-pltpu.roll(g,32,1))
     return g*c+t*s
 
-def attn_bwd_kernel(q,k,v,do,lse,c,s,dq,dk,dv,dka,dva,dqa):
-    r_=pl.program_id(1)
-    @pl.when(r_==0)
-    def _():
-        dka[...]=jnp.zeros_like(dka); dva[...]=jnp.zeros_like(dva)
-    ki=lax.broadcasted_iota(jnp.int32,(QB,QB),0); qi_=lax.broadcasted_iota(jnp.int32,(QB,QB),1)
+def attn_bwd_kernel(q,k,v,do,lse,delta,c,s,dq,dk,dv,dka,dva):
+    n=3*QB
     low=lax.broadcasted_iota(jnp.int32,(QB,128),1)%64<32
-    for qi in range(T//QB):
+    nb=T//QB
+    for qi in range(nb-1,-1,-1):
         rows=slice(qi*QB,(qi+1)*QB); kn=(qi+1)*QB
-        qb=q[0,rows,:]; dob=do[0,rows,:]; kb=k[0,0:kn,:]
-        st=dot(kb,qb,NT)
-        pt=jnp.exp(st-lse[0,:,rows])
-        pd=jnp.where(ki<=qi_,pt[kn-QB:],0.0)
+        qb=q[:,rows,:].reshape(n,128); dob=do[:,rows,:].reshape(n,128); kb=k[0,0:kn,:]
+        cat=lambda r: jnp.concatenate([r[h,:,rows] for h in range(3)],axis=-1)
+        pt=jnp.exp(dot(kb,qb,NT)-cat(lse))
+        pd=jnp.where(causal(0,(QB,n)),pt[kn-QB:],0.0)
         pt=pd if qi==0 else jnp.concatenate([pt[:kn-QB],pd],axis=0)
-        dpt=dot(v[0,0:kn,:],dob,NT)
-        dva[0:kn,:]+=dot(pt.astype(BF),dob)
-        t=pt*dpt
-        delta=jnp.sum(t,axis=0,keepdims=True)
-        dst=(t-pt*delta).astype(BF)
-        dka[0:kn,:]+=dot(dst,qb)
-        dqr=dot(dst,kb,TN)*0.125
-        dq[0,rows,:]=unrot(dqr,c[rows,:],s[rows,:],low).astype(BF)
-    @pl.when(r_==2)
-    def _():
-        for qi in range(T//QB):
-            rows=slice(qi*QB,(qi+1)*QB)
-            dk[0,rows,:]=unrot(dka[rows,:],c[rows,:],s[rows,:],low).astype(BF)
-            dv[0,rows,:]=dva[rows,:].astype(BF)
-
-def attn_bwd(q,k,v,do,lse,c,s,g0,ng):
-    qs=pl.BlockSpec((1,T,128),lambda g,r:(3*(g+g0)+r,0,0)); ks=pl.BlockSpec((1,T,128),lambda g,r:(g+g0,0,0))
-    qo=pl.BlockSpec((1,T,128),lambda g,r:(3*g+r,0,0)); ko=pl.BlockSpec((1,T,128),lambda g,r:(g,0,0))
-    return pl.pallas_call(attn_bwd_kernel,grid=(ng,3),in_specs=[qs,ks,ks,qs,pl.BlockSpec((1,1,T),lambda g,r:(3*g+r,0,0)),const((T,128)),const((T,128))],
+        dst=(pt*(dot(v[0,0:kn,:],dob,NT)-cat(delta))).astype(BF)
+        a=dot(pt.astype(BF),dob); b=dot(dst,qb)
+        if qi==nb-1: dva[...]=a; dka[...]=b
+        else: dva[0:kn,:]+=a; dka[0:kn,:]+=b
+        g=dot(dst,kb,TN)*0.125
+        for h in range(3):
+            dq[h,rows,:]=unrot(g[h*QB:(h+1)*QB],c[rows,:],s[rows,:],low).astype(BF)
+    for qi in range(nb):
+        rows=slice(qi*QB,(qi+1)*QB)
+        dk[0,rows,:]=unrot(dka[rows,:],c[rows,:],s[rows,:],low).astype(BF)
+        dv[0,rows,:]=dva[rows,:].astype(BF)
+
+def attn_bwd(q,k,v,do,lse,delta,c,s,g0,ng):
+    qs=pl.BlockSpec((3,T,128),lambda g:(g+g0,0,0)); ks=pl.BlockSpec((1,T,128),lambda g:(g+g0,0,0))
+    qo=pl.BlockSpec((3,T,128),lambda g:(g,0,0)); ko=pl.BlockSpec((1,T,128),lambda g:(g,0,0))
+    return pl.pallas_call(attn_bwd_kernel,grid=(ng,),in_specs=[qs,ks,ks,qs]+[pl.BlockSpec((3,1,T),lambda g:(g+g0,0,0))]*2+[const((T,128)),const((T,128))],
         out_specs=[qo,ko,ko],
         out_shape=[sds((3*ng,T,128),BF),sds((ng,T,128),BF),sds((ng,T,128),BF)],
-        scratch_shapes=[pltpu.VMEM((T,128),F32),pltpu.VMEM((T,128),F32),pltpu.VMEM((8,128),F32)],
-        compiler_params=params(),cost_estimate=cost(9*ng), name="attn_bwd")(q,k,v,do,lse,c,s)
+        scratch_shapes=[pltpu.VMEM((T,128),F32),pltpu.VMEM((T,128),F32)],
+        compiler_params=params(),cost_estimate=cost(9*ng),name="attn_bwd")(q,k,v,do,lse,delta,c,s)
 
 EPS=1e-5
 WN=1664
-CUT=160
 def prefetch(grid,in_specs,out_specs,scratch): return pltpu.PrefetchScalarGridSpec(num_scalar_prefetch=1,grid=grid,in_specs=in_specs,out_specs=out_specs,scratch_shapes=scratch)
 def tok(i,idx): return (flip(i%2,idx[3]),flip(i//2,idx[2]),0,0)
 tok_spec=lambda: pl.BlockSpec((1,1,D,256),tok)
@@ -576,21 +602,18 @@
 def zeros(r,n,dt=F32): return jnp.zeros((r,n),dt)
 
 def qkv_kernel(idx, x, c, s, *refs):
-    pa=refs[:4]; pb=refs[4:8]
-    n1,q,k,v,w,wo,gains,s1,sem=refs[8:]
+    pc=refs[:8]
+    n1,q,k,v,w,gains,s1,sem=refs[8:]
     i=pl.program_id(0)
     @pl.when(i==0)
     def _():
-        for order,pc,lo,n in (("yx",pa,0,CUT),("xy",pb,CUT,256-CUT)):
-            for p,f,xx,ctx,_ in pieces_of(idx,order):
-                for dz in range(4):
-                    pltpu.make_async_copy(pc[p].at[f,dz], s1.at[lax.rem(idx[0]+dz,4)*2+xx,ctx,pl.ds(lo,n)], sem).start()
+        for src,dpi,ctx,_,_ in places(idx,"z",pc):
+            pltpu.make_async_copy(src, s1.at[dpi,ctx], sem).start()
         pltpu.make_async_copy(s1,s1,sem).wait()
         for t in range(4):
             rows=slice(240*t,240*t+240)
             w[rows,:]=jnp.concatenate([s1[d,t,0:240,0:120] for d in range(8)]+[s1[d,t,0:240,128:168] for d in range(8)]+[s1[d,t,0:240,168:208] for d in range(8)]+[zeros(240,64,BF)],axis=-1)
-            wo[rows,:]=jnp.concatenate([s1[d,t,0:240,256:376] for d in range(8)]+[zeros(240,64,BF)],axis=-1)
-        w[960:1024,:]=zeros(64,WN,BF); wo[960:1024,:]=zeros(64,DP,BF)
+        w[960:1024,:]=zeros(64,WN,BF)
         gl=[s1[d,t,240:256,0:128].astype(F32)[0:1,0:60] for d in range(8) for t in range(4)]
         gains[0:1,:]=jnp.concatenate(gl[:16]+[zeros(1,64)],axis=-1)
         gains[1:2,:]=jnp.concatenate(gl[16:]+[zeros(1,64)],axis=-1)
@@ -614,14 +637,24 @@
     for e in range(5):
         v[e]=jnp.concatenate([h[:,1280+64*e:1344+64*e].astype(BF),one],axis=-1)
 
-def qkv_fwd(idx,x,c,s,pa,pb):
+def qkv_fwd(idx,x,c,s,pc):
     return pl.pallas_call(qkv_kernel,grid_spec=prefetch((4,),[row_spec(DP),row_spec(128),row_spec(128)]+[ANY]*8,
-        [row_spec(DP),head_spec(15),head_spec(5),head_spec(5),cst((DP,WN)),cst((DP,DP)),cst((2,DP))],
-        [pltpu.VMEM((8,4,256,384),BF),pltpu.SemaphoreType.DMA]),
-        out_shape=[sds((T,DP),BF),sds((15,T,128),BF),sds((5,T,128),BF),sds((5,T,128),BF),sds((DP,WN),BF),sds((DP,DP),BF),sds((2,DP),F32)],
-        compiler_params=params(),cost_estimate=cost(16), name="qkv_fwd")(idx,x,c,s,*pa,*pb)
-
-def out_kernel(idx,o1,o2,x,gains,wo,att,mid,n2):
+        [row_spec(DP),head_spec(15),head_spec(5),head_spec(5),cst((DP,WN)),cst((2,DP))],
+        [pltpu.VMEM((8,4,256,256),BF),pltpu.SemaphoreType.DMA]),
+        out_shape=[sds((T,DP),BF),sds((15,T,128),BF),sds((5,T,128),BF),sds((5,T,128),BF),sds((DP,WN),BF),sds((2,DP),F32)],
+        compiler_params=params(),cost_estimate=cost(16), name="qkv_fwd")(idx,x,c,s,*pc)
+
+def out_kernel(idx,o1,o2,x,gains,*refs):
+    pc=refs[:8]
+    att,mid,n2,wo,ws,sem=refs[8:]
+    @pl.when(pl.program_id(0)==0)
+    def _():
+        for src,dpi,ctx,_,_ in places(idx,"z",pc):
+            for t in range(3):
+                pltpu.make_async_copy(src.at[pl.ds(368,80),pl.ds(128*t,128)], ws.at[dpi,pl.ds(pl.multiple_of(ctx*240+80*t,16),80)], sem).start()
+        pltpu.make_async_copy(ws,ws,sem).wait()
+        wo[0:D,:]=jnp.concatenate([ws[d][:,0:120] for d in range(8)]+[zeros(D,64,BF)],axis=-1)
+        wo[D:DP,:]=zeros(64,DP,BF)
     a=jnp.concatenate([o[h][:,0:64] for o in (o1,o2) for h in range(o.shape[0])]+[zeros(256,64,BF)],axis=-1)
     att[...]=a
     m=dot(a,wo[...])+x[...].astype(F32)
@@ -629,9 +662,9 @@
     r=lax.rsqrt(jnp.sum(m*m,axis=-1,keepdims=True)*(1.0/D)+EPS)
     n2[...]=(m*r*gains[1:2,:]).astype(BF)
 
-def out_fwd(idx,o1,o2,x,gains,wo):
-    return pl.pallas_call(out_kernel,grid_spec=prefetch((4,),[head_spec(o1.shape[0]),head_spec(o2.shape[0]),row_spec(DP),cst((2,DP)),cst((DP,DP))],
-        [row_spec(DP)]*3,[]),out_shape=[sds((T,DP),BF),sds((T,DP),F32),sds((T,DP),BF)],compiler_params=params(),cost_estimate=cost(9), name="out_fwd")(idx,o1,o2,x,gains,wo)
+def out_fwd(idx,o1,o2,x,gains,pc):
+    return pl.pallas_call(out_kernel,grid_spec=prefetch((4,),[head_spec(o1.shape[0]),head_spec(o2.shape[0]),row_spec(DP),cst((2,DP))]+[ANY]*8,
+        [row_spec(DP)]*3+[cst((DP,DP))],[pltpu.VMEM((8,D,128),BF),pltpu.SemaphoreType.DMA]),out_shape=[sds((T,DP),BF),sds((T,DP),F32),sds((T,DP),BF),sds((DP,DP),BF)],compiler_params=params(),cost_estimate=cost(9),name="out_fwd")(idx,o1,o2,x,gains,*pc)
 
 def tok_in_kernel(idx,h,r,g,o):
     y=idx[2]; c=idx[3]
@@ -641,8 +674,9 @@
 def tok_in(idx,h,r,g):
     return pl.pallas_call(tok_in_kernel,in_specs=[SMEM]+[pl.BlockSpec(memory_space=pltpu.VMEM)]*3,out_specs=pl.BlockSpec(memory_space=pltpu.VMEM),out_shape=sds((T,DP),BF),compiler_params=params(),cost_estimate=cost(4),name="tok_in")(idx,h,r,g)
 
-def out_bwd_kernel(idx,dn2,cb,mid,gains,wo,att,dmid,do,dg,ok,os_,dbr_s,st,sem):
+def out_bwd_kernel(idx,dn2,cb,mid,gains,wo,att,kin,sin,dmid,do,dg,ok,os_,delta,dbr_s,st,sem):
     i=pl.program_id(0)
+    rows=pl.ds(pl.multiple_of(i*256,256),256)
     m=mid[...]; r=lax.rsqrt(jnp.sum(m*m,axis=-1,keepdims=True)*(1.0/D)+EPS)
     d=dn2[...]; gd=gains[1:2,:]*d
     dm=cb[...].astype(F32)+r*gd-m*(r*r*r)*(jnp.sum(gd*m,axis=-1,keepdims=True)*(1.0/D))
@@ -650,10 +684,15 @@
     g=jnp.sum(d*m*r,axis=0,keepdims=True)
     dg[...]=g+jnp.where(i==0,0.0,dg[...])
     b=dm.astype(BF)
-    dbr_s[pl.ds(pl.multiple_of(i*256,256),256),:]=b
-    da=dot(b,wo[...],NT)
+    dbr_s[rows,:]=b
+    da=dot(b,wo[...],NT).astype(BF)
     z64=zeros(256,64,BF)
-    for h in range(15): do[h]=jnp.concatenate([da[:,64*h:64*h+64].astype(BF),z64],axis=-1)
+    for h in range(15): do[h]=jnp.concatenate([da[:,64*h:64*h+64],z64],axis=-1)
+    p=da.astype(F32)*att[rows,:].astype(F32)
+    hi=p.astype(BF); lo=(p-hi.astype(F32)).astype(BF)
+    e=jnp.where(lax.broadcasted_iota(jnp.int32,(DP,128),0)//64==lax.broadcasted_iota(jnp.int32,(DP,128),1),1.0,0.0).astype(BF)
+    de=(dot(hi,e)+dot(lo,e)).T
+    for h in range(15): delta[h]=de[h:h+1,:]
     @pl.when(i==3)
     def _():
         for mm in range(4):
@@ -662,56 +701,56 @@
                 st[k,256*mm:256*mm+256,:]=jnp.concatenate([rr[:,120*k:120*k+120],zeros(256,8)],axis=-1).astype(BF)
         for k in range(8):
             for t in range(4):
-                put(idx,st.at[k,pl.ds(240*t,CUT)],ok,os_,sem,False,k,t,pl.ds(0,CUT)); put(idx,st.at[k,pl.ds(240*t+CUT,240-CUT)],ok,os_,sem,True,k,t,pl.ds(CUT,240-CUT))
+                put(idx,st.at[k,pl.ds(240*t,128)],ok,os_,sem,k,t,pl.ds(368,128),pl.ds(0,128)); put(idx,st.at[k,pl.ds(240*t+128,112)],ok,os_,sem,k,t,pl.ds(368,112),pl.ds(128,128))
         pltpu.make_async_copy(st.at[:,pl.ds(0,960)],st.at[:,pl.ds(0,960)],sem).wait()
 
-def out_bwd(idx,dn2,cb,mid,gains,wo,att):
-    return pl.pallas_call(out_bwd_kernel,grid_spec=prefetch((4,),[row_spec(DP)]*3+[cst((2,DP)),cst((DP,DP)),cst((T,DP))],
-        [row_spec(DP),head_spec(15),cst((1,DP)),ANY,ANY],[pltpu.VMEM((T,DP),BF),pltpu.VMEM((8,DP,128),BF),pltpu.SemaphoreType.DMA]),
-        out_shape=[sds((T,DP),F32),sds((15,T,128),BF),sds((1,DP),F32)]+[sds((2,2,4,240,128),BF)]*2,
-        compiler_params=params(),cost_estimate=cost(16), name="out_bwd")(idx,dn2,cb,mid,gains,wo,att)
-
-def qkv_bwd_kernel(idx,dq1,dk1,dv1,dq2,dk2,dv2,x,gains,n1,dmid,w,dg2,hg,wk,ws,dh_s,st,sg,dg1,sem):
+def out_bwd(idx,dn2,cb,mid,gains,wo,att,keep,send):
+    return pl.pallas_call(out_bwd_kernel,grid_spec=prefetch((4,),[row_spec(DP)]*3+[cst((2,DP)),cst((DP,DP)),cst((T,DP)),ANY,ANY],
+        [row_spec(DP),head_spec(15),cst((1,DP)),ANY,ANY,pl.BlockSpec((15,1,256),lambda i,idx:(0,0,i))],[pltpu.VMEM((T,DP),BF),pltpu.VMEM((8,DP,128),BF),pltpu.SemaphoreType.DMA]),
+        out_shape=[sds((T,DP),F32),sds((15,T,128),BF),sds((1,DP),F32)]+[sds(keep.shape,BF)]*2+[sds((15,1,T),F32)],input_output_aliases={7:3,8:4},
+        compiler_params=params(),cost_estimate=cost(16), name="out_bwd")(idx,dn2,cb,mid,gains,wo,att,keep,send)
+
+def qkv_dx_kernel(idx,dq1,dk1,dv1,dq2,dk2,dv2,dq3,dk3,dv3,x,gains,dmid,w,hg,dh,dg1):
     i=pl.program_id(0)
-    dh=jnp.concatenate([r[h][:,0:64] for r in (dq1,dq2,dk1,dk2,dv1,dv2) for h in range(r.shape[0])]+[zeros(256,64,BF)],axis=-1)
-    dh_s[pl.ds(pl.multiple_of(i*256,256),256),:]=dh
-    d=dot(dh,w[...],NT)[:,0:D]
-    xf=x[:,0:D].astype(F32)
+    h=jnp.concatenate([r[h][:,0:64] for r in (dq1,dq2,dq3,dk1,dk2,dk3,dv1,dv2,dv3) for h in range(r.shape[0])]+[zeros(256,64,BF)],axis=-1)
+    dh[...]=h
+    d=dot(h,w[...],NT)
+    xf=x[...].astype(F32)
     r=lax.rsqrt(jnp.sum(xf*xf,axis=-1,keepdims=True)*(1.0/D)+EPS)
-    gd=gains[0:1,0:D]*d
-    hh=dmid[:,0:D]+r*gd-xf*(r*r*r)*(jnp.sum(gd*xf,axis=-1,keepdims=True)*(1.0/D))
-    hg[0,0]=jnp.concatenate([hh,zeros(256,64)],axis=-1).T[:D,:].astype(BF)
+    gd=gains[0:1,:]*d
+    hh=dmid[...]+r*gd-xf*(r*r*r)*(jnp.sum(gd*xf,axis=-1,keepdims=True)*(1.0/D))
+    hg[0,0]=hh.T[:D,:].astype(BF)
     g=jnp.sum(d*xf*r,axis=0,keepdims=True)
     dg1[...]=g+jnp.where(i==0,0.0,dg1[...])
-    @pl.when(i==3)
-    def _():
-        for m in range(4):
-            r_=dot(n1[:,256*m:256*m+256],dh_s[...],TN)
-            for k in range(8):
-                st[k,256*m:256*m+256,:]=jnp.concatenate([r_[:,120*k:120*k+120],zeros(256,8),r_[:,960+40*k:1000+40*k],r_[:,1280+40*k:1320+40*k],zeros(256,48)],axis=-1).astype(BF)
+
+def qkv_dx(idx,g1,g2,g3,x,gains,dmid,w):
+    return pl.pallas_call(qkv_dx_kernel,grid_spec=prefetch((4,),[head_spec(a.shape[0]) for a in (*g1,*g2,*g3)]+[row_spec(DP),cst((2,DP)),row_spec(DP),cst((DP,WN))],
+        [tok_spec(),row_spec(WN),cst((1,DP))],[]),out_shape=[sds((2,2,D,256),BF),sds((T,WN),BF),sds((1,DP),F32)],
+        compiler_params=params(),cost_estimate=cost(9),name="qkv_dx")(idx,*g1,*g2,*g3,x,gains,dmid,w)
+
+def qkv_dw_kernel(idx,n1,dh,dg1,dg2,wk,ws,st,sg,sem):
+    m=pl.program_id(0)
+    r=dot(n1[...],dh[...],TN)
+    rows=pl.ds(pl.multiple_of(256*m,256),256)
+    for k in range(8):
+        st[k,rows,:]=jnp.concatenate([r[:,120*k:120*k+120],zeros(256,8),r[:,960+40*k:1000+40*k],r[:,1280+40*k:1320+40*k],zeros(256,48)],axis=-1).astype(BF)
+    @pl.when(m==3)
+    def _():
         sg[...]=jnp.zeros_like(sg)
         for k in range(8):
             for t in range(4):
                 o=(4*k+t)*60
                 src=dg1[:,o:o+60] if k<4 else dg2[:,o-960:o-900]
                 sg[k,t,:,0:128]=jnp.broadcast_to(jnp.concatenate([src,zeros(1,68)],axis=-1),(16,128)).astype(BF)
-                c,xx,y,z=slot_of(idx,k,t)
-                def go(dst):
-                    pltpu.make_async_copy(st.at[k,pl.ds(240*t,CUT)],dst.at[xx,y,z,pl.ds(0,CUT)],sem).start()
-                    pltpu.make_async_copy(st.at[k,pl.ds(240*t+CUT,240-CUT)],dst.at[y,xx,z,pl.ds(CUT,240-CUT)],sem).start()
-                    pltpu.make_async_copy(sg.at[k,t],dst.at[y,xx,z,pl.ds(240,16)],sem).start()
-                @pl.when(c==0)
-                def _(): go(wk)
-                @pl.when(c==1)
-                def _(): go(ws)
+                put(idx,st.at[k,pl.ds(240*t,240)],wk,ws,sem,k,t,pl.ds(0,240))
+                put(idx,sg.at[k,t],wk,ws,sem,k,t,pl.ds(240,16))
         pltpu.make_async_copy(st.at[:,pl.ds(0,960)],st.at[:,pl.ds(0,960)],sem).wait()
         pltpu.make_async_copy(sg,sg,sem).wait()
 
-def qkv_bwd(idx,g1,g2,x,gains,n1,dmid,w,dg2):
-    return pl.pallas_call(qkv_bwd_kernel,grid_spec=prefetch((4,),[head_spec(a.shape[0]) for a in (*g1,*g2)]+[row_spec(DP),cst((2,DP)),cst((T,DP)),row_spec(DP),cst((DP,WN)),cst((1,DP))],
-        [tok_spec(),ANY,ANY],[pltpu.VMEM((T,WN),BF),pltpu.VMEM((8,DP,256),BF),pltpu.VMEM((8,4,16,256),BF),pltpu.VMEM((1,D),F32),pltpu.SemaphoreType.DMA]),
-        out_shape=[sds((2,2,D,256),BF)]+[sds((2,2,4,256,256),BF)]*2,
-        compiler_params=params(),cost_estimate=cost(18), name="qkv_bwd")(idx,*g1,*g2,x,gains,n1,dmid,w,dg2)
+def qkv_dw(idx,n1,dh,dg1,dg2):
+    return pl.pallas_call(qkv_dw_kernel,grid_spec=prefetch((4,),[pl.BlockSpec((T,256),lambda m,idx:(0,m)),cst((T,WN)),cst((1,DP)),cst((1,DP))],
+        [ANY,ANY],[pltpu.VMEM((8,DP,256),BF),pltpu.VMEM((8,4,16,256),BF),pltpu.SemaphoreType.DMA]),out_shape=[sds((2,2,4,256,256),BF)]*2,
+        compiler_params=params(),cost_estimate=cost(9),name="qkv_dw")(idx,n1,dh,dg1,dg2)
 
 def tok_out_kernel(idx,a,r,b,o):
     y=idx[2]; c=idx[3]
@@ -727,6 +766,9 @@
     return lax.ppermute(a, axis, [(i, i ^ bit) for i in range(n)])
 
 def move(a, name):
+    if name == "xy":
+        n = lax.axis_size("ctx")
+        return lax.ppermute(a, ("dp", "ctx"), [(i, (i // n ^ 1) * n + (i % n ^ 2)) for i in range(n * lax.axis_size("dp"))])
     if name == "x": return swap(a, "dp", 1)
     if name == "y": return swap(a, "ctx", 2)
     return swap(a, "ctx", 1)
@@ -737,43 +779,29 @@
 def after(a, *others):
     return lax.optimization_barrier((a,) + others)[0]
 
-def gather_z(shard, cut):
-    ps = [shard] + [from_z(shard, k) for k in (1, 2, 3)]
-    return jnp.stack([p[:cut] for p in ps]), jnp.stack([p[cut:] for p in ps])
-
-def gather_first(g):
-    a, b = g
-    return jnp.stack([a, move(a, "y")]), jnp.stack([b, move(b, "x")])
-
-def gather_second(g):
-    a, b = g
-    return (a, move(a, "x")), (b, move(b, "y"))
-
-def gather_core(g):
-    return [list(h) + [move(p, "c") for p in h] for h in g]
+def gather_z(shard):
+    return jnp.stack([shard] + [from_z(shard, k) for k in (1, 2, 3)])
+
+def gather_rest(g):
+    ps = [g] + [move(g, name) for name in ("y", "x", "xy")]
+    return ps + [move(p, "c") for p in ps]
+
+def gather_flat(shard):
+    g = jnp.stack([shard] + [move(shard, name) for name in ("y", "x", "xy")])
+    ps = [g] + [from_z(g, k) for k in (1, 2, 3)]
+    return ps + [move(p, "c") for p in ps]
 
 def add(*terms):
     total = terms[0].astype(F32)
     for t in terms[1:]: total = total + t.astype(F32)
     return total
 
-def reduce_core(send):
-    return move(send, "c")
-
-def reduce_first(keep, rc, cut):
-    low = add(keep[1], rc[1]).astype(BF)
-    return move(low[:, :, :cut], "x"), move(low[:, :, cut:], "y")
-
-def reduce_second(keep, rc, r1, cut):
-    a, b = r1
-    low = add(keep[0, 1], rc[0, 1])
-    return (move((low[:, :cut] + a[1].astype(F32)).astype(BF), "y"),
-            move((low[:, cut:] + b[1].astype(F32)).astype(BF), "x"))
-
-def reduce_z(keep, rc, r1, r2):
-    own = add(keep[0, 0], rc[0, 0], jnp.concatenate([r1[0][0], r1[1][0]], axis=1), jnp.concatenate(r2, axis=1))
-    low = own.astype(BF)
-    return own[0], [from_z(low[k], 4 - k) for k in (1, 2, 3)]
+def reduce_pieces(keep, send):
+    rc = move(send, "c")
+    parts = reduce_one(keep, rc)
+    parts = [move(p, n) for p, n in zip(parts, ("x", "y", "xy"))]
+    own, *rest = reduce_two(keep, rc, *parts)
+    return add(own, *[from_z(p, 3 - k) for k, p in enumerate(rest)])
 
 def exchange_in_y(idx, a):
     return move(lax.dynamic_slice_in_dim(a, 2 * (1 - idx[2]), 2, 0), "y")
@@ -789,8 +817,8 @@
     di, ci = lax.axis_index("dp"), lax.axis_index("ctx")
     idx = jnp.stack([di // 2, di % 2, ci // 2, ci % 2]).astype(jnp.int32)
     pz = lambda r, n: jnp.zeros((r, n), BF)
-    c1 = jnp.concatenate([w_query, pz(240, 8), w_key, w_value, pz(240, 48), w_out, pz(240, 8)], axis=1)
-    gain_row = jnp.pad(norm_gains.reshape(1, 60), ((0, 15), (0, 324)))
+    c1 = jnp.concatenate([w_query, pz(240, 8), w_key, w_value, pz(240, 48)], axis=1)
+    gain_row = jnp.pad(norm_gains.reshape(1, 60), ((0, 15), (0, 196)))
     c1 = jnp.concatenate([c1, gain_row], axis=0)
     def pack(lo, hi):
         s = hi - lo
@@ -799,61 +827,57 @@
         d = jnp.pad(d, ((0, 0), (0, 8)))
         d = jnp.concatenate([d[128 * t:128 * t + 128] for t in range(2 * s // 128)], axis=1)
         return jnp.concatenate([gu, d], axis=0)
+    wo = jnp.pad(w_out, ((0, 0), (0, 8)))
+    wo = jnp.concatenate([wo[80 * t:80 * t + 80] for t in range(3)], axis=1)
     ht, ct = jnp.swapaxes(hidden_in, 1, 2), jnp.swapaxes(cotangent, 1, 2)
     xr = exchange_in_y(idx, ht)
-    g1 = gather_z(c1, CUT)
-    ga = gather_z(after(pack(*SPLIT[0]), g1[0]), 240)
-    gb = gather_z(after(pack(*SPLIT[1]), ga[0]), 240)
+    g1 = gather_z(c1)
+    ga = gather_z(jnp.concatenate([pack(*SPLIT[0]), wo], axis=0))
+    p1 = gather_rest(g1)
+    xr = after(xr, p1[1])
     xg = exchange_in_c(idx, ht, xr)
     x = tok_in(idx, ht, xr, xg)
-    p1 = gather_core(gather_second(gather_first(g1)))
-    pa = gather_core(gather_second(gather_first(ga)))
-    pb = gather_core(gather_second(gather_first(gb)))
+    pa = gather_rest(ga)
+    pb = gather_flat(pack(*SPLIT[1]))
     cr = exchange_in_y(idx, ct)
     cg = exchange_in_c(idx, ct, cr)
     cos, sin = rope_tables(jnp.arange(T).astype(F32), HD)
     cos, sin = jnp.tile(cos, (1, 2)), jnp.tile(sin, (1, 2))
-    n1, q, k, v, w, wo, gains = qkv_fwd(idx, x, cos, sin, *p1)
+    n1, q, k, v, w, gains = qkv_fwd(idx, x, cos, sin, p1)
     o1, lse1 = attn_fwd(q, k, v, 0, 3)
     o2, lse2 = attn_fwd(q, k, v, 3, 2)
-    att, mid, n2 = out_fwd(idx, o1, o2, x, gains, wo)
-    acc, ha, wda = ffn_fwd(idx, n2, mid, *pa, False)
-    out, hb, wdb = ffn_fwd(idx, n2, acc, *pb, True)
+    att, mid, n2, wo = out_fwd(idx, o1, o2, x, gains, pa)
+    acc, ha, wda = ffn_fwd(idx, n2, mid, pa, "z", False)
+    out, hb, wdb = ffn_fwd(idx, n2, acc, pb, "xy", True)
     cb = tok_in(idx, ct, cr, cg)
     hr = move(out[1], "c")
     hb_ = move(jnp.stack([out[0, 1], hr[1]]), "y")
     hidden_out = tok_out(idx, out, hr, hb_)
-    dn2, ka, sa = ffn_bwd(idx, cb, n2, ha, wda, jnp.zeros((T, DP), F32), pa[0])
-    ra_c = reduce_core(sa)
-    dn2, kb, sb = ffn_bwd(idx, cb, n2, hb, wdb, dn2, pb[0])
-    rb_c = reduce_core(sb)
-    dmid, do, dg2, ko, so = out_bwd(idx, dn2, cb, mid, gains, wo, att)
-    ro_c = reduce_core(so)
-    b1 = attn_bwd(q, k, v, do, lse1, cos, sin, 0, 3)
-    b2 = attn_bwd(q, k, v, do, lse2, cos, sin, 3, 2)
-    hg, kq, sq = qkv_bwd(idx, b1, b2, x, gains, n1, dmid, w, dg2)
-    rq_c = reduce_core(sq)
+    dn2, ka, sa = ffn_bwd(idx, cb, n2, ha, wda, None, pa, "z", 368)
+    dn2, kb, sb = ffn_bwd(idx, cb, n2, hb, wdb, dn2, pb, "xy", 496)
+    dmid, do, dg2, kb, sb, delta = out_bwd(idx, dn2, cb, mid, gains, wo, att, kb, sb)
+    lse = jnp.concatenate([lse1, lse2], axis=0)
+    b1 = attn_bwd(q, k, v, do, lse, delta, cos, sin, 0, 1)
+    b2 = attn_bwd(q, k, v, do, lse, delta, cos, sin, 1, 2)
+    b3 = attn_bwd(q, k, v, do, lse, delta, cos, sin, 3, 2)
+    hg, dh, dg1 = qkv_dx(idx, b1, b2, b3, x, gains, dmid, w)
+    kq, sq = qkv_dw(idx, n1, dh, dg1, dg2)
     gr = move(hg[1], "c")
     gb_ = move(jnp.stack([hg[0, 1], gr[1]]), "y")
     hidden_grad = tok_out(idx, hg, gr, gb_)
     factor = 1.0 / math.sqrt(lax.axis_size("dp") * hidden_in.shape[0] * T)
-    def finish(keep, rc, cut):
-        r1 = reduce_first(keep, rc, cut)
-        r2 = reduce_second(keep, rc, r1, cut)
-        own, others = reduce_z(keep, rc, r1, r2)
-        return add(own, *others) * factor
-    ra = finish(ka, ra_c, 240)
-    rb = finish(kb, rb_c, 240)
-    ro = finish(ko, ro_c, CUT)
-    rq = finish(kq, rq_c, CUT)
+    ra = reduce_pieces(ka, sa) * factor
+    rb = reduce_pieces(kb, sb) * factor
+    rq = reduce_pieces(kq, sq) * factor
+    ro = jnp.concatenate([rb[368:496, :120], rb[368:480, 128:248]], axis=0)
     gate, up, down = [], [], []
     for (lo, hi), r in zip(SPLIT, (ra, rb)):
         s = hi - lo
         gate.append(r[:240, :s]); up.append(r[:240, s:])
-        d = jnp.concatenate([r[240:, 128 * t:128 * t + 128] for t in range(2 * s // 128)], axis=0)[:, :120]
+        d = jnp.concatenate([r[240:368, 128 * t:128 * t + 128] for t in range(2 * s // 128)], axis=0)[:, :120]
         down.append((d[:s], d[s:]))
     return (jnp.swapaxes(hidden_out, 1, 2), jnp.swapaxes(hidden_grad, 1, 2), rq[240, :60], rq[:240, :120], rq[:240, 128:168],
-            rq[:240, 168:208], ro[:, :120], jnp.concatenate(gate, axis=1), jnp.concatenate(up, axis=1),
+            rq[:240, 168:208], ro, jnp.concatenate(gate, axis=1), jnp.concatenate(up, axis=1),
             jnp.concatenate([down[0][0], down[1][0], down[0][1], down[1][1]], axis=0))
 
 

time: 598 us -> 590 us (0.987)
  waiting for transfers between devices: 184 us -> 203 us
  other arithmetic: 34.4 us -> 18.5 us
  starting transfers between devices: 74.1 us -> 59.2 us
  Pallas kernels: 259 us -> 268 us
  local copies, waits for them, and re-layouts: 37 us -> 30.6 us
    ppermute x0 -> x6, waiting for transfers between devices: none -> 34.1 us  [move(): lax.ppermute(a, ('dp', 'ctx'), [(i, (i // n ^ 1) * n + (i % n ^ 2)) for i...]
    ppermute x21 -> x18, waiting for transfers between devices: 59.9 us -> 43.7 us  [from_z(): lax.ppermute(a, 'dp', [((z + k) % 4 * 2 + x, z * 2 + x) for z in range(4)...]
    convert_element_type x16 -> x0, other arithmetic: 14.1 us -> none  [the longest x4 5.18 us: reduce_z(): low = own.astype(BF)]
    ppermute x52 -> x35, starting transfers between devices: 36.2 us -> 22.8 us  [swap(): return lax.ppermute(a, axis, [(i, i ^ bit) for i in range(n)])]
    pallas_call x9 -> x17, Pallas kernels: 204 us -> 212 us  [the longest x2 59.5 us: ffn_bwd(): pl.pallas_call(functools.partial(ffn_bwd_kernel, S, kind, dn2in is None),...]
    ppermute x21 -> x18, starting transfers between devices: 37.9 us -> 30.6 us  [from_z(): lax.ppermute(a, 'dp', [((z + k) % 4 * 2 + x, z * 2 + x) for z in range(4)...]
    another operation x25 -> x0, local copies, waits for them, and re-layouts: 6.53 us -> none  [the longest x24 6.52 us: gather_z(): return (jnp.stack([p[:cut] for p in ps]), jnp.stack([p[cut:] for p in ps]))]
    ppermute x52 -> x35, waiting for transfers between devices: 124 us -> 125 us  [swap(): return lax.ppermute(a, axis, [(i, i ^ bit) for i in range(n)])]
  transfers between devices with their start and end apart: 73 -> 59, of which waited for: 33 -> 20; matrix products, arithmetic and copies ran while one was open for 10% -> 6% of each run, Pallas kernels for 33% -> 30%
where the time goes in v2:
time: 590 us; the launch traced here: 581 us
  Pallas kernels  268 us (45%)
  waiting for transfers between devices  203 us (34%)
  starting transfers between devices  59.2 us (10%)
  local copies, waits for them, and re-layouts  30.6 us (5%)
  other arithmetic  18.5 us (3%)
    ppermute x35, waiting for transfers between devices, swap(): return lax.ppermute(a, axis, [(i, i ^ bit) for i in range(n)])  125 us
    pallas_call x2, Pallas kernels, ffn_bwd(): pl.pallas_call(functools.partial(ffn_bwd_kernel, S, kind, dn2in is None),...  59.5 us
    ppermute x18, waiting for transfers between devices, from_z(): lax.ppermute(a, 'dp', [((z + k) % 4 * 2 + x, z * 2 + x) for z in range(4)...  43.7 us
    pallas_call x2, Pallas kernels, ffn_fwd(): pl.pallas_call(functools.partial(ffn_fwd_kernel, S, kind, last), grid_spe...  41.6 us
    pallas_call x3, Pallas kernels, attn_bwd(): pl.pallas_call(attn_bwd_kernel, grid=(ng,), in_specs=[qs, ks, ks, qs] + [...  37.4 us
    ppermute x6, waiting for transfers between devices, move(): lax.ppermute(a, ('dp', 'ctx'), [(i, (i // n ^ 1) * n + (i % n ^ 2)) for i...  34.1 us
    ppermute x18, starting transfers between devices, from_z(): lax.ppermute(a, 'dp', [((z + k) % 4 * 2 + x, z * 2 + x) for z in range(4)...  30.6 us
    pallas_call x2, Pallas kernels, attn_fwd(): pl.pallas_call(attn_fwd_kernel, grid=(ng,), in_specs=[qs, ks, ks], out_sp...  22.8 us
  transfers between devices with their start and end apart: 59, of which 20 were waited for; matrix products, arithmetic and copies ran while one was open for 6% of the time, Pallas kernels for 30%

profile of v2, /device:TPU:0, one launch (start us, length us, event | category | flops | bytes accessed | tf_op | source)
XLA Modules:
  0.0 580.8 jit_solution(18217800801522214308)
XLA Ops:
  32.9 17.4 %collective-permute-done.4.refs_1_ = bf16[4,256,256]{2,1,0:T(8,128)(2,1)} collective-permute-done((bf16[4,256,256]{2,1,0:T(8,128)(2,1)}, bf16[4,256,256]{2,1,0:T(8,128)(2,1)}, u32[]{:S(2)}, u32[]{:S(2)}) %collective-permute-start.4) | collective-permute-done | bytes 524320 | tf_op jit(solution)/shard_map/ppermute | solution.py:766
  77.9 7.6 %collective-permute-done.7.refs_3_ = bf16[4,256,256]{2,1,0:T(8,128)(2,1)} collective-permute-done((bf16[4,256,256]{2,1,0:T(8,128)(2,1)}, bf16[4,256,256]{2,1,0:T(8,128)(2,1)}, u32[]{:S(2)}, u32[]{:S(2)}) %collective-permute-start.7) | collective-permute-done | bytes 524320 | tf_op jit(solution)/shard_map/ppermute | solution.py:771
  101.6 14.2 %qkv_fwd.1 = (bf16[1024,1024]{1,0:T(8,128)(2,1)}, bf16[15,1024,128]{2,1,0:T(8,128)(2,1)}, bf16[5,1024,128]{2,1,0:T(8,128)(2,1)}, bf16[5,1024,128]{2,1,0:T(8,128)...) custom-call(s32[4]{0:T(128)} %pad_add_fusion.idx, bf16[1024,1024]{1,0:T(8,128)(2,1)} %tok_in.2.x, ...), custom_call_target="tpu_custom_call" | custom-call | flops 14400000000 | bytes 32000000 | tf_op jit(solution)/shard_map/qkv_fwd/pallas_call | solution.py:641
  115.9 13.3 %attn_fwd.2 = (bf16[9,1024,128]{2,1,0:T(8,128)(2,1)}, f32[9,1,1024]{2,1,0:T(1,128)}) custom-call(bf16[15,1024,128]{2,1,0:T(8,128)(2,1)} %get-tuple-element.79.q, bf16[5,1024,128]{2,1,0:T(8,128)(2,1)} %get-tuple-element.80.k, bf16[5,1024,128]{2,1,0:T(8,128)(2,1)} %get-tuple-element.81.v), custom_call_target="tpu_custom_call" | custom-call | flops 16199999488 | bytes 36000000 | tf_op jit(solution)/shard_map/attn_fwd/pallas_call | solution.py:554
  129.2 14.5 %collective-permute-done.26.refs_2_.refs_3_ = bf16[4,368,256]{2,1,0:T(8,128)(2,1)} collective-permute-done((bf16[4,368,256]{2,1,0:T(8,128)(2,1)S(1)}, bf16[4,368,256]{2,1,0:T(8,128)(2,1)}, u32[]{:S(2)}, u32[]{:S(2)}) %collective-permute-start.26) | collective-permute-done | bytes 753696 | tf_op jit(solution)/shard_map/ppermute | solution.py:777
  145.4 15.8 %collective-permute-done.17.refs_3_ = bf16[4,448,384]{2,1,0:T(8,128)(2,1)} collective-permute-done((bf16[4,448,384]{2,1,0:T(8,128)(2,1)S(1)}, bf16[4,448,384]{2,1,0:T(8,128)(2,1)}, u32[]{:S(2)}, u32[]{:S(2)}) %collective-permute-start.17) | collective-permute-done | bytes 1376288 | tf_op jit(solution)/shard_map/ppermute | solution.py:771
  161.7 9.5 %attn_fwd.3 = (bf16[6,1024,128]{2,1,0:T(8,128)(2,1)}, f32[6,1,1024]{2,1,0:T(1,128)}) custom-call(bf16[15,1024,128]{2,1,0:T(8,128)(2,1)} %get-tuple-element.79.q, bf16[5,1024,128]{2,1,0:T(8,128)(2,1)} %get-tuple-element.80.k, bf16[5,1024,128]{2,1,0:T(8,128)(2,1)} %get-tuple-element.81.v), custom_call_target="tpu_custom_call" | custom-call | flops 10800000000 | bytes 24000000 | tf_op jit(solution)/shard_map/attn_fwd/pallas_call | solution.py:554
  177.2 11.0 %out_fwd.1 = (bf16[1024,1024]{1,0:T(8,128)(2,1)}, f32[1024,1024]{1,0:T(8,128)}, bf16[1024,1024]{1,0:T(8,128)(2,1)}, bf16[1024,1024]{1,0:T(8,128)(2,1)}) custom-call(s32[4]{0:T(128)} %pad_add_fusion.idx, bf16[9,1024,128]{2,1,0:T(8,128)(2,1)} %get-tuple-element.82.o1, bf16[6,1024,128]{2,1,0:T(8,128)(2,1)} %get-tuple-element.83.o2, ...), custom_call_target="tpu_custom_call" | custom-call | flops 8099999744 | bytes 18000000 | tf_op jit(solution)/shard_map/out_fwd/pallas_call | solution.py:666
  188.2 23.4 %ffn_fwd.2 = (f32[1024,1024]{1,0:T(8,128)}, bf16[2,1024,1536]{2,1,0:T(8,128)(2,1)}, bf16[2,768,1024]{2,1,0:T(8,128)(2,1)}) custom-call(s32[4]{0:T(128)} %pad_add_fusion.idx, bf16[1024,1024]{1,0:T(8,128)(2,1)} %get-tuple-element.85.n2.n2h, f32[1024,1024]{1,0:T(8,128)} %get-tuple-element.86.mid, bf16[4,448,384]{2,1,0:T(8,128)(2,1)} %copy-done.1, ...), custom_call_target="tpu_custom_call" | custom-call | flops 17999998976 | bytes 40000000 | tf_op jit(solution)/shard_map/ffn_fwd/pallas_call | solution.py:418
  211.6 33.3 %ffn_bwd.2 = (f32[1024,1024]{1,0:T(8,128)}, bf16[2,2,4,368,384]{4,3,2,1,0:T(8,128)(2,1)}, bf16[2,2,4,368,384]{4,3,2,1,0:T(8,128)(2,1)}) custom-call(s32[4]{0:T(128)} %pad_add_fusion.idx, bf16[1024,1024]{1,0:T(8,128)(2,1)} %tok_in.3.cb, bf16[2,1024,1536]{2,1,0:T(8,128)(2,1)} %get-tuple-element.91.h, bf16[2,768,1024]{2,1,0:T(8,128)(2,1)} %get-tuple-element.92.wd, ...), custom_call_target="tpu_custom_call" | custom-call | flops 29699999744 | bytes 66000000 | tf_op jit(solution)/shard_map/ffn_bwd/pallas_call | solution.py:504
  246.3 18.2 %ffn_fwd.3 = (bf16[2,2,960,256]{3,2,1,0:T(8,128)(2,1)}, bf16[2,1024,1024]{2,1,0:T(8,128)(2,1)}, bf16[2,512,1024]{2,1,0:T(8,128)(2,1)}) custom-call(s32[4]{0:T(128)} %pad_add_fusion.idx, bf16[1024,1024]{1,0:T(8,128)(2,1)} %get-tuple-element.85.n2.n2h, f32[1024,1024]{1,0:T(8,128)} %get-tuple-element.87.mid, bf16[4,368,256]{2,1,0:T(8,128)(2,1)} %copy-done.9, ...), custom_call_target="tpu_custom_call" | custom-call | flops 17999998976 | bytes 40000000 | tf_op jit(solution)/shard_map/ffn_fwd/pallas_call | solution.py:418
  264.5 26.3 %ffn_bwd.3 = (f32[1024,1024]{1,0:T(8,128)}, bf16[2,2,4,496,256]{4,3,2,1,0:T(8,128)(2,1)}, bf16[2,2,4,496,256]{4,3,2,1,0:T(8,128)(2,1)}) custom-call(s32[4]{0:T(128)} %pad_add_fusion.idx, bf16[1024,1024]{1,0:T(8,128)(2,1)} %tok_in.3.cb, bf16[2,1024,1024]{2,1,0:T(8,128)(2,1)} %get-tuple-element.89.h, bf16[2,512,1024]{2,1,0:T(8,128)(2,1)} %get-tuple-element.90.wd, ...), custom_call_target="tpu_custom_call" | custom-call | flops 29699999744 | bytes 66000000 | tf_op jit(solution)/shard_map/ffn_bwd/pallas_call | solution.py:504
  290.8 16.8 %out_bwd.1 = (f32[1024,1024]{1,0:T(8,128)}, bf16[15,1024,128]{2,1,0:T(8,128)(2,1)}, f32[1,1024]{1,0:T(1,128)}, bf16[2,2,4,496,256]{4,3,2,1,0:T(8,128)(2,1)}, bf1...) custom-call(s32[4]{0:T(128)} %pad_add_fusion.idx, ...), custom_call_target="tpu_custom_call", output_to_operand_aliasing={{3}: (7, {}), {4}: (8, {})} | custom-call | flops 14400000000 | bytes 32000000 | tf_op jit(solution)/shard_map/out_bwd/pallas_call | solution.py:708
  307.6 14.4 %attn_bwd.5 = (bf16[6,1024,128]{2,1,0:T(8,128)(2,1)}, bf16[2,1024,128]{2,1,0:T(8,128)(2,1)}, bf16[2,1024,128]{2,1,0:T(8,128)(2,1)}) custom-call(bf16[15,1024,128]{2,1,0:T(8,128)(2,1)} %get-tuple-element.79.q, bf16[5,1024,128]{2,1,0:T(8,128)(2,1)} %get-tuple-element.80.k, bf16[5,1024,128]{2,1,0:T(8,128)(2,1)} %get-tuple-element.81.v, ...), custom_call_target="tpu_custom_call" | custom-call | flops 16199999488 | bytes 36000000 | tf_op jit(solution)/shard_map/attn_bwd/pallas_call | solution.py:588
  322.0 14.5 %attn_bwd.4 = (bf16[6,1024,128]{2,1,0:T(8,128)(2,1)}, bf16[2,1024,128]{2,1,0:T(8,128)(2,1)}, bf16[2,1024,128]{2,1,0:T(8,128)(2,1)}) custom-call(bf16[15,1024,128]{2,1,0:T(8,128)(2,1)} %get-tuple-element.79.q, bf16[5,1024,128]{2,1,0:T(8,128)(2,1)} %get-tuple-element.80.k, bf16[5,1024,128]{2,1,0:T(8,128)(2,1)} %get-tuple-element.81.v, ...), custom_call_target="tpu_custom_call" | custom-call | flops 16199999488 | bytes 36000000 | tf_op jit(solution)/shard_map/attn_bwd/pallas_call | solution.py:588
  336.6 8.4 %attn_bwd.3 = (bf16[3,1024,128]{2,1,0:T(8,128)(2,1)}, bf16[1,1024,128]{2,1,0:T(8,128)(2,1)}, bf16[1,1024,128]{2,1,0:T(8,128)(2,1)}) custom-call(bf16[15,1024,128]{2,1,0:T(8,128)(2,1)} %get-tuple-element.79.q, bf16[5,1024,128]{2,1,0:T(8,128)(2,1)} %get-tuple-element.80.k, bf16[5,1024,128]{2,1,0:T(8,128)(2,1)} %get-tuple-element.81.v, ...), custom_call_target="tpu_custom_call" | custom-call | flops 8099999744 | bytes 18000000 | tf_op jit(solution)/shard_map/attn_bwd/pallas_call | solution.py:588
  345.5 11.8 %qkv_dx.1 = (bf16[2,2,960,256]{3,2,1,0:T(8,128)(2,1)}, bf16[1024,1664]{1,0:T(8,128)(2,1)}, f32[1,1024]{1,0:T(1,128)}) custom-call(s32[4]{0:T(128)} %pad_add_fusion.idx, bf16[3,1024,128]{2,1,0:T(8,128)(2,1)} %get-tuple-element.103.dq1, bf16[1,1024,128]{2,1,0:T(8,128)(2,1)} %get-tuple-element.104.dk1, bf16[1,1024,128]{2,1,0:T(8,128)(2,1)} %get-tuple-element.105.dv1, ...), custom_call_target="tpu_custom_call" | custom-call | flops 8099999744 | bytes 18000000 | tf_op jit(solution)/shard_map/qkv_dx/pallas_call | solution.py:727
  357.3 10.4 %qkv_dw.1 = (bf16[2,2,4,256,256]{4,3,2,1,0:T(8,128)(2,1)}, bf16[2,2,4,256,256]{4,3,2,1,0:T(8,128)(2,1)}) custom-call(s32[4]{0:T(128)} %pad_add_fusion.idx, bf16[1024,1024]{1,0:T(8,128)(2,1)} %get-tuple-element.115.n1, bf16[1024,1664]{1,0:T(8,128)(2,1)} %get-tuple-element.116.dh, f32[1,1024]{1,0:T(1,128)} %get-tuple-element.117.dg1, ...), custom_call_target="tpu_custom_call" | custom-call | flops 8099999744 | bytes 18000000 | tf_op jit(solution)/shard_map/qkv_dw/pallas_call | solution.py:751
  391.3 8.4 %collective-permute-done.37.b = bf16[2,960,256]{2,1,0:T(8,128)(2,1)} collective-permute-done((bf16[2,960,256]{2,1,0:T(8,128)(2,1)}, bf16[2,960,256]{2,1,0:T(8,128)(2,1)}, u32[]{:S(2)}, u32[]{:S(2)}) %collective-permute-start.37) | collective-permute-done | bytes 983072 | tf_op jit(solution)/shard_map/ppermute | solution.py:766
  400.2 20.5 %collective-permute-done.33.b = bf16[2,960,256]{2,1,0:T(8,128)(2,1)} collective-permute-done((bf16[2,960,256]{2,1,0:T(8,128)(2,1)}, bf16[2,960,256]{2,1,0:T(8,128)(2,1)}, u32[]{:S(2)}, u32[]{:S(2)}) %collective-permute-start.33) | collective-permute-done | bytes 983072 | tf_op jit(solution)/shard_map/ppermute | solution.py:766
  422.8 31.0 %collective-permute-done.40.b = bf16[4,256,256]{2,1,0:T(8,128)(2,1)} collective-permute-done((bf16[4,256,256]{2,1,0:T(8,128)(2,1)}, bf16[4,256,256]{2,1,0:T(8,128)(2,1)}, u32[]{:S(2)}, u32[]{:S(2)}) %collective-permute-start.40) | collective-permute-done | bytes 524320 | tf_op jit(solution)/shard_map/ppermute | solution.py:766
  474.5 11.4 %collective-permute-done.47.b = bf16[4,496,256]{2,1,0:T(8,128)(2,1)S(1)} collective-permute-done((bf16[4,496,256]{2,1,0:T(8,128)(2,1)}, bf16[4,496,256]{2,1,0:T(8,128)(2,1)S(1)}, u32[]{:S(2)}, u32[]{:S(2)}) %collective-permute-start.47) | collective-permute-done | bytes 1015840 | tf_op jit(solution)/shard_map/ppermute | solution.py:766
  527.4 21.6 %collective-permute-done.54.b = bf16[4,368,384]{2,1,0:T(8,128)(2,1)S(1)} collective-permute-done((bf16[4,368,384]{2,1,0:T(8,128)(2,1)}, bf16[4,368,384]{2,1,0:T(8,128)(2,1)S(1)}, u32[]{:S(2)}, u32[]{:S(2)}) %collective-permute-start.54) | collective-permute-done | bytes 1130528 | tf_op jit(solution)/shard_map/ppermute | solution.py:766
  567.2 9.1 %collective-permute-done.57 = bf16[368,384]{1,0:T(8,128)(2,1)S(1)} collective-permute-done((bf16[368,384]{1,0:T(8,128)(2,1)}, bf16[368,384]{1,0:T(8,128)(2,1)S(1)}, u32[]{:S(2)}, u32[]{:S(2)}) %collective-permute-start.57) | collective-permute-done | bytes 282656 | tf_op jit(solution)/shard_map/ppermute | solution.py:777
  (266 shorter events, 196.4 us)
Async XLA Ops:
  12.1 39.6 %collective-permute-start = (bf16[2,960,256]{2,1,0:T(8,128)(2,1)S(1)}, bf16[2,960,256]{2,1,0:T(8,128)(2,1)}, u32[]{:S(2)}, u32[]{:S(2)}) collective-permute-start(bf16[2,960,256]{2,1,0:T(8,128)(2,1)S(1)} %dynamic-slice_bitcast_fusion.1), channel_id=1, source_target_pairs={{0,2},{1,3},{2,0},{3,1},{4,6},{5,7},{6,4},{7,5},{8,10},{9,11},{10,... | collective-permute-start | bytes 2949128 | tf_op jit(solution)/shard_map/ppermute | solution.py:766
  18.3 44.0 %collective-permute-start.12 = (bf16[448,384]{1,0:T(8,128)(2,1)}, bf16[448,384]{1,0:T(8,128)(2,1)}, u32[]{:S(2)}, u32[]{:S(2)}) collective-permute-start(bf16[448,384]{1,0:T(8,128)(2,1)} %maximum_maximum_fusion), channel_id=1, source_target_pairs={{8,0},{12,4},{16,8},{20,12},{24,16},{28,20},{0,24},{4,28},{9,1},{1... | collective-permute-start | bytes 1032200 | tf_op jit(solution)/shard_map/ppermute | solution.py:777
  25.0 40.4 %collective-permute-start.13 = (bf16[448,384]{1,0:T(8,128)(2,1)}, bf16[448,384]{1,0:T(8,128)(2,1)}, u32[]{:S(2)}, u32[]{:S(2)}) collective-permute-start(bf16[448,384]{1,0:T(8,128)(2,1)} %maximum_maximum_fusion), channel_id=1, source_target_pairs={{16,0},{20,4},{24,8},{28,12},{0,16},{4,20},{8,24},{12,28},{17,1},{... | collective-permute-start | bytes 1032200 | tf_op jit(solution)/shard_map/ppermute | solution.py:777
  51.7 37.1 %collective-permute-start.34 = (bf16[2,960,256]{2,1,0:T(8,128)(2,1)}, bf16[2,960,256]{2,1,0:T(8,128)(2,1)}, u32[]{:S(2)}, u32[]{:S(2)}) collective-permute-start(bf16[2,960,256]{2,1,0:T(8,128)(2,1)} %dynamic-slice_bitcast_fusion), channel_id=1, source_target_pairs={{0,2},{1,3},{2,0},{3,1},{4,6},{5,7},{6,4},{7,5},{8,10},{9,11},{10,... | collective-permute-start | bytes 2949128 | tf_op jit(solution)/shard_map/ppermute | solution.py:766
  57.3 32.7 %collective-permute-start.5 = (bf16[2,960,256]{2,1,0:T(8,128)(2,1)}, bf16[2,960,256]{2,1,0:T(8,128)(2,1)}, u32[]{:S(2)}, u32[]{:S(2)}) collective-permute-start(bf16[2,960,256]{2,1,0:T(8,128)(2,1)} %pad_maximum_fusion.1), channel_id=1, source_target_pairs={{0,1},{1,0},{2,3},{3,2},{4,5},{5,4},{6,7},{7,6},{8,9},{9,8},{10,11... | collective-permute-start | bytes 2949128 | tf_op jit(solution)/shard_map/ppermute | solution.py:766
  97.9 45.7 %collective-permute-start.26 = (bf16[4,368,256]{2,1,0:T(8,128)(2,1)S(1)}, bf16[4,368,256]{2,1,0:T(8,128)(2,1)}, u32[]{:S(2)}, u32[]{:S(2)}) collective-permute-start(bf16[4,368,256]{2,1,0:T(8,128)(2,1)S(1)} %pad_maximum_fusion.5.refs_0_.refs_1_), channel_id=1, source_target_pairs={{16,0},{20,4},{24,8},{28,12},{0,16},{4,20},{8,24},{12,28},{17,1},{... | collective-permute-start | bytes 2261000 | tf_op jit(solution)/shard_map/ppermute | solution.py:777
  98.1 46.7 %collective-permute-start.15 = (bf16[4,448,384]{2,1,0:T(8,128)(2,1)S(1)}, bf16[4,448,384]{2,1,0:T(8,128)(2,1)}, u32[]{:S(2)}, u32[]{:S(2)}) collective-permute-start(bf16[4,448,384]{2,1,0:T(8,128)(2,1)S(1)} %pad_maximum_fusion.refs_0_), channel_id=1, source_target_pairs={{0,2},{1,3},{2,0},{3,1},{4,6},{5,7},{6,4},{7,5},{8,10},{9,11},{10,... | collective-permute-start | bytes 4128776 | tf_op jit(solution)/shard_map/ppermute | solution.py:766
  99.8 45.1 %collective-permute-start.16 = (bf16[4,448,384]{2,1,0:T(8,128)(2,1)S(1)}, bf16[4,448,384]{2,1,0:T(8,128)(2,1)}, u32[]{:S(2)}, u32[]{:S(2)}) collective-permute-start(bf16[4,448,384]{2,1,0:T(8,128)(2,1)S(1)} %pad_maximum_fusion.refs_0_), channel_id=1, source_target_pairs={{0,4},{4,0},{8,12},{12,8},{16,20},{20,16},{24,28},{28,24},{1,5},{5... | collective-permute-start | bytes 4128776 | tf_op jit(solution)/shard_map/ppermute | solution.py:766
  100.3 60.9 %collective-permute-start.17 = (bf16[4,448,384]{2,1,0:T(8,128)(2,1)S(1)}, bf16[4,448,384]{2,1,0:T(8,128)(2,1)}, u32[]{:S(2)}, u32[]{:S(2)}) collective-permute-start(bf16[4,448,384]{2,1,0:T(8,128)(2,1)S(1)} %pad_maximum_fusion.refs_0_), channel_id=1, source_target_pairs={{0,6},{1,7},{2,4},{3,5},{4,2},{5,3},{6,0},{7,1},{8,14},{9,15},{10,... | collective-permute-start | bytes 4128776 | tf_op jit(solution)/shard_map/ppermute | solution.py:771
  115.8 45.4 %collective-permute-start.35 = (bf16[2,960,256]{2,1,0:T(8,128)(2,1)S(1)}, bf16[2,960,256]{2,1,0:T(8,128)(2,1)}, u32[]{:S(2)}, u32[]{:S(2)}) collective-permute-start(bf16[2,960,256]{2,1,0:T(8,128)(2,1)S(1)} %pad_maximum_fusion.3), channel_id=1, source_target_pairs={{0,1},{1,0},{2,3},{3,2},{4,5},{5,4},{6,7},{7,6},{8,9},{9,8},{10,11... | collective-permute-start | bytes 2949128 | tf_op jit(solution)/shard_map/ppermute | solution.py:766
  176.1 68.8 %collective-permute-start.28 = (bf16[4,368,256]{2,1,0:T(8,128)(2,1)S(1)}, bf16[4,368,256]{2,1,0:T(8,128)(2,1)S(1)}, u32[]{:S(2)}, u32[]{:S(2)}) collective-permute-start(bf16[4,368,256]{2,1,0:T(8,128)(2,1)S(1)} %pad_maximum_fusion.5.refs_0_.refs_1_), channel_id=1, source_target_pairs={{0,1},{1,0},{2,3},{3,2},{4,5},{5,4},{6,7},{7,6},{8,9},{9,8},{10,11... | collective-permute-start | bytes 2261000 | tf_op jit(solution)/shard_map/ppermute | solution.py:766
  176.2 68.7 %collective-permute-start.29 = (bf16[4,368,256]{2,1,0:T(8,128)(2,1)}, bf16[4,368,256]{2,1,0:T(8,128)(2,1)S(1)}, u32[]{:S(2)}, u32[]{:S(2)}) collective-permute-start(bf16[4,368,256]{2,1,0:T(8,128)(2,1)} %collective-permute-done.25.refs_1_.refs_2_), channel_id=1, source_target_pairs={{0,1},{1,0},{2,3},{3,2},{4,5},{5,4},{6,7},{7,6},{8,9},{9,8},{10,11... | collective-permute-start | bytes 2261000 | tf_op jit(solution)/shard_map/ppermute | solution.py:766
  176.7 68.3 %collective-permute-start.30 = (bf16[4,368,256]{2,1,0:T(8,128)(2,1)}, bf16[4,368,256]{2,1,0:T(8,128)(2,1)S(1)}, u32[]{:S(2)}, u32[]{:S(2)}) collective-permute-start(bf16[4,368,256]{2,1,0:T(8,128)(2,1)} %collective-permute-done.26.refs_2_.refs_3_), channel_id=1, source_target_pairs={{0,1},{1,0},{2,3},{3,2},{4,5},{5,4},{6,7},{7,6},{8,9},{9,8},{10,11... | collective-permute-start | bytes 2261000 | tf_op jit(solution)/shard_map/ppermute | solution.py:766
  176.8 68.2 %collective-permute-start.31 = (bf16[4,368,256]{2,1,0:T(8,128)(2,1)}, bf16[4,368,256]{2,1,0:T(8,128)(2,1)}, u32[]{:S(2)}, u32[]{:S(2)}) collective-permute-start(bf16[4,368,256]{2,1,0:T(8,128)(2,1)} %collective-permute-done.27.refs_3_.refs_4_), channel_id=1, source_target_pairs={{0,1},{1,0},{2,3},{3,2},{4,5},{5,4},{6,7},{7,6},{8,9},{9,8},{10,11... | collective-permute-start | bytes 2261000 | tf_op jit(solution)/shard_map/ppermute | solution.py:766
  336.6 47.4 %collective-permute-start.45 = (bf16[2,2,4,496,256]{4,3,2,1,0:T(8,128)(2,1)}, bf16[2,2,4,496,256]{4,3,2,1,0:T(8,128)(2,1)S(1)}, u32[]{:S(2)}, u32[]{:S(2)}) collective-permute-start(bf16[2,2,4,496,256]{4,3,2,1,0:T(8,128)(2,1)} %get-tuple-element.129), channel_id=1, source_target_pairs={{0,1},{1,0},{2,3},{3,2},{4,5},{5,4},{6,7},{7,6},{8,9},{9,8},{10,11... | collective-permute-start | bytes 12189704 | tf_op jit(solution)/shard_map/ppermute | solution.py:766
  345.1 148.7 %collective-permute-start.52 = (bf16[2,2,4,368,384]{4,3,2,1,0:T(8,128)(2,1)}, bf16[2,2,4,368,384]{4,3,2,1,0:T(8,128)(2,1)}, u32[]{:S(2)}, u32[]{:S(2)}) collective-permute-start(bf16[2,2,4,368,384]{4,3,2,1,0:T(8,128)(2,1)} %get-tuple-element.138), channel_id=1, source_target_pairs={{0,1},{1,0},{2,3},{3,2},{4,5},{5,4},{6,7},{7,6},{8,9},{9,8},{10,11... | collective-permute-start | bytes 13565960 | tf_op jit(solution)/shard_map/ppermute | solution.py:766
  377.8 43.0 %collective-permute-start.33 = (bf16[2,960,256]{2,1,0:T(8,128)(2,1)}, bf16[2,960,256]{2,1,0:T(8,128)(2,1)}, u32[]{:S(2)}, u32[]{:S(2)}) collective-permute-start(bf16[2,960,256]{2,1,0:T(8,128)(2,1)} %pad_maximum_fusion.2), channel_id=1, source_target_pairs={{0,2},{1,3},{2,0},{3,1},{4,6},{5,7},{6,4},{7,5},{8,10},{9,11},{10,... | collective-permute-start | bytes 2949128 | tf_op jit(solution)/shard_map/ppermute | solution.py:766
  383.4 39.2 %collective-permute-start.39 = (bf16[4,256,256]{2,1,0:T(8,128)(2,1)}, bf16[4,256,256]{2,1,0:T(8,128)(2,1)}, u32[]{:S(2)}, u32[]{:S(2)}) collective-permute-start(bf16[4,256,256]{2,1,0:T(8,128)(2,1)} %get-tuple-element.121), channel_id=1, source_target_pairs={{0,4},{4,0},{8,12},{12,8},{16,20},{20,16},{24,28},{28,24},{1,5},{5... | collective-permute-start | bytes 1572872 | tf_op jit(solution)/shard_map/ppermute | solution.py:766
  384.0 69.8 %collective-permute-start.40 = (bf16[4,256,256]{2,1,0:T(8,128)(2,1)}, bf16[4,256,256]{2,1,0:T(8,128)(2,1)}, u32[]{:S(2)}, u32[]{:S(2)}) collective-permute-start(bf16[4,256,256]{2,1,0:T(8,128)(2,1)} %get-tuple-element.122), channel_id=1, source_target_pairs={{0,2},{1,3},{2,0},{3,1},{4,6},{5,7},{6,4},{7,5},{8,10},{9,11},{10,... | collective-permute-start | bytes 1572872 | tf_op jit(solution)/shard_map/ppermute | solution.py:766
  399.7 72.6 %collective-permute-start.46 = (bf16[4,496,256]{2,1,0:T(8,128)(2,1)}, bf16[4,496,256]{2,1,0:T(8,128)(2,1)S(1)}, u32[]{:S(2)}, u32[]{:S(2)}) collective-permute-start(bf16[4,496,256]{2,1,0:T(8,128)(2,1)} %get-tuple-element.130), channel_id=1, source_target_pairs={{0,4},{4,0},{8,12},{12,8},{16,20},{20,16},{24,28},{28,24},{1,5},{5... | collective-permute-start | bytes 3047432 | tf_op jit(solution)/shard_map/ppermute | solution.py:766
  420.8 65.1 %collective-permute-start.47 = (bf16[4,496,256]{2,1,0:T(8,128)(2,1)}, bf16[4,496,256]{2,1,0:T(8,128)(2,1)S(1)}, u32[]{:S(2)}, u32[]{:S(2)}) collective-permute-start(bf16[4,496,256]{2,1,0:T(8,128)(2,1)} %get-tuple-element.131), channel_id=1, source_target_pairs={{0,2},{1,3},{2,0},{3,1},{4,6},{5,7},{6,4},{7,5},{8,10},{9,11},{10,... | collective-permute-start | bytes 3047432 | tf_op jit(solution)/shard_map/ppermute | solution.py:766
  422.6 64.2 %collective-permute-start.48 = (bf16[4,496,256]{2,1,0:T(8,128)(2,1)}, bf16[4,496,256]{2,1,0:T(8,128)(2,1)S(1)}, u32[]{:S(2)}, u32[]{:S(2)}) collective-permute-start(bf16[4,496,256]{2,1,0:T(8,128)(2,1)} %get-tuple-element.132), channel_id=1, source_target_pairs={{0,6},{1,7},{2,4},{3,5},{4,2},{5,3},{6,0},{7,1},{8,14},{9,15},{10,... | collective-permute-start | bytes 3047432 | tf_op jit(solution)/shard_map/ppermute | solution.py:771
  499.9 49.1 %collective-permute-start.54 = (bf16[4,368,384]{2,1,0:T(8,128)(2,1)}, bf16[4,368,384]{2,1,0:T(8,128)(2,1)S(1)}, u32[]{:S(2)}, u32[]{:S(2)}) collective-permute-start(bf16[4,368,384]{2,1,0:T(8,128)(2,1)} %get-tuple-element.140), channel_id=1, source_target_pairs={{0,2},{1,3},{2,0},{3,1},{4,6},{5,7},{6,4},{7,5},{8,10},{9,11},{10,... | collective-permute-start | bytes 3391496 | tf_op jit(solution)/shard_map/ppermute | solution.py:766
  501.7 49.1 %collective-permute-start.55 = (bf16[4,368,384]{2,1,0:T(8,128)(2,1)}, bf16[4,368,384]{2,1,0:T(8,128)(2,1)}, u32[]{:S(2)}, u32[]{:S(2)}) collective-permute-start(bf16[4,368,384]{2,1,0:T(8,128)(2,1)} %get-tuple-element.141), channel_id=1, source_target_pairs={{0,6},{1,7},{2,4},{3,5},{4,2},{5,3},{6,0},{7,1},{8,14},{9,15},{10,... | collective-permute-start | bytes 3391496 | tf_op jit(solution)/shard_map/ppermute | solution.py:771
  (71 other events, 1210.5 us)

commit v3 on v2

--- a/solution.py
+++ b/solution.py
@@ -342,11 +342,11 @@
 T=1024; D=960; DP=1024
 NT=(((1,),(1,)),((),())); NN=(((1,),(0,)),((),())); TN=(((0,),(0,)),((),()))
 def dot(a,b,dn=NN): return lax.dot_general(a,b,dn,preferred_element_type=F32)
-ANY=pl.BlockSpec(memory_space=pl.ANY)
+ANY=pl.BlockSpec(memory_space=pltpu.HBM)
 SMEM=pl.BlockSpec(memory_space=pltpu.SMEM)
 def flip(a,b): return lax.bitwise_xor(a,b)
 def const(shape): return pl.BlockSpec(shape,lambda *g:(0,)*len(shape))
-def params(): return pltpu.CompilerParams(vmem_limit_bytes=60<<20)
+def params(mib): return pltpu.CompilerParams(vmem_limit_bytes=mib<<20)
 def cost(us): return pl.CostEstimate(flops=int(us*9e8),bytes_accessed=int(us*2e6),transcendentals=0)
 def sds(shape,dt): return jax.ShapeDtypeStruct(shape,dt)
 
@@ -420,7 +420,7 @@
         out_specs=[ospec, pl.BlockSpec((1,256,8*S),lambda j,i,idx:(j,i,0)), pl.BlockSpec((1,4*S,DP),lambda j,i,idx:(j,0,0))],
         scratch_shapes=[pltpu.VMEM((8,DP,2*S),BF),pltpu.VMEM((4,8,2*S,128),BF),pltpu.VMEM((T,DP),F32),pltpu.SemaphoreType.DMA((2,2))]),
         out_shape=[sds((2,2,D,256),BF) if last else sds((T,DP),F32),sds((2,T,8*S),BF),sds((2,4*S,DP),BF)],
-        compiler_params=params(), cost_estimate=cost(20), name="ffn_fwd")(idx,n2,mid,*gp)
+        compiler_params=params(60), cost_estimate=cost(20), name="ffn_fwd")(idx,n2,mid,*gp)
 
 def slot_of(idx, dpi, ctx):
     z=dpi//2; x=dpi%2; y=ctx//2; c=ctx%2
@@ -506,7 +506,7 @@
         out_specs=[full,ANY,ANY],
         out_shape=[sds((T,DP),F32)]+[sds((2,2,4,rows,2*S),BF)]*2,
         scratch_shapes=[pltpu.VMEM((T,DP),BF),pltpu.VMEM((8,DP,2*S),BF),pltpu.VMEM((T,8*S),BF),pltpu.VMEM((T,4*S),BF),pltpu.VMEM((DP,8*S),BF),pltpu.VMEM((8,4*S,128),BF)]+[pltpu.SemaphoreType.DMA((2,))]*3,
-        compiler_params=params(), cost_estimate=cost(33), name="ffn_bwd")(idx,cb,h,wd,n2,*([] if dn2in is None else [dn2in]),*gp)
+        compiler_params=params(60), cost_estimate=cost(33), name="ffn_bwd")(idx,cb,h,wd,n2,*([] if dn2in is None else [dn2in]),*gp)
 
 def block(f): return f.astype(F32)
 def reduce_one_kernel(keep, rc, sx, sy, sxy):
@@ -515,7 +515,7 @@
 def reduce_one(keep, rc):
     _,_,_,r,n=keep.shape
     b=pl.BlockSpec((2,2,1,r,n),lambda k:(0,0,k,0,0)); o=pl.BlockSpec((1,r,n),lambda k:(k,0,0))
-    return pl.pallas_call(reduce_one_kernel,grid=(4,),in_specs=[b,b],out_specs=[o]*3,out_shape=[sds((4,r,n),BF)]*3,compiler_params=params(),cost_estimate=cost(3),name="reduce_one")(keep,rc)
+    return pl.pallas_call(reduce_one_kernel,grid=(4,),in_specs=[b,b],out_specs=[o]*3,out_shape=[sds((4,r,n),BF)]*3,compiler_params=params(18),cost_estimate=cost(3),name="reduce_one")(keep,rc)
 def reduce_two_kernel(keep, rc, a, b, c, own, s1, s2, s3):
     k=pl.program_id(0)
     t=block(keep[0,0,0])+block(rc[0,0,0])+block(a[0])+block(b[0])+block(c[0])
@@ -527,7 +527,7 @@
 def reduce_two(keep, rc, a, b, c):
     _,_,_,r,n=keep.shape
     kb=pl.BlockSpec((1,1,1,r,n),lambda k:(0,0,k,0,0)); ib=pl.BlockSpec((1,r,n),lambda k:(k,0,0)); ob=pl.BlockSpec((r,n),lambda k:(0,0))
-    return pl.pallas_call(reduce_two_kernel,grid=(4,),in_specs=[kb,kb,ib,ib,ib],out_specs=[ob]*4,out_shape=[sds((r,n),F32)]+[sds((r,n),BF)]*3,compiler_params=params(),cost_estimate=cost(3),name="reduce_two")(keep,rc,a,b,c)
+    return pl.pallas_call(reduce_two_kernel,grid=(4,),in_specs=[kb,kb,ib,ib,ib],out_specs=[ob]*4,out_shape=[sds((r,n),F32)]+[sds((r,n),BF)]*3,compiler_params=params(12),cost_estimate=cost(3),name="reduce_two")(keep,rc,a,b,c)
 
 NEG=-1e30
 QB=256
@@ -553,7 +553,7 @@
     qs=pl.BlockSpec((3,T,128),lambda g:(g+g0,0,0)); ks=pl.BlockSpec((1,T,128),lambda g:(g+g0,0,0))
     return pl.pallas_call(attn_fwd_kernel,grid=(ng,),in_specs=[qs,ks,ks],
         out_specs=[pl.BlockSpec((3,T,128),lambda g:(g,0,0)),pl.BlockSpec((3,1,T),lambda g:(g,0,0))],
-        out_shape=[sds((3*ng,T,128),BF),sds((3*ng,1,T),F32)],compiler_params=params(),cost_estimate=cost(6*ng),name="attn_fwd")(q,k,v)
+        out_shape=[sds((3*ng,T,128),BF),sds((3*ng,1,T),F32)],compiler_params=params(60),cost_estimate=cost(6*ng),name="attn_fwd")(q,k,v)
 
 def unrot(g,c,s,low):
     t=jnp.where(low,pltpu.roll(g,96,1),-pltpu.roll(g,32,1))
@@ -589,7 +589,7 @@
         out_specs=[qo,ko,ko],
         out_shape=[sds((3*ng,T,128),BF),sds((ng,T,128),BF),sds((ng,T,128),BF)],
         scratch_shapes=[pltpu.VMEM((T,128),F32),pltpu.VMEM((T,128),F32)],
-        compiler_params=params(),cost_estimate=cost(9*ng),name="attn_bwd")(q,k,v,do,lse,delta,c,s)
+        compiler_params=params(30),cost_estimate=cost(9*ng),name="attn_bwd")(q,k,v,do,lse,delta,c,s)
 
 EPS=1e-5
 WN=1664
@@ -642,7 +642,7 @@
         [row_spec(DP),head_spec(15),head_spec(5),head_spec(5),cst((DP,WN)),cst((2,DP))],
         [pltpu.VMEM((8,4,256,256),BF),pltpu.SemaphoreType.DMA]),
         out_shape=[sds((T,DP),BF),sds((15,T,128),BF),sds((5,T,128),BF),sds((5,T,128),BF),sds((DP,WN),BF),sds((2,DP),F32)],
-        compiler_params=params(),cost_estimate=cost(16), name="qkv_fwd")(idx,x,c,s,*pc)
+        compiler_params=params(60),cost_estimate=cost(16), name="qkv_fwd")(idx,x,c,s,*pc)
 
 def out_kernel(idx,o1,o2,x,gains,*refs):
     pc=refs[:8]
@@ -664,7 +664,7 @@
 
 def out_fwd(idx,o1,o2,x,gains,pc):
     return pl.pallas_call(out_kernel,grid_spec=prefetch((4,),[head_spec(o1.shape[0]),head_spec(o2.shape[0]),row_spec(DP),cst((2,DP))]+[ANY]*8,
-        [row_spec(DP)]*3+[cst((DP,DP))],[pltpu.VMEM((8,D,128),BF),pltpu.SemaphoreType.DMA]),out_shape=[sds((T,DP),BF),sds((T,DP),F32),sds((T,DP),BF),sds((DP,DP),BF)],compiler_params=params(),cost_estimate=cost(9),name="out_fwd")(idx,o1,o2,x,gains,*pc)
+        [row_spec(DP)]*3+[cst((DP,DP))],[pltpu.VMEM((8,D,128),BF),pltpu.SemaphoreType.DMA]),out_shape=[sds((T,DP),BF),sds((T,DP),F32),sds((T,DP),BF),sds((DP,DP),BF)],compiler_params=params(60),cost_estimate=cost(9),name="out_fwd")(idx,o1,o2,x,gains,*pc)
 
 def tok_in_kernel(idx,h,r,g,o):
     y=idx[2]; c=idx[3]
@@ -672,7 +672,7 @@
         b=2*flip(y,ys)+flip(c,cs)
         o[pl.ds(pl.multiple_of(256*b,256),256),:]=jnp.concatenate([v,zeros(64,256,BF)],axis=0).T
 def tok_in(idx,h,r,g):
-    return pl.pallas_call(tok_in_kernel,in_specs=[SMEM]+[pl.BlockSpec(memory_space=pltpu.VMEM)]*3,out_specs=pl.BlockSpec(memory_space=pltpu.VMEM),out_shape=sds((T,DP),BF),compiler_params=params(),cost_estimate=cost(4),name="tok_in")(idx,h,r,g)
+    return pl.pallas_call(tok_in_kernel,in_specs=[SMEM]+[pl.BlockSpec(memory_space=pltpu.VMEM)]*3,out_specs=pl.BlockSpec(memory_space=pltpu.VMEM),out_shape=sds((T,DP),BF),compiler_params=params(14),cost_estimate=cost(4),name="tok_in")(idx,h,r,g)
 
 def out_bwd_kernel(idx,dn2,cb,mid,gains,wo,att,kin,sin,dmid,do,dg,ok,os_,delta,dbr_s,st,sem):
     i=pl.program_id(0)
@@ -708,7 +708,7 @@
     return pl.pallas_call(out_bwd_kernel,grid_spec=prefetch((4,),[row_spec(DP)]*3+[cst((2,DP)),cst((DP,DP)),cst((T,DP)),ANY,ANY],
         [row_spec(DP),head_spec(15),cst((1,DP)),ANY,ANY,pl.BlockSpec((15,1,256),lambda i,idx:(0,0,i))],[pltpu.VMEM((T,DP),BF),pltpu.VMEM((8,DP,128),BF),pltpu.SemaphoreType.DMA]),
         out_shape=[sds((T,DP),F32),sds((15,T,128),BF),sds((1,DP),F32)]+[sds(keep.shape,BF)]*2+[sds((15,1,T),F32)],input_output_aliases={7:3,8:4},
-        compiler_params=params(),cost_estimate=cost(16), name="out_bwd")(idx,dn2,cb,mid,gains,wo,att,keep,send)
+        compiler_params=params(60),cost_estimate=cost(16), name="out_bwd")(idx,dn2,cb,mid,gains,wo,att,keep,send)
 
 def qkv_dx_kernel(idx,dq1,dk1,dv1,dq2,dk2,dv2,dq3,dk3,dv3,x,gains,dmid,w,hg,dh,dg1):
     i=pl.program_id(0)
@@ -726,7 +726,7 @@
 def qkv_dx(idx,g1,g2,g3,x,gains,dmid,w):
     return pl.pallas_call(qkv_dx_kernel,grid_spec=prefetch((4,),[head_spec(a.shape[0]) for a in (*g1,*g2,*g3)]+[row_spec(DP),cst((2,DP)),row_spec(DP),cst((DP,WN))],
         [tok_spec(),row_spec(WN),cst((1,DP))],[]),out_shape=[sds((2,2,D,256),BF),sds((T,WN),BF),sds((1,DP),F32)],
-        compiler_params=params(),cost_estimate=cost(9),name="qkv_dx")(idx,*g1,*g2,*g3,x,gains,dmid,w)
+        compiler_params=params(24),cost_estimate=cost(9),name="qkv_dx")(idx,*g1,*g2,*g3,x,gains,dmid,w)
 
 def qkv_dw_kernel(idx,n1,dh,dg1,dg2,wk,ws,st,sg,sem):
     m=pl.program_id(0)
@@ -750,7 +750,7 @@
 def qkv_dw(idx,n1,dh,dg1,dg2):
     return pl.pallas_call(qkv_dw_kernel,grid_spec=prefetch((4,),[pl.BlockSpec((T,256),lambda m,idx:(0,m)),cst((T,WN)),cst((1,DP)),cst((1,DP))],
         [ANY,ANY],[pltpu.VMEM((8,DP,256),BF),pltpu.VMEM((8,4,16,256),BF),pltpu.SemaphoreType.DMA]),out_shape=[sds((2,2,4,256,256),BF)]*2,
-        compiler_params=params(),cost_estimate=cost(9),name="qkv_dw")(idx,n1,dh,dg1,dg2)
+        compiler_params=params(60),cost_estimate=cost(9),name="qkv_dw")(idx,n1,dh,dg1,dg2)
 
 def tok_out_kernel(idx,a,r,b,o):
     y=idx[2]; c=idx[3]
@@ -758,7 +758,7 @@
     o[2*(1-y)+c]=b[0]; o[2*(1-y)+1-c]=b[1]
 def tok_out(idx,a,r,b):
     v=pl.BlockSpec(memory_space=pltpu.VMEM)
-    return pl.pallas_call(tok_out_kernel,grid=(1,),in_specs=[SMEM,pl.BlockSpec((1,1,D,256),lambda i:(0,0,0,0)),pl.BlockSpec((1,D,256),lambda i:(0,0,0)),v],out_specs=v,out_shape=sds((4,D,256),BF),compiler_params=params(),cost_estimate=cost(4),name="tok_out")(idx,a,r,b)
+    return pl.pallas_call(tok_out_kernel,grid=(1,),in_specs=[SMEM,pl.BlockSpec((1,1,D,256),lambda i:(0,0,0,0)),pl.BlockSpec((1,D,256),lambda i:(0,0,0)),v],out_specs=v,out_shape=sds((4,D,256),BF),compiler_params=params(10),cost_estimate=cost(4),name="tok_out")(idx,a,r,b)
 
 
 def swap(a, axis, bit):

time: 590 us -> 579 us (0.981)
  Pallas kernels: 268 us -> 232 us
  local copies, waits for them, and re-layouts: 30.6 us -> 42 us
  waiting for transfers between devices: 203 us -> 212 us
    ppermute x35, waiting for transfers between devices: 125 us -> 139 us  [swap(): return lax.ppermute(a, axis, [(i, i ^ bit) for i in range(n)])]
    unnamed x86 -> x128, local copies, waits for them, and re-layouts: 11.6 us -> 24.4 us
    pallas_call x3, Pallas kernels: 37.4 us -> 28.4 us  [attn_bwd(): pl.pallas_call(attn_bwd_kernel, grid=(ng,), in_specs=[qs, ks, ks, qs] + [...]
    pallas_call x3, Pallas kernels: 15.1 us -> 6.89 us  [reduce_one(): pl.pallas_call(reduce_one_kernel, grid=(4,), in_specs=[b, b], out_specs=[...]
    pallas_call x3, Pallas kernels: 13.3 us -> 5.39 us  [reduce_two(): pl.pallas_call(reduce_two_kernel, grid=(4,), in_specs=[kb, kb, ib, ib, ib...]
  transfers between devices with their start and end apart: 59 -> 59, of which waited for: 20 -> 20; matrix products, arithmetic and copies ran while one was open for 6% -> 6% of each run, Pallas kernels for 30% -> 25%
where the time goes in v3:
time: 579 us; the launch traced here: 570 us
  Pallas kernels  232 us (40%)
  waiting for transfers between devices  212 us (37%)
  starting transfers between devices  64.8 us (11%)
  local copies, waits for them, and re-layouts  42 us (7%)
  other arithmetic  17.8 us (3%)
    ppermute x35, waiting for transfers between devices, swap(): return lax.ppermute(a, axis, [(i, i ^ bit) for i in range(n)])  139 us
    pallas_call x2, Pallas kernels, ffn_bwd(): pl.pallas_call(functools.partial(ffn_bwd_kernel, S, kind, dn2in is None),...  59.4 us
    ppermute x18, waiting for transfers between devices, from_z(): lax.ppermute(a, 'dp', [((z + k) % 4 * 2 + x, z * 2 + x) for z in range(4)...  42.9 us
    pallas_call x2, Pallas kernels, ffn_fwd(): pl.pallas_call(functools.partial(ffn_fwd_kernel, S, kind, last), grid_spe...  41.6 us
    ppermute x18, starting transfers between devices, from_z(): lax.ppermute(a, 'dp', [((z + k) % 4 * 2 + x, z * 2 + x) for z in range(4)...  35.7 us
    ppermute x6, waiting for transfers between devices, move(): lax.ppermute(a, ('dp', 'ctx'), [(i, (i // n ^ 1) * n + (i % n ^ 2)) for i...  30.1 us
    pallas_call x3, Pallas kernels, attn_bwd(): pl.pallas_call(attn_bwd_kernel, grid=(ng,), in_specs=[qs, ks, ks, qs] + [...  28.4 us
    unnamed x128, local copies, waits for them, and re-layouts  24.4 us
  transfers between devices with their start and end apart: 59, of which 20 were waited for; matrix products, arithmetic and copies ran while one was open for 6% of the time, Pallas kernels for 25%

profile of v3, /device:TPU:0, one launch (start us, length us, event | category | flops | bytes accessed | tf_op | source)
XLA Modules:
  0.0 569.9 jit_solution(15831231364704812127)
XLA Ops:
  21.0 10.7 %collective-permute-start.13 = (bf16[448,384]{1,0:T(8,128)(2,1)}, bf16[448,384]{1,0:T(8,128)(2,1)}, u32[]{:S(2)}, u32[]{:S(2)}) collective-permute-start(bf16[448,384]{1,0:T(8,128)(2,1)} %maximum_maximum_fusion), channel_id=1, source_target_pairs={{16,0},{20,4},{24,8},{28,12},{0,16},{4,20},{8,24},{12,28},{17,1},{... | collective-permute-start | bytes 1032200 | tf_op jit(solution)/shard_map/ppermute | solution.py:777
  38.1 13.3 %collective-permute-done.4.refs_1_ = bf16[4,256,256]{2,1,0:T(8,128)(2,1)} collective-permute-done((bf16[4,256,256]{2,1,0:T(8,128)(2,1)}, bf16[4,256,256]{2,1,0:T(8,128)(2,1)}, u32[]{:S(2)}, u32[]{:S(2)}) %collective-permute-start.4) | collective-permute-done | bytes 524320 | tf_op jit(solution)/shard_map/ppermute | solution.py:766
  102.1 14.2 %qkv_fwd.1 = (bf16[1024,1024]{1,0:T(8,128)(2,1)}, bf16[15,1024,128]{2,1,0:T(8,128)(2,1)}, bf16[5,1024,128]{2,1,0:T(8,128)(2,1)}, bf16[5,1024,128]{2,1,0:T(8,128)...) custom-call(s32[4]{0:T(128)} %copy-done.12, bf16[1024,1024]{1,0:T(8,128)(2,1)} %copy-done.17, f32[1024,128]{1,0:T(8,128)} %copy.39.c, ...), custom_call_target="tpu_custom_call" | custom-call | flops 14400000000 | bytes 32000000 | tf_op jit(solution)/shard_map/qkv_fwd/pallas_call | solution.py:641
  116.4 13.3 %attn_fwd.2 = (bf16[9,1024,128]{2,1,0:T(8,128)(2,1)}, f32[9,1,1024]{2,1,0:T(1,128)}) custom-call(bf16[15,1024,128]{2,1,0:T(8,128)(2,1)} %get-tuple-element.79.q, bf16[5,1024,128]{2,1,0:T(8,128)(2,1)} %get-tuple-element.80.k, bf16[5,1024,128]{2,1,0:T(8,128)(2,1)} %get-tuple-element.81.v), custom_call_target="tpu_custom_call" | custom-call | flops 16199999488 | bytes 36000000 | tf_op jit(solution)/shard_map/attn_fwd/pallas_call | solution.py:554
  129.7 15.5 %collective-permute-done.26.refs_2_.refs_3_ = bf16[4,368,256]{2,1,0:T(8,128)(2,1)} collective-permute-done((bf16[4,368,256]{2,1,0:T(8,128)(2,1)}, bf16[4,368,256]{2,1,0:T(8,128)(2,1)}, u32[]{:S(2)}, u32[]{:S(2)}) %collective-permute-start.26) | collective-permute-done | bytes 753696 | tf_op jit(solution)/shard_map/ppermute | solution.py:777
  146.3 15.3 %collective-permute-done.17.refs_3_ = bf16[4,448,384]{2,1,0:T(8,128)(2,1)} collective-permute-done((bf16[4,448,384]{2,1,0:T(8,128)(2,1)}, bf16[4,448,384]{2,1,0:T(8,128)(2,1)}, u32[]{:S(2)}, u32[]{:S(2)}) %collective-permute-start.17) | collective-permute-done | bytes 1376288 | tf_op jit(solution)/shard_map/ppermute | solution.py:771
  162.1 9.5 %attn_fwd.3 = (bf16[6,1024,128]{2,1,0:T(8,128)(2,1)}, f32[6,1,1024]{2,1,0:T(1,128)}) custom-call(bf16[15,1024,128]{2,1,0:T(8,128)(2,1)} %get-tuple-element.79.q, bf16[5,1024,128]{2,1,0:T(8,128)(2,1)} %get-tuple-element.80.k, bf16[5,1024,128]{2,1,0:T(8,128)(2,1)} %get-tuple-element.81.v), custom_call_target="tpu_custom_call" | custom-call | flops 10800000000 | bytes 24000000 | tf_op jit(solution)/shard_map/attn_fwd/pallas_call | solution.py:554
  176.6 11.0 %out_fwd.1 = (bf16[1024,1024]{1,0:T(8,128)(2,1)}, f32[1024,1024]{1,0:T(8,128)}, bf16[1024,1024]{1,0:T(8,128)(2,1)}, bf16[1024,1024]{1,0:T(8,128)(2,1)}) custom-call(s32[4]{0:T(128)} %copy-done.12, bf16[9,1024,128]{2,1,0:T(8,128)(2,1)} %get-tuple-element.82.o1, bf16[6,1024,128]{2,1,0:T(8,128)(2,1)} %get-tuple-element.83.o2, bf16[1024,1024]{1,0:T(8,128)(2,1)} %copy-done.17, ...), custom_call_target="tpu_custom_call" | custom-call | flops 8099999744 | bytes 18000000 | tf_op jit(solution)/shard_map/out_fwd/pallas_call | solution.py:666
  187.6 23.4 %ffn_fwd.2 = (f32[1024,1024]{1,0:T(8,128)}, bf16[2,1024,1536]{2,1,0:T(8,128)(2,1)}, bf16[2,768,1024]{2,1,0:T(8,128)(2,1)}) custom-call(s32[4]{0:T(128)} %copy-done.12, bf16[1024,1024]{1,0:T(8,128)(2,1)} %get-tuple-element.85.n2.n2h, f32[1024,1024]{1,0:T(8,128)} %get-tuple-element.86.mid, bf16[4,448,384]{2,1,0:T(8,128)(2,1)} %pad_maximum_fusion.refs_0_, ...), custom_call_target="tpu_custom_call" | custom-call | flops 17999998976 | bytes 40000000 | tf_op jit(solution)/shard_map/ffn_fwd/pallas_call | solution.py:418
  211.0 33.2 %ffn_bwd.2 = (f32[1024,1024]{1,0:T(8,128)}, bf16[2,2,4,368,384]{4,3,2,1,0:T(8,128)(2,1)}, bf16[2,2,4,368,384]{4,3,2,1,0:T(8,128)(2,1)}) custom-call(s32[4]{0:T(128)} %copy-done.12, bf16[1024,1024]{1,0:T(8,128)(2,1)} %copy-done.19, bf16[2,1024,1536]{2,1,0:T(8,128)(2,1)} %get-tuple-element.91.h, bf16[2,768,1024]{2,1,0:T(8,128)(2,1)} %get-tuple-element.92.wd, ...), custom_call_target="tpu_custom_call" | custom-call | flops 29699999744 | bytes 66000000 | tf_op jit(solution)/shard_map/ffn_bwd/pallas_call | solution.py:504
  245.9 18.3 %ffn_fwd.3 = (bf16[2,2,960,256]{3,2,1,0:T(8,128)(2,1)}, bf16[2,1024,1024]{2,1,0:T(8,128)(2,1)}, bf16[2,512,1024]{2,1,0:T(8,128)(2,1)}) custom-call(s32[4]{0:T(128)} %copy-done.12, bf16[1024,1024]{1,0:T(8,128)(2,1)} %get-tuple-element.85.n2.n2h, f32[1024,1024]{1,0:T(8,128)} %get-tuple-element.87.mid, bf16[4,368,256]{2,1,0:T(8,128)(2,1)} %pad_maximum_fusion.5.refs_0_.refs_1_, ...), custom_call_target="tpu_custom_call" | custom-call | flops 17999998976 | bytes 40000000 | tf_op jit(solution)/shard_map/ffn_fwd/pallas_call | solution.py:418
  264.2 26.2 %ffn_bwd.3 = (f32[1024,1024]{1,0:T(8,128)}, bf16[2,2,4,496,256]{4,3,2,1,0:T(8,128)(2,1)}, bf16[2,2,4,496,256]{4,3,2,1,0:T(8,128)(2,1)}) custom-call(s32[4]{0:T(128)} %copy-done.12, bf16[1024,1024]{1,0:T(8,128)(2,1)} %copy-done.19, bf16[2,1024,1024]{2,1,0:T(8,128)(2,1)} %get-tuple-element.89.h, bf16[2,512,1024]{2,1,0:T(8,128)(2,1)} %get-tuple-element.90.wd, ...), custom_call_target="tpu_custom_call" | custom-call | flops 29699999744 | bytes 66000000 | tf_op jit(solution)/shard_map/ffn_bwd/pallas_call | solution.py:504
  290.4 16.9 %out_bwd.1 = (f32[1024,1024]{1,0:T(8,128)}, bf16[15,1024,128]{2,1,0:T(8,128)(2,1)}, f32[1,1024]{1,0:T(1,128)}, bf16[2,2,4,496,256]{4,3,2,1,0:T(8,128)(2,1)}, bf1...) custom-call(s32[4]{0:T(128)} %copy-done.12, ...), custom_call_target="tpu_custom_call", output_to_operand_aliasing={{3}: (7, {}), {4}: (8, {})} | custom-call | flops 14400000000 | bytes 32000000 | tf_op jit(solution)/shard_map/out_bwd/pallas_call | solution.py:708
  312.4 11.2 %attn_bwd.5 = (bf16[6,1024,128]{2,1,0:T(8,128)(2,1)S(1)}, bf16[2,1024,128]{2,1,0:T(8,128)(2,1)S(1)}, bf16[2,1024,128]{2,1,0:T(8,128)(2,1)S(1)}) custom-call(bf16[15,1024,128]{2,1,0:T(8,128)(2,1)S(1)} %copy-done.23, bf16[5,1024,128]{2,1,0:T(8,128)(2,1)S(1)} %copy-done.26, bf16[5,1024,128]{2,1,0:T(8,128)(2,1)S(1)} %copy-done.28, ...), custom_call_target="tpu_custom_call" | custom-call | flops 16199999488 | bytes 36000000 | tf_op jit(solution)/shard_map/attn_bwd/pallas_call | solution.py:588
  323.7 11.4 %attn_bwd.4 = (bf16[6,1024,128]{2,1,0:T(8,128)(2,1)S(1)}, bf16[2,1024,128]{2,1,0:T(8,128)(2,1)S(1)}, bf16[2,1024,128]{2,1,0:T(8,128)(2,1)S(1)}) custom-call(bf16[15,1024,128]{2,1,0:T(8,128)(2,1)S(1)} %copy-done.24, bf16[5,1024,128]{2,1,0:T(8,128)(2,1)S(1)} %copy-done.26, bf16[5,1024,128]{2,1,0:T(8,128)(2,1)S(1)} %copy-done.28, ...), custom_call_target="tpu_custom_call" | custom-call | flops 16199999488 | bytes 36000000 | tf_op jit(solution)/shard_map/attn_bwd/pallas_call | solution.py:588
  352.6 10.4 %qkv_dw.1 = (bf16[2,2,4,256,256]{4,3,2,1,0:T(8,128)(2,1)}, bf16[2,2,4,256,256]{4,3,2,1,0:T(8,128)(2,1)}) custom-call(s32[4]{0:T(128)} %copy-done.12, bf16[1024,1024]{1,0:T(8,128)(2,1)} %get-tuple-element.115.n1, bf16[1024,1664]{1,0:T(8,128)(2,1)} %copy-done.22, f32[1,1024]{1,0:T(1,128)} %copy-done.32, f32[1,1024]{1,0:T(1,128)} %get-tuple-element.118.dg2), custom_call_target="tpu_custom_call" | custom-call | flops 8099999744 | bytes 18000000 | tf_op jit(solution)/shard_map/qkv_dw/pallas_call | solution.py:751
  375.7 17.9 %collective-permute-done.37.b = bf16[2,960,256]{2,1,0:T(8,128)(2,1)S(1)} collective-permute-done((bf16[2,960,256]{2,1,0:T(8,128)(2,1)S(1)}, bf16[2,960,256]{2,1,0:T(8,128)(2,1)S(1)}, u32[]{:S(2)}, u32[]{:S(2)}) %collective-permute-start.37) | collective-permute-done | bytes 983072 | tf_op jit(solution)/shard_map/ppermute | solution.py:766
  394.2 20.5 %collective-permute-done.33.b = bf16[2,960,256]{2,1,0:T(8,128)(2,1)S(1)} collective-permute-done((bf16[2,960,256]{2,1,0:T(8,128)(2,1)S(1)}, bf16[2,960,256]{2,1,0:T(8,128)(2,1)S(1)}, u32[]{:S(2)}, u32[]{:S(2)}) %collective-permute-start.33) | collective-permute-done | bytes 983072 | tf_op jit(solution)/shard_map/ppermute | solution.py:766
  416.7 31.0 %collective-permute-done.40.b = bf16[4,256,256]{2,1,0:T(8,128)(2,1)S(1)} collective-permute-done((bf16[4,256,256]{2,1,0:T(8,128)(2,1)S(1)}, bf16[4,256,256]{2,1,0:T(8,128)(2,1)S(1)}, u32[]{:S(2)}, u32[]{:S(2)}) %collective-permute-start.40) | collective-permute-done | bytes 524320 | tf_op jit(solution)/shard_map/ppermute | solution.py:766
  453.3 7.6 %collective-permute-done.41.c = bf16[4,256,256]{2,1,0:T(8,128)(2,1)S(1)} collective-permute-done((bf16[4,256,256]{2,1,0:T(8,128)(2,1)S(1)}, bf16[4,256,256]{2,1,0:T(8,128)(2,1)S(1)}, u32[]{:S(2)}, u32[]{:S(2)}) %collective-permute-start.41) | collective-permute-done | bytes 524320 | tf_op jit(solution)/shard_map/ppermute | solution.py:771
  463.6 16.3 %collective-permute-done.47.b = bf16[4,496,256]{2,1,0:T(8,128)(2,1)S(1)} collective-permute-done((bf16[4,496,256]{2,1,0:T(8,128)(2,1)S(1)}, bf16[4,496,256]{2,1,0:T(8,128)(2,1)S(1)}, u32[]{:S(2)}, u32[]{:S(2)}) %collective-permute-start.47) | collective-permute-done | bytes 1015840 | tf_op jit(solution)/shard_map/ppermute | solution.py:766
  508.3 9.2 %collective-permute-done.53.a = bf16[4,368,384]{2,1,0:T(8,128)(2,1)S(1)} collective-permute-done((bf16[4,368,384]{2,1,0:T(8,128)(2,1)}, bf16[4,368,384]{2,1,0:T(8,128)(2,1)S(1)}, u32[]{:S(2)}, u32[]{:S(2)}) %collective-permute-start.53) | collective-permute-done | bytes 1130528 | tf_op jit(solution)/shard_map/ppermute | solution.py:766
  517.5 21.7 %collective-permute-done.54.b = bf16[4,368,384]{2,1,0:T(8,128)(2,1)S(1)} collective-permute-done((bf16[4,368,384]{2,1,0:T(8,128)(2,1)}, bf16[4,368,384]{2,1,0:T(8,128)(2,1)S(1)}, u32[]{:S(2)}, u32[]{:S(2)}) %collective-permute-start.54) | collective-permute-done | bytes 1130528 | tf_op jit(solution)/shard_map/ppermute | solution.py:766
  557.4 9.1 %collective-permute-done.57 = bf16[368,384]{1,0:T(8,128)(2,1)S(1)} collective-permute-done((bf16[368,384]{1,0:T(8,128)(2,1)S(1)}, bf16[368,384]{1,0:T(8,128)(2,1)S(1)}, u32[]{:S(2)}, u32[]{:S(2)}) %collective-permute-start.57) | collective-permute-done | bytes 282656 | tf_op jit(solution)/shard_map/ppermute | solution.py:777
  (312 shorter events, 181.0 us)
Async XLA Ops:
  13.1 39.7 %collective-permute-start = (bf16[2,960,256]{2,1,0:T(8,128)(2,1)}, bf16[2,960,256]{2,1,0:T(8,128)(2,1)S(1)}, u32[]{:S(2)}, u32[]{:S(2)}) collective-permute-start(bf16[2,960,256]{2,1,0:T(8,128)(2,1)} %dynamic-slice_bitcast_fusion.1), channel_id=1, source_target_pairs={{0,2},{1,3},{2,0},{3,1},{4,6},{5,7},{6,4},{7,5},{8,10},{9,11},{10,... | collective-permute-start | bytes 2949128 | tf_op jit(solution)/shard_map/ppermute | solution.py:766
  16.2 46.9 %collective-permute-start.12 = (bf16[448,384]{1,0:T(8,128)(2,1)}, bf16[448,384]{1,0:T(8,128)(2,1)}, u32[]{:S(2)}, u32[]{:S(2)}) collective-permute-start(bf16[448,384]{1,0:T(8,128)(2,1)} %maximum_maximum_fusion), channel_id=1, source_target_pairs={{8,0},{12,4},{16,8},{20,12},{24,16},{28,20},{0,24},{4,28},{9,1},{1... | collective-permute-start | bytes 1032200 | tf_op jit(solution)/shard_map/ppermute | solution.py:777
  21.0 47.7 %collective-permute-start.13 = (bf16[448,384]{1,0:T(8,128)(2,1)}, bf16[448,384]{1,0:T(8,128)(2,1)}, u32[]{:S(2)}, u32[]{:S(2)}) collective-permute-start(bf16[448,384]{1,0:T(8,128)(2,1)} %maximum_maximum_fusion), channel_id=1, source_target_pairs={{16,0},{20,4},{24,8},{28,12},{0,16},{4,20},{8,24},{12,28},{17,1},{... | collective-permute-start | bytes 1032200 | tf_op jit(solution)/shard_map/ppermute | solution.py:777
  52.9 37.1 %collective-permute-start.34 = (bf16[2,960,256]{2,1,0:T(8,128)(2,1)}, bf16[2,960,256]{2,1,0:T(8,128)(2,1)}, u32[]{:S(2)}, u32[]{:S(2)}) collective-permute-start(bf16[2,960,256]{2,1,0:T(8,128)(2,1)} %dynamic-slice_bitcast_fusion), channel_id=1, source_target_pairs={{0,2},{1,3},{2,0},{3,1},{4,6},{5,7},{6,4},{7,5},{8,10},{9,11},{10,... | collective-permute-start | bytes 2949128 | tf_op jit(solution)/shard_map/ppermute | solution.py:766
  58.9 33.2 %collective-permute-start.5 = (bf16[2,960,256]{2,1,0:T(8,128)(2,1)}, bf16[2,960,256]{2,1,0:T(8,128)(2,1)}, u32[]{:S(2)}, u32[]{:S(2)}) collective-permute-start(bf16[2,960,256]{2,1,0:T(8,128)(2,1)} %pad_maximum_fusion.1), channel_id=1, source_target_pairs={{0,1},{1,0},{2,3},{3,2},{4,5},{5,4},{6,7},{7,6},{8,9},{9,8},{10,11... | collective-permute-start | bytes 2949128 | tf_op jit(solution)/shard_map/ppermute | solution.py:766
  96.9 48.3 %collective-permute-start.26 = (bf16[4,368,256]{2,1,0:T(8,128)(2,1)}, bf16[4,368,256]{2,1,0:T(8,128)(2,1)}, u32[]{:S(2)}, u32[]{:S(2)}) collective-permute-start(bf16[4,368,256]{2,1,0:T(8,128)(2,1)} %pad_maximum_fusion.5.refs_0_.refs_1_), channel_id=1, source_target_pairs={{16,0},{20,4},{24,8},{28,12},{0,16},{4,20},{8,24},{12,28},{17,1},{... | collective-permute-start | bytes 2261000 | tf_op jit(solution)/shard_map/ppermute | solution.py:777
  98.6 47.1 %collective-permute-start.15 = (bf16[4,448,384]{2,1,0:T(8,128)(2,1)}, bf16[4,448,384]{2,1,0:T(8,128)(2,1)}, u32[]{:S(2)}, u32[]{:S(2)}) collective-permute-start(bf16[4,448,384]{2,1,0:T(8,128)(2,1)} %pad_maximum_fusion.refs_0_), channel_id=1, source_target_pairs={{0,2},{1,3},{2,0},{3,1},{4,6},{5,7},{6,4},{7,5},{8,10},{9,11},{10,... | collective-permute-start | bytes 4128776 | tf_op jit(solution)/shard_map/ppermute | solution.py:766
  100.1 45.7 %collective-permute-start.16 = (bf16[4,448,384]{2,1,0:T(8,128)(2,1)}, bf16[4,448,384]{2,1,0:T(8,128)(2,1)}, u32[]{:S(2)}, u32[]{:S(2)}) collective-permute-start(bf16[4,448,384]{2,1,0:T(8,128)(2,1)} %pad_maximum_fusion.refs_0_), channel_id=1, source_target_pairs={{0,4},{4,0},{8,12},{12,8},{16,20},{20,16},{24,28},{28,24},{1,5},{5... | collective-permute-start | bytes 4128776 | tf_op jit(solution)/shard_map/ppermute | solution.py:766
  100.7 61.0 %collective-permute-start.17 = (bf16[4,448,384]{2,1,0:T(8,128)(2,1)}, bf16[4,448,384]{2,1,0:T(8,128)(2,1)}, u32[]{:S(2)}, u32[]{:S(2)}) collective-permute-start(bf16[4,448,384]{2,1,0:T(8,128)(2,1)} %pad_maximum_fusion.refs_0_), channel_id=1, source_target_pairs={{0,6},{1,7},{2,4},{3,5},{4,2},{5,3},{6,0},{7,1},{8,14},{9,15},{10,... | collective-permute-start | bytes 4128776 | tf_op jit(solution)/shard_map/ppermute | solution.py:771
  116.3 45.3 %collective-permute-start.35 = (bf16[2,960,256]{2,1,0:T(8,128)(2,1)S(1)}, bf16[2,960,256]{2,1,0:T(8,128)(2,1)S(1)}, u32[]{:S(2)}, u32[]{:S(2)}) collective-permute-start(bf16[2,960,256]{2,1,0:T(8,128)(2,1)S(1)} %copy-done.35), channel_id=1, source_target_pairs={{0,1},{1,0},{2,3},{3,2},{4,5},{5,4},{6,7},{7,6},{8,9},{9,8},{10,11... | collective-permute-start | bytes 2949128 | tf_op jit(solution)/shard_map/ppermute | solution.py:766
  175.6 68.6 %collective-permute-start.28 = (bf16[4,368,256]{2,1,0:T(8,128)(2,1)}, bf16[4,368,256]{2,1,0:T(8,128)(2,1)S(1)}, u32[]{:S(2)}, u32[]{:S(2)}) collective-permute-start(bf16[4,368,256]{2,1,0:T(8,128)(2,1)} %pad_maximum_fusion.5.refs_0_.refs_1_), channel_id=1, source_target_pairs={{0,1},{1,0},{2,3},{3,2},{4,5},{5,4},{6,7},{7,6},{8,9},{9,8},{10,11... | collective-permute-start | bytes 2261000 | tf_op jit(solution)/shard_map/ppermute | solution.py:766
  175.6 68.6 %collective-permute-start.29 = (bf16[4,368,256]{2,1,0:T(8,128)(2,1)}, bf16[4,368,256]{2,1,0:T(8,128)(2,1)S(1)}, u32[]{:S(2)}, u32[]{:S(2)}) collective-permute-start(bf16[4,368,256]{2,1,0:T(8,128)(2,1)} %collective-permute-done.25.refs_1_.refs_2_), channel_id=1, source_target_pairs={{0,1},{1,0},{2,3},{3,2},{4,5},{5,4},{6,7},{7,6},{8,9},{9,8},{10,11... | collective-permute-start | bytes 2261000 | tf_op jit(solution)/shard_map/ppermute | solution.py:766
  176.1 68.1 %collective-permute-start.30 = (bf16[4,368,256]{2,1,0:T(8,128)(2,1)}, bf16[4,368,256]{2,1,0:T(8,128)(2,1)S(1)}, u32[]{:S(2)}, u32[]{:S(2)}) collective-permute-start(bf16[4,368,256]{2,1,0:T(8,128)(2,1)} %collective-permute-done.26.refs_2_.refs_3_), channel_id=1, source_target_pairs={{0,1},{1,0},{2,3},{3,2},{4,5},{5,4},{6,7},{7,6},{8,9},{9,8},{10,11... | collective-permute-start | bytes 2261000 | tf_op jit(solution)/shard_map/ppermute | solution.py:766
  176.2 68.1 %collective-permute-start.31 = (bf16[4,368,256]{2,1,0:T(8,128)(2,1)}, bf16[4,368,256]{2,1,0:T(8,128)(2,1)S(1)}, u32[]{:S(2)}, u32[]{:S(2)}) collective-permute-start(bf16[4,368,256]{2,1,0:T(8,128)(2,1)} %collective-permute-done.27.refs_3_.refs_4_), channel_id=1, source_target_pairs={{0,1},{1,0},{2,3},{3,2},{4,5},{5,4},{6,7},{7,6},{8,9},{9,8},{10,11... | collective-permute-start | bytes 2261000 | tf_op jit(solution)/shard_map/ppermute | solution.py:766
  335.2 38.3 %collective-permute-start.45 = (bf16[2,2,4,496,256]{4,3,2,1,0:T(8,128)(2,1)}, bf16[2,2,4,496,256]{4,3,2,1,0:T(8,128)(2,1)S(1)}, u32[]{:S(2)}, u32[]{:S(2)}) collective-permute-start(bf16[2,2,4,496,256]{4,3,2,1,0:T(8,128)(2,1)} %get-tuple-element.129), channel_id=1, source_target_pairs={{0,1},{1,0},{2,3},{3,2},{4,5},{5,4},{6,7},{7,6},{8,9},{9,8},{10,11... | collective-permute-start | bytes 12189704 | tf_op jit(solution)/shard_map/ppermute | solution.py:766
  341.1 143.5 %collective-permute-start.52 = (bf16[2,2,4,368,384]{4,3,2,1,0:T(8,128)(2,1)}, bf16[2,2,4,368,384]{4,3,2,1,0:T(8,128)(2,1)}, u32[]{:S(2)}, u32[]{:S(2)}) collective-permute-start(bf16[2,2,4,368,384]{4,3,2,1,0:T(8,128)(2,1)} %get-tuple-element.138), channel_id=1, source_target_pairs={{0,1},{1,0},{2,3},{3,2},{4,5},{5,4},{6,7},{7,6},{8,9},{9,8},{10,11... | collective-permute-start | bytes 13565960 | tf_op jit(solution)/shard_map/ppermute | solution.py:766
  370.8 43.8 %collective-permute-start.33 = (bf16[2,960,256]{2,1,0:T(8,128)(2,1)S(1)}, bf16[2,960,256]{2,1,0:T(8,128)(2,1)S(1)}, u32[]{:S(2)}, u32[]{:S(2)}) collective-permute-start(bf16[2,960,256]{2,1,0:T(8,128)(2,1)S(1)} %pad_maximum_fusion.2), channel_id=1, source_target_pairs={{0,2},{1,3},{2,0},{3,1},{4,6},{5,7},{6,4},{7,5},{8,10},{9,11},{10,... | collective-permute-start | bytes 2949128 | tf_op jit(solution)/shard_map/ppermute | solution.py:766
  372.8 43.6 %collective-permute-start.39 = (bf16[4,256,256]{2,1,0:T(8,128)(2,1)S(1)}, bf16[4,256,256]{2,1,0:T(8,128)(2,1)S(1)}, u32[]{:S(2)}, u32[]{:S(2)}) collective-permute-start(bf16[4,256,256]{2,1,0:T(8,128)(2,1)S(1)} %get-tuple-element.121), channel_id=1, source_target_pairs={{0,4},{4,0},{8,12},{12,8},{16,20},{20,16},{24,28},{28,24},{1,5},{5... | collective-permute-start | bytes 1572872 | tf_op jit(solution)/shard_map/ppermute | solution.py:766
  373.5 74.2 %collective-permute-start.40 = (bf16[4,256,256]{2,1,0:T(8,128)(2,1)S(1)}, bf16[4,256,256]{2,1,0:T(8,128)(2,1)S(1)}, u32[]{:S(2)}, u32[]{:S(2)}) collective-permute-start(bf16[4,256,256]{2,1,0:T(8,128)(2,1)S(1)} %get-tuple-element.122), channel_id=1, source_target_pairs={{0,2},{1,3},{2,0},{3,1},{4,6},{5,7},{6,4},{7,5},{8,10},{9,11},{10,... | collective-permute-start | bytes 1572872 | tf_op jit(solution)/shard_map/ppermute | solution.py:766
  393.6 69.3 %collective-permute-start.46 = (bf16[4,496,256]{2,1,0:T(8,128)(2,1)S(1)}, bf16[4,496,256]{2,1,0:T(8,128)(2,1)S(1)}, u32[]{:S(2)}, u32[]{:S(2)}) collective-permute-start(bf16[4,496,256]{2,1,0:T(8,128)(2,1)S(1)} %get-tuple-element.130), channel_id=1, source_target_pairs={{0,4},{4,0},{8,12},{12,8},{16,20},{20,16},{24,28},{28,24},{1,5},{5... | collective-permute-start | bytes 3047432 | tf_op jit(solution)/shard_map/ppermute | solution.py:766
  414.7 65.2 %collective-permute-start.47 = (bf16[4,496,256]{2,1,0:T(8,128)(2,1)S(1)}, bf16[4,496,256]{2,1,0:T(8,128)(2,1)S(1)}, u32[]{:S(2)}, u32[]{:S(2)}) collective-permute-start(bf16[4,496,256]{2,1,0:T(8,128)(2,1)S(1)} %get-tuple-element.131), channel_id=1, source_target_pairs={{0,2},{1,3},{2,0},{3,1},{4,6},{5,7},{6,4},{7,5},{8,10},{9,11},{10,... | collective-permute-start | bytes 3047432 | tf_op jit(solution)/shard_map/ppermute | solution.py:766
  416.4 64.9 %collective-permute-start.48 = (bf16[4,496,256]{2,1,0:T(8,128)(2,1)S(1)}, bf16[4,496,256]{2,1,0:T(8,128)(2,1)S(1)}, u32[]{:S(2)}, u32[]{:S(2)}) collective-permute-start(bf16[4,496,256]{2,1,0:T(8,128)(2,1)S(1)} %get-tuple-element.132), channel_id=1, source_target_pairs={{0,6},{1,7},{2,4},{3,5},{4,2},{5,3},{6,0},{7,1},{8,14},{9,15},{10,... | collective-permute-start | bytes 3047432 | tf_op jit(solution)/shard_map/ppermute | solution.py:771
  490.1 49.1 %collective-permute-start.54 = (bf16[4,368,384]{2,1,0:T(8,128)(2,1)}, bf16[4,368,384]{2,1,0:T(8,128)(2,1)S(1)}, u32[]{:S(2)}, u32[]{:S(2)}) collective-permute-start(bf16[4,368,384]{2,1,0:T(8,128)(2,1)} %get-tuple-element.140), channel_id=1, source_target_pairs={{0,2},{1,3},{2,0},{3,1},{4,6},{5,7},{6,4},{7,5},{8,10},{9,11},{10,... | collective-permute-start | bytes 3391496 | tf_op jit(solution)/shard_map/ppermute | solution.py:766
  491.9 48.8 %collective-permute-start.55 = (bf16[4,368,384]{2,1,0:T(8,128)(2,1)}, bf16[4,368,384]{2,1,0:T(8,128)(2,1)S(1)}, u32[]{:S(2)}, u32[]{:S(2)}) collective-permute-start(bf16[4,368,384]{2,1,0:T(8,128)(2,1)} %get-tuple-element.141), channel_id=1, source_target_pairs={{0,6},{1,7},{2,4},{3,5},{4,2},{5,3},{6,0},{7,1},{8,14},{9,15},{10,... | collective-permute-start | bytes 3391496 | tf_op jit(solution)/shard_map/ppermute | solution.py:771
  (95 other events, 1286.3 us)
